TPU v7x, 32 devices: a whole 2x2x4 slice. The times are simulated.
32 devices in a mesh: fsdp: 32 (over z, y, x, core).
Axes of the slice: x: 2, y: 2, z: 4, core: 2. Of those that a mesh axis runs over, the one named last changes fastest.
Arguments:
- inputs: bfloat16 [6144, 1280], P('fsdp'), may hold values from -6 to 6
- ln1_gain: float32 [1280], P('fsdp'), may hold values from 0.5 to 1.5
- ln1_bias: float32 [1280], P('fsdp'), may hold values from -1 to 1
- w_query: float32 [1280, 1280], P('fsdp'), may hold values from -0.3125 to 0.3125
- b_query: float32 [1280], P('fsdp'), may hold values from -2.5 to 2.5
- w_key: float32 [1280, 1280], P('fsdp'), may hold values from -0.15625 to 0.15625
- w_value: float32 [1280, 1280], P('fsdp'), may hold values from -0.15625 to 0.15625
- b_value: float32 [1280], P('fsdp'), may hold values from -2.5 to 2.5
- w_out: float32 [1280, 1280], P('fsdp'), may hold values from -0.625 to 0.625
- b_out: float32 [1280], P('fsdp'), may hold values from -2.5 to 2.5
- ln2_gain: float32 [1280], P('fsdp'), may hold values from 0.5 to 1.5
- ln2_bias: float32 [1280], P('fsdp'), may hold values from -1 to 1
- w_up: float32 [1280, 5120], P('fsdp'), may hold values from -0.15625 to 0.15625
- b_up: float32 [5120], P('fsdp'), may hold values from -2.5 to 2.5
- w_down: float32 [5120, 1280], P('fsdp'), may hold values from -0.078125 to 0.078125
- b_down: float32 [1280], P('fsdp'), may hold values from -2.5 to 2.5
- lengths: int32 [4], replicated, may hold values from 1153 to 1536, as said below
- cotangent: bfloat16 [6144, 1280], P('fsdp'), may hold values from -6 to 6
Outputs:
- output: float32 [6144, 1280], P('fsdp')
- grad_inputs: float32 [6144, 1280], P('fsdp')
- grad_ln1_gain: float32 [1280], P('fsdp')
- grad_ln1_bias: float32 [1280], P('fsdp')
- grad_w_query: float32 [1280, 1280], P('fsdp')
- grad_b_query: float32 [1280], P('fsdp')
- grad_w_key: float32 [1280, 1280], P('fsdp')
- grad_w_value: float32 [1280, 1280], P('fsdp')
- grad_b_value: float32 [1280], P('fsdp')
- grad_w_out: float32 [1280, 1280], P('fsdp')
- grad_b_out: float32 [1280], P('fsdp')
- grad_ln2_gain: float32 [1280], P('fsdp')
- grad_ln2_bias: float32 [1280], P('fsdp')
- grad_w_up: float32 [1280, 5120], P('fsdp')
- grad_b_up: float32 [5120], P('fsdp')
- grad_w_down: float32 [5120, 1280], P('fsdp')
- grad_b_down: float32 [1280], P('fsdp')
Inputs may be any that keep to these rules, and one draw needn't show every extreme that they name: Frames of clip c at positions lengths[c] and beyond are padding; some clip has exactly 1536 real frames and some exactly 1153.
All inputs are finite; a program needn't handle non-finite values.
Results may differ from a plain program's by a relative error of at most 0.014.
The roundings to bfloat16 on the way count: a program that leaves them out, or rounds other values in their place, can miss the bound.
Values may be sent and summed in bfloat16 or wider, within the bound.
A program may use at most 320 MiB of HBM per device.

v0:
```python
import math

import jax
import jax.numpy as jnp
from jax import lax
from jax.sharding import PartitionSpec as P

D = 1280
H = 16
HD = 80
CLIP_LEN = 1536


epsilon = 1e-05
masked_value = -1e30


def swapped(block, axis, bit):
    count = lax.axis_size(axis)
    route = []
    for low in range(count):
        high = low | 1 << bit
        if high != low and high < count:
            route += [(low, high), (high, low)]
    return lax.ppermute(block, axis, route)


def layer_norm(values, gain, offset):
    average = jnp.mean(values, axis=-1, keepdims=True)
    centred = values - average
    variance = jnp.mean(centred * centred, axis=-1, keepdims=True)
    return centred * lax.rsqrt(variance + epsilon) * gain + offset


def norm_backward(values, gain, grad_out):

    def normalize(values_in, gain_in):
        return layer_norm(values_in, gain_in, 0.0)

    unused, pullback = jax.vjp(normalize, values, gain)
    grad_values, grad_gain = pullback(grad_out)
    return (grad_values, grad_gain, jnp.sum(grad_out, axis=0))


def gelu_exact(values):
    return jax.nn.gelu(values, approximate=False)


def matmul(left, right):
    return jnp.dot(left, right, preferred_element_type=jnp.float32)


def outer_sum(left, right):
    return lax.dot_general(
        left, right, (((0,), (0,)), ((), ())), preferred_element_type=jnp.float32
    )


def times_transposed(left, right):
    return lax.dot_general(
        left, right, (((1,), (1,)), ((), ())), preferred_element_type=jnp.float32
    )


def column_sums(matrix):
    return jnp.sum(matrix.astype(jnp.float32), axis=0)


def split_heads(matrix):
    return matrix.reshape(matrix.shape[0], H, HD).transpose(1, 0, 2)


def merge_heads(stacked):
    return stacked.transpose(1, 0, 2).reshape(stacked.shape[1], H * HD)


def on_device(
    inputs,
    ln1_gain,
    ln1_bias,
    w_query,
    b_query,
    w_key,
    w_value,
    b_value,
    w_out,
    b_out,
    ln2_gain,
    ln2_bias,
    w_up,
    b_up,
    w_down,
    b_down,
    lengths,
    cotangent,
):
    (
        whole_ln1_gain,
        whole_ln1_bias,
        whole_w_query,
        whole_b_query,
        whole_w_key,
        whole_w_value,
        whole_b_value,
        whole_w_out,
        whole_b_out,
        whole_ln2_gain,
        whole_ln2_bias,
        whole_w_up,
        whole_b_up,
        whole_w_down,
        whole_b_down,
    ) = (
        lax.all_gather(ln1_gain.astype(jnp.bfloat16), "fsdp", axis=0, tiled=True),
        lax.all_gather(ln1_bias.astype(jnp.bfloat16), "fsdp", axis=0, tiled=True),
        lax.all_gather(w_query.astype(jnp.bfloat16), "fsdp", axis=0, tiled=True),
        lax.all_gather(b_query.astype(jnp.bfloat16), "fsdp", axis=0, tiled=True),
        lax.all_gather(w_key.astype(jnp.bfloat16), "fsdp", axis=0, tiled=True),
        lax.all_gather(w_value.astype(jnp.bfloat16), "fsdp", axis=0, tiled=True),
        lax.all_gather(b_value.astype(jnp.bfloat16), "fsdp", axis=0, tiled=True),
        lax.all_gather(w_out.astype(jnp.bfloat16), "fsdp", axis=0, tiled=True),
        lax.all_gather(b_out.astype(jnp.bfloat16), "fsdp", axis=0, tiled=True),
        lax.all_gather(ln2_gain.astype(jnp.bfloat16), "fsdp", axis=0, tiled=True),
        lax.all_gather(ln2_bias.astype(jnp.bfloat16), "fsdp", axis=0, tiled=True),
        lax.all_gather(w_up.astype(jnp.bfloat16), "fsdp", axis=0, tiled=True),
        lax.all_gather(b_up.astype(jnp.bfloat16), "fsdp", axis=0, tiled=True),
        lax.all_gather(w_down.astype(jnp.bfloat16), "fsdp", axis=0, tiled=True),
        lax.all_gather(b_down.astype(jnp.bfloat16), "fsdp", axis=0, tiled=True),
    )
    device_index = lax.axis_index("fsdp")
    row_count = inputs.shape[0]
    group_size = CLIP_LEN // row_count
    levels = group_size.bit_length() - 1
    length = lengths[device_index // group_size]
    key_valid = (jnp.arange(CLIP_LEN, dtype=jnp.int32) < length)[None, :]
    score_scale = 1.0 / math.sqrt(HD)
    source = inputs.astype(jnp.float32)
    normed = layer_norm(
        source, whole_ln1_gain.astype(jnp.float32), whole_ln1_bias.astype(jnp.float32)
    ).astype(jnp.bfloat16)
    query_rows = (matmul(normed, whole_w_query) + whole_b_query.astype(jnp.float32)).astype(
        jnp.bfloat16
    )
    key_rows = matmul(normed, whole_w_key).astype(jnp.bfloat16)
    value_rows = (matmul(normed, whole_w_value) + whole_b_value.astype(jnp.float32)).astype(
        jnp.bfloat16
    )
    key_all, value_all = (key_rows, value_rows)
    for bit_number in range(levels):
        other_key, other_value = swapped((key_all, value_all), "fsdp", bit_number)
        upper_half = device_index // (1 << bit_number) % 2 == 1
        key_all = jnp.where(
            upper_half,
            jnp.concatenate([other_key, key_all], axis=0),
            jnp.concatenate([key_all, other_key], axis=0),
        )
        value_all = jnp.where(
            upper_half,
            jnp.concatenate([other_value, value_all], axis=0),
            jnp.concatenate([value_all, other_value], axis=0),
        )

    def head_scores(query_head, key_head):
        scores = times_transposed(query_head, key_head) * score_scale
        return jnp.where(key_valid, scores, masked_value)

    def head_forward(operands):
        query_head, key_head, value_head = operands
        masked = head_scores(query_head, key_head)
        largest = jnp.max(masked, axis=-1, keepdims=True)
        exponent = jnp.exp(masked - largest)
        total = jnp.sum(exponent, axis=-1, keepdims=True)
        attn_weights = (exponent / total).astype(jnp.bfloat16)
        return (matmul(attn_weights, value_head), (largest + jnp.log(total))[:, 0])

    query_heads = split_heads(query_rows)
    key_heads = split_heads(key_all)
    value_heads = split_heads(value_all)
    mixed_heads, log_totals = lax.map(head_forward, (query_heads, key_heads, value_heads))
    attended = merge_heads(mixed_heads).astype(jnp.bfloat16)
    residual = source + (matmul(attended, whole_w_out) + whole_b_out.astype(jnp.float32))
    normed_two = layer_norm(
        residual, whole_ln2_gain.astype(jnp.float32), whole_ln2_bias.astype(jnp.float32)
    ).astype(jnp.bfloat16)
    hidden = matmul(normed_two, whole_w_up) + whole_b_up.astype(jnp.float32)
    activated = gelu_exact(hidden).astype(jnp.bfloat16)
    output = residual + (matmul(activated, whole_w_down) + whole_b_down.astype(jnp.float32))
    (
        back_w_query,
        back_w_key,
        back_w_value,
        back_w_out,
        back_w_up,
        back_w_down,
        back_ln1_gain,
        back_ln2_gain,
    ) = (
        lax.all_gather(w_query.astype(jnp.bfloat16), "fsdp", axis=0, tiled=True),
        lax.all_gather(w_key.astype(jnp.bfloat16), "fsdp", axis=0, tiled=True),
        lax.all_gather(w_value.astype(jnp.bfloat16), "fsdp", axis=0, tiled=True),
        lax.all_gather(w_out.astype(jnp.bfloat16), "fsdp", axis=0, tiled=True),
        lax.all_gather(w_up.astype(jnp.bfloat16), "fsdp", axis=0, tiled=True),
        lax.all_gather(w_down.astype(jnp.bfloat16), "fsdp", axis=0, tiled=True),
        lax.all_gather(ln1_gain.astype(jnp.bfloat16), "fsdp", axis=0, tiled=True),
        lax.all_gather(ln2_gain.astype(jnp.bfloat16), "fsdp", axis=0, tiled=True),
    )
    grad_b_down = column_sums(cotangent)
    grad_activated = times_transposed(cotangent, back_w_down)
    unused, gelu_pullback = jax.vjp(gelu_exact, hidden)
    grad_hidden = gelu_pullback(grad_activated)[0].astype(jnp.bfloat16)
    shard_w_down = lax.psum_scatter(
        outer_sum(activated, cotangent), "fsdp", scatter_dimension=0, tiled=True
    )
    grad_b_up = column_sums(grad_hidden)
    grad_normed_two = times_transposed(grad_hidden, back_w_up)
    grad_from_second, grad_ln2_gain, grad_ln2_bias = norm_backward(
        residual, back_ln2_gain.astype(jnp.float32), grad_normed_two
    )
    grad_residual = cotangent.astype(jnp.float32) + grad_from_second
    grad_branch = grad_residual.astype(jnp.bfloat16)
    grad_b_out = column_sums(grad_branch)
    grad_attended = times_transposed(grad_branch, back_w_out).astype(jnp.bfloat16)

    def head_backward(operands):
        query_head, key_head, value_head, grad_head, log_total = operands
        masked = head_scores(query_head, key_head)
        attn_weights = jnp.exp(masked - log_total[:, None])
        grad_weights = times_transposed(grad_head, value_head)
        inner = jnp.sum(attn_weights * grad_weights, axis=-1, keepdims=True)
        grad_scores = (attn_weights * (grad_weights - inner)).astype(jnp.bfloat16)
        grad_query = matmul(grad_scores, key_head) * score_scale
        grad_key = outer_sum(grad_scores, query_head) * score_scale
        grad_value = outer_sum(attn_weights.astype(jnp.bfloat16), grad_head)
        return (grad_query, grad_key, grad_value)

    grad_query_heads, grad_key_heads, grad_value_heads = lax.map(
        head_backward, (query_heads, key_heads, value_heads, split_heads(grad_attended), log_totals)
    )
    grad_queries = merge_heads(grad_query_heads).astype(jnp.bfloat16)
    grad_key_all = merge_heads(grad_key_heads)
    grad_value_all = merge_heads(grad_value_heads)
    for bit_number in reversed(range(levels)):
        half_rows = grad_key_all.shape[0] // 2
        upper_half = device_index // (1 << bit_number) % 2 == 1
        lower_key, higher_key = (grad_key_all[:half_rows], grad_key_all[half_rows:])
        lower_value, higher_value = (grad_value_all[:half_rows], grad_value_all[half_rows:])
        keep_key = jnp.where(upper_half, higher_key, lower_key)
        send_key = jnp.where(upper_half, lower_key, higher_key)
        keep_value = jnp.where(upper_half, higher_value, lower_value)
        send_value = jnp.where(upper_half, lower_value, higher_value)
        got_key, got_value = (
            swapped(send_key.astype(jnp.bfloat16), "fsdp", bit_number).astype(send_key.dtype),
            swapped(send_value.astype(jnp.bfloat16), "fsdp", bit_number).astype(send_value.dtype),
        )
        grad_key_all = keep_key + got_key
        grad_value_all = keep_value + got_value
    grad_keys = grad_key_all.astype(jnp.bfloat16)
    grad_values = grad_value_all.astype(jnp.bfloat16)
    grad_b_query = column_sums(grad_queries)
    grad_b_value = column_sums(grad_values)
    grad_normed = (
        times_transposed(grad_queries, back_w_query)
        + times_transposed(grad_keys, back_w_key)
        + times_transposed(grad_values, back_w_value)
    )
    grad_from_first, grad_ln1_gain, grad_ln1_bias = norm_backward(
        source, back_ln1_gain.astype(jnp.float32), grad_normed
    )
    grad_inputs = grad_residual + grad_from_first
    stacked = lax.psum_scatter(
        jnp.concatenate(
            [
                jnp.concatenate(
                    [
                        outer_sum(normed, grad_queries),
                        outer_sum(normed, grad_keys),
                        outer_sum(normed, grad_values),
                        outer_sum(attended, grad_branch),
                    ],
                    axis=1,
                ),
                outer_sum(normed_two, grad_hidden),
            ],
            axis=1,
        ),
        "fsdp",
        scatter_dimension=0,
        tiled=True,
    )
    shard_w_up = stacked[:, 4 * D :]
    shard_w_query = stacked[:, 0:D]
    shard_w_key = stacked[:, D : 2 * D]
    shard_w_value = stacked[:, 2 * D : 3 * D]
    shard_w_out = stacked[:, 3 * D : 4 * D]
    (
        shard_ln1_gain,
        shard_ln1_bias,
        shard_b_query,
        shard_b_value,
        shard_b_out,
        shard_ln2_gain,
        shard_ln2_bias,
        shard_b_up,
        shard_b_down,
    ) = (
        lax.psum_scatter(grad_ln1_gain, "fsdp", scatter_dimension=0, tiled=True),
        lax.psum_scatter(grad_ln1_bias, "fsdp", scatter_dimension=0, tiled=True),
        lax.psum_scatter(grad_b_query, "fsdp", scatter_dimension=0, tiled=True),
        lax.psum_scatter(grad_b_value, "fsdp", scatter_dimension=0, tiled=True),
        lax.psum_scatter(grad_b_out, "fsdp", scatter_dimension=0, tiled=True),
        lax.psum_scatter(grad_ln2_gain, "fsdp", scatter_dimension=0, tiled=True),
        lax.psum_scatter(grad_ln2_bias, "fsdp", scatter_dimension=0, tiled=True),
        lax.psum_scatter(grad_b_up, "fsdp", scatter_dimension=0, tiled=True),
        lax.psum_scatter(grad_b_down, "fsdp", scatter_dimension=0, tiled=True),
    )
    return (
        output,
        grad_inputs,
        shard_ln1_gain,
        shard_ln1_bias,
        shard_w_query,
        shard_b_query,
        shard_w_key,
        shard_w_value,
        shard_b_value,
        shard_w_out,
        shard_b_out,
        shard_ln2_gain,
        shard_ln2_bias,
        shard_w_up,
        shard_b_up,
        shard_w_down,
        shard_b_down,
    )


def solution(mesh):
    in_specs = (
        P("fsdp", None),
        P("fsdp"),
        P("fsdp"),
        P("fsdp", None),
        P("fsdp"),
        P("fsdp", None),
        P("fsdp", None),
        P("fsdp"),
        P("fsdp", None),
        P("fsdp"),
        P("fsdp"),
        P("fsdp"),
        P("fsdp", None),
        P("fsdp"),
        P("fsdp", None),
        P("fsdp"),
        P(),
        P("fsdp", None),
    )
    out_specs = (
        P("fsdp", None),
        P("fsdp", None),
        P("fsdp"),
        P("fsdp"),
        P("fsdp", None),
        P("fsdp"),
        P("fsdp", None),
        P("fsdp", None),
        P("fsdp"),
        P("fsdp", None),
        P("fsdp"),
        P("fsdp"),
        P("fsdp"),
        P("fsdp", None),
        P("fsdp"),
        P("fsdp", None),
        P("fsdp"),
    )
    return jax.shard_map(
        on_device, mesh=mesh, in_specs=in_specs, out_specs=out_specs, check_vma=False
    )
```

profile of v0, /device:TPU:0, one launch (start us, length us, event | category | flops | bytes accessed | tf_op | source)
XLA Modules:
  0.0 1647.6 jit_solution(5950444463934327169)
XLA Ops:
  14.1 2.0 convert_element_type.234
  16.1 2.0 convert_element_type.238
  20.4 44.0 %all-reduce.19 = (bf16[1280]{0:T(1024)(128)(2,1)S(1)}, bf16[1280]{0:T(1024)(128)(2,1)S(1)}, bf16[1280]{0:T(1024)(128)(2,1)S(1)}, bf16[1280]{0:T(1024)(128)(2,1)S...) all-reduce(bf16[1280]{0:T(1024)(128)(2,1)S(1)} %dynamic-update-slic, ...), channel_id=1, replica_groups=mesh['fsdp'=32] {'fsdp'}, use_global_device_ids=true, to_apply=%add.2 | all-reduce | flops 15360 | bytes 61440
  64.9 9.2 all-gather.9.cloned.1.call-done
  74.1 2.8 convolution_convert_fusion.1
  77.3 58.6 %all-gather.11.cloned.1.call-done = bf16[1280,1280]{1,0:T(8,128)(2,1)} async-done(((bf16[40,1280]{1,0:T(8,128)(2,1)}), bf16[1280,1280]{1,0:T(8,128)(2,1)}) %all-gather.11.cloned.1.call-update) | async-done | bytes 3276816 | tf_op jit(solution)/shard_map/all_gather | solution.py:119
  135.8 2.8 fusion.57
  143.1 23.5 %collective-permute-done.1 = bf16[384,1280]{1,0:T(8,128)(2,1)S(1)} collective-permute-done((bf16[384,1280]{1,0:T(8,128)(2,1)}, bf16[384,1280]{1,0:T(8,128)(2,1)S(1)}, u32[]{:S(2)}, u32[]{:S(2)}) %collective-permute-start.1) | collective-permute-done | bytes 983072 | tf_op jit(solution)/shard_map/ppermute | solution.py:25
  166.5 3.6 maximum_select_fusion.2
  171.4 22.8 %collective-permute-done.4 = bf16[384,1280]{1,0:T(8,128)(2,1)S(1)} collective-permute-done((bf16[384,1280]{1,0:T(8,128)(2,1)S(1)}, bf16[384,1280]{1,0:T(8,128)(2,1)S(1)}, u32[]{:S(2)}, u32[]{:S(2)}) %collective-permute-start.4) | collective-permute-done | bytes 983072 | tf_op jit(solution)/shard_map/ppermute | solution.py:25
  194.2 2.1 maximum_select_fusion.4
  198.4 2.1 copy.136
  200.5 2.1 copy.132
  204.0 3.6 fusion.56
  210.0 2.1 copy.135
  212.1 2.1 copy.131
  214.2 4.4 maximum_select_fusion.7
  219.9 2.2 copy.134
  222.2 3.4 maximum_select_fusion.3
  226.1 4.0 copy.129
  230.1 5.7 fusion.47
  235.8 7.7 copy.138
  243.6 25.5 %collective-permute-done.5 = bf16[768,1280]{1,0:T(8,128)(2,1)} collective-permute-done((bf16[768,1280]{1,0:T(8,128)(2,1)}, bf16[768,1280]{1,0:T(8,128)(2,1)}, u32[]{:S(2)}, u32[]{:S(2)}) %collective-permute-start.5) | collective-permute-done | bytes 1966112 | tf_op jit(solution)/shard_map/ppermute | solution.py:25
  269.1 4.0 copy.133
  273.1 4.7 fusion.48
  277.8 7.8 copy.139
  285.6 83.9 %while.28 = (s32[]{:T(128)}, bf16[16,192,80]{1,2,0:T(8,128)(2,1)S(1)}, f32[16,192]{1,0:T(8,128)}, bf16[16,192,80]{2,1,0:T(8,128)(2,1)}, bf16[16,1536,80]{2,1,0:T...) while((s32[]{:T(128)}, ...), condition=%wide.region_5.6_spmd.clone, body=%wide.region_2.5_spmd.clone.sunk | while | flops 96732480 | bytes 4469869 | solution.py:179
  369.5 2.9 fusion.85
  372.7 9.5 convolution_add_fusion
  382.1 86.8 %all-gather.17.cloned.1.call-done = bf16[5120,1280]{1,0:T(8,128)(2,1)} async-done(((bf16[160,1280]{1,0:T(8,128)(2,1)}), bf16[5120,1280]{1,0:T(8,128)(2,1)}) %all-gather.17.cloned.1.call-update) | async-done | bytes 13107216 | tf_op jit(solution)/shard_map/all_gather | solution.py:127
  468.9 17.2 %convert_reduce_fusion = (f32[5120]{0:T(1024)S(1)}, bf16[192,5120]{1,0:T(8,128)(2,1)S(1)}, f32[192,5120]{1,0:T(8,128)}) fusion(f32[192,5120]{1,0:T(8,128)} %convolution_add_fusion, bf16[192,1280]{1,0:T(8,128)(2,1)S(1)} %copy-done.7, bf16[5120,1280]{1,0:T(8,128)(2,1)} %all-gather.17.cloned.1.call-done), kind=kOutput, calls=%fused_computation.70 | convolution fusion | flops 2589322240 | bytes 23449600 | tf_op jit(solution)/shard_map/dot_general | solution.py:60
  486.2 10.1 multiply_reduce_fusion.1
  500.9 153.4 %while.29 = (s32[]{:T(128)}, bf16[16,192,80]{1,2,0:T(8,128)(2,1)S(1)}, f32[16,1536,80]{1,2,0:T(8,128)}, f32[16,1536,80]{1,2,0:T(8,128)}, bf16[16,192,80]{2,1,0:T...) while((s32[]{:T(128)}, ...), condition=%wide.region_12.13_spmd.clone, body=%wide.region_10.12_spmd.clone.sunk | while | flops 238723392 | bytes 11284349 | solution.py:236
  508.7 1.9 fusion.148
  547.0 1.9 fusion.148
  614.1 1.9 fusion.148
  623.7 1.9 fusion.148
  654.3 5.2 select_convert_fusion.1
  659.5 4.0 copy.145
  664.9 4.9 select_convert_fusion
  669.8 4.0 copy.147
  674.4 5.8 slice_select_fusion.1
  680.2 5.7 slice_select_fusion
  685.9 5.4 copy.146
  691.4 5.9 copy.148
  697.3 4.0 convolution_dynamic-update-slice_fusion.4
  701.3 8.2 collective-permute-done.6
  709.5 2.2 convert_add_fusion.1
  713.4 37.5 %collective-permute-done.9 = bf16[768,1280]{1,0:T(8,128)(2,1)} collective-permute-done((bf16[768,1280]{1,0:T(8,128)(2,1)}, bf16[768,1280]{1,0:T(8,128)(2,1)}, u32[]{:S(2)}, u32[]{:S(2)}) %collective-permute-start.9) | collective-permute-done | bytes 1966112 | tf_op jit(solution)/shard_map/ppermute | solution.py:25
  750.9 2.0 convert_add_fusion
  755.1 21.2 %collective-permute-done.10 = bf16[384,1280]{1,0:T(8,128)(2,1)S(1)} collective-permute-done((bf16[384,1280]{1,0:T(8,128)(2,1)S(1)}, bf16[384,1280]{1,0:T(8,128)(2,1)S(1)}, u32[]{:S(2)}, u32[]{:S(2)}) %collective-permute-start.10) | collective-permute-done | bytes 983072 | tf_op jit(solution)/shard_map/ppermute | solution.py:25
  777.0 4.0 convolution_dynamic-update-slice_fusion.3
  781.2 4.0 convolution_dynamic-update-slice_fusion.2
  785.2 3.9 convolution_dynamic-update-slice_fusion.1
  789.1 10.7 convolution_dynamic-update-slice_fusion
  799.9 3.9 multiply_convert_fusion.1
  803.8 10.9 fusion.87
  816.9 3.4 fusion.86
  820.4 8.8 fusion.55
  834.7 47.6 %all-reduce.18 = (f32[1280]{0:T(1024)S(1)}, f32[1280]{0:T(1024)S(1)}, f32[1280]{0:T(1024)S(1)}, f32[1280]{0:T(1024)S(1)}, f32[1280]{0:T(1024)S(1)}, /*index=5*/f...) all-reduce(f32[1280]{0:T(1024)S(1)} %get-tuple-element.224, ...), channel_id=2, replica_groups=mesh['fsdp'=32] {'fsdp'}, use_global_device_ids=true, to_apply=%region_16.17.clone | all-reduce | flops 15360 | bytes 122880
  887.6 462.3 %reduce-scatter.3.cloned.1.call-done = f32[40,10240]{1,0:T(8,128)} async-done(((f32[1280,10240]{1,0:T(8,128)}), f32[40,10240]{1,0:T(8,128)}) %reduce-scatter.3.cloned.1.call-update) | async-done | bytes 1638416 | tf_op jit(solution)/shard_map/reduce_scatter | solution.py:270
  1349.8 2.1 slice.88
  1351.9 2.1 fusion.84
  1354.1 286.5 %reduce-scatter.5.cloned.1.call-done = f32[160,1280]{1,0:T(8,128)} async-done(((f32[5120,1280]{1,0:T(8,128)}), f32[160,1280]{1,0:T(8,128)}) %reduce-scatter.5.cloned.1.call-update) | async-done | bytes 819216 | tf_op jit(solution)/shard_map/reduce_scatter | solution.py:211
  (421 shorter events, 277.0 us)
Async XLA Ops:
  7.2 11.0 copy-start.28
  7.2 11.0 copy-start.29
  7.2 11.0 copy-start.30
  7.2 11.0 copy-start.31
  7.2 11.0 copy-start.32
  7.2 11.0 copy-start.33
  7.3 11.0 copy-start.34
  7.3 11.0 copy-start.27
  7.3 11.0 copy-start.35
  7.3 57.2 %copy-start = (bf16[192,1280]{1,0:T(8,128)(2,1)S(1)}, bf16[192,1280]{1,0:T(8,128)(2,1)}, u32[]{:S(2)}) copy-start(bf16[192,1280]{1,0:T(8,128)(2,1)} %param.22) | copy-start | bytes 1474564
  7.3 66.8 %all-gather.9.cloned.1.call-start = ((), (), s32[]{:S(2)}) async-start(), calls=%async_computation.3 | async-start | bytes 3379200 | tf_op jit(solution)/shard_map/all_gather | solution.py:118
  9.0 126.8 %all-gather.11.cloned.1.call-start = ((), (), s32[]{:S(2)}) async-start(), calls=%async_computation.4 | async-start | bytes 3379200 | tf_op jit(solution)/shard_map/all_gather | solution.py:119
  10.7 193.3 %all-gather.7.cloned.1.call-start = ((), (), s32[]{:S(2)}) async-start(), calls=%async_computation.2 | async-start | bytes 3379200 | tf_op jit(solution)/shard_map/all_gather | solution.py:116
  12.3 357.1 %all-gather.13.cloned.1.call-start = ((), (), s32[]{:S(2)}) async-start(), calls=%async_computation.5 | async-start | bytes 3379200 | tf_op jit(solution)/shard_map/all_gather | solution.py:121
  14.0 358.7 %all-gather.15.cloned.1.call-start = ((), (), s32[]{:S(2)}) async-start(), calls=%async_computation.6 | async-start | bytes 13516800 | tf_op jit(solution)/shard_map/all_gather | solution.py:125
  16.0 452.9 %all-gather.17.cloned.1.call-start = ((), (), s32[]{:S(2)}) async-start(), calls=%async_computation.7 | async-start | bytes 13516800 | tf_op jit(solution)/shard_map/all_gather | solution.py:127
  18.1 1331.8 %reduce-scatter.3.cloned.1.call-start = ((), (), s32[]{:S(2)}) async-start(), calls=%async_computation.8 | async-start | bytes 54067200 | tf_op jit(solution)/shard_map/reduce_scatter | solution.py:270
  64.9 73.8 %copy-start.24 = (f32[192]{0:T(256)}, f32[192]{0:T(256)S(1)}, u32[]{:S(2)}) copy-start(f32[192]{0:T(256)S(1)} %fusion.67) | copy-start | bytes 2308
  76.9 64.7 %copy-start.21 = (bf16[192,1280]{1,0:T(8,128)(2,1)}, bf16[192,1280]{1,0:T(8,128)(2,1)S(1)}, u32[]{:S(2)}) copy-start(bf16[192,1280]{1,0:T(8,128)(2,1)S(1)} %convolution_convert_fusion.1) | copy-start | bytes 1474564
  76.9 62.0 %collective-permute-start = (bf16[192,1280]{1,0:T(8,128)(2,1)S(1)}, bf16[192,1280]{1,0:T(8,128)(2,1)S(1)}, u32[]{:S(2)}, u32[]{:S(2)}) collective-permute-start(bf16[192,1280]{1,0:T(8,128)(2,1)S(1)} %convolution_convert_fusion.1), channel_id=1, source_target_pairs={{0,1},{1,0},{2,3},{3,2},{4,5},{5,4},{6,7},{7,6},{8,9},{9,8},{10,11... | collective-permute-start | bytes 1474568 | tf_op jit(solution)/shard_map/ppermute | solution.py:25
  138.6 3.3 copy-start.23
  138.7 3.0 collective-permute-start.3
  139.0 2.7 copy-start.20
  140.2 26.3 %collective-permute-start.1 = (bf16[384,1280]{1,0:T(8,128)(2,1)}, bf16[384,1280]{1,0:T(8,128)(2,1)S(1)}, u32[]{:S(2)}, u32[]{:S(2)}) collective-permute-start(bf16[384,1280]{1,0:T(8,128)(2,1)} %maximum_select_fusion.6), channel_id=1, source_target_pairs={{0,2},{2,0},{1,3},{3,1},{4,6},{6,4},{5,7},{7,5},{8,10},{10,8},{9,1... | collective-permute-start | bytes 2949128 | tf_op jit(solution)/shard_map/ppermute | solution.py:25
  141.7 0.8 copy-start.22
  142.5 51.7 %collective-permute-start.4 = (bf16[384,1280]{1,0:T(8,128)(2,1)S(1)}, bf16[384,1280]{1,0:T(8,128)(2,1)S(1)}, u32[]{:S(2)}, u32[]{:S(2)}) collective-permute-start(bf16[384,1280]{1,0:T(8,128)(2,1)S(1)} %maximum_select_fusion.8), channel_id=1, source_target_pairs={{0,2},{2,0},{1,3},{3,1},{4,6},{6,4},{5,7},{7,5},{8,10},{10,8},{9,1... | collective-permute-start | bytes 2949128 | tf_op jit(solution)/shard_map/ppermute | solution.py:25
  143.1 54.7 %copy-start.36 = (s32[4]{0:T(128)S(1)}, s32[4]{0:T(128)}, u32[]{:S(2)}) copy-start(s32[4]{0:T(128)} %param.38) | copy-start | bytes 52
  170.1 56.0 %collective-permute-start.2 = (bf16[768,1280]{1,0:T(8,128)(2,1)}, bf16[768,1280]{1,0:T(8,128)(2,1)}, u32[]{:S(2)}, u32[]{:S(2)}) collective-permute-start(bf16[768,1280]{1,0:T(8,128)(2,1)} %maximum_select_fusion.2), channel_id=1, source_target_pairs={{0,4},{4,0},{1,5},{5,1},{2,6},{6,2},{3,7},{7,3},{8,12},{12,8},{9,1... | collective-permute-start | bytes 5898248 | tf_op jit(solution)/shard_map/ppermute | solution.py:25
  194.2 13.4 copy-start.14
  196.3 72.8 %collective-permute-start.5 = (bf16[768,1280]{1,0:T(8,128)(2,1)}, bf16[768,1280]{1,0:T(8,128)(2,1)}, u32[]{:S(2)}, u32[]{:S(2)}) collective-permute-start(bf16[768,1280]{1,0:T(8,128)(2,1)} %maximum_select_fusion.4), channel_id=1, source_target_pairs={{0,4},{4,0},{1,5},{5,1},{2,6},{6,2},{3,7},{7,3},{8,12},{12,8},{9,1... | collective-permute-start | bytes 5898248 | tf_op jit(solution)/shard_map/ppermute | solution.py:25
  222.2 3.4 copy-start.15
  372.6 96.3 %copy-start.7 = (bf16[192,1280]{1,0:T(8,128)(2,1)S(1)}, bf16[192,1280]{1,0:T(8,128)(2,1)}, u32[]{:S(2)}) copy-start(bf16[192,1280]{1,0:T(8,128)(2,1)} %param.39) | copy-start | bytes 1474564
  486.2 10.1 copy-start.18
  496.3 2.3 copy-start.3
  496.7 0.9 copy-start.4
  654.3 42.9 %copy-start.6 = (bf16[16,192,80]{1,2,0:T(8,128)(2,1)}, bf16[16,192,80]{1,2,0:T(8,128)(2,1)S(1)}, u32[]{:S(2)}) copy-start(bf16[16,192,80]{1,2,0:T(8,128)(2,1)S(1)} %get-tuple-element.111) | copy-start | bytes 1474564
  663.5 46.0 %collective-permute-start.6 = (bf16[768,1280]{1,0:T(8,128)(2,1)}, bf16[768,1280]{1,0:T(8,128)(2,1)}, u32[]{:S(2)}, u32[]{:S(2)}) collective-permute-start(bf16[768,1280]{1,0:T(8,128)(2,1)} %copy.145), channel_id=1, source_target_pairs={{0,4},{4,0},{1,5},{5,1},{2,6},{6,2},{3,7},{7,3},{8,12},{12,8},{9,1... | collective-permute-start | bytes 5898248 | tf_op jit(solution)/shard_map/ppermute | solution.py:25
  673.8 77.1 %collective-permute-start.9 = (bf16[768,1280]{1,0:T(8,128)(2,1)}, bf16[768,1280]{1,0:T(8,128)(2,1)}, u32[]{:S(2)}, u32[]{:S(2)}) collective-permute-start(bf16[768,1280]{1,0:T(8,128)(2,1)} %copy.147), channel_id=1, source_target_pairs={{0,4},{4,0},{1,5},{5,1},{2,6},{6,2},{3,7},{7,3},{8,12},{12,8},{9,1... | collective-permute-start | bytes 5898248 | tf_op jit(solution)/shard_map/ppermute | solution.py:25
  697.2 12.2 copy-start.2
  709.5 41.4 %copy-start.1 = (f32[768,1280]{1,0:T(8,128)S(1)}, f32[768,1280]{1,0:T(8,128)}, u32[]{:S(2)}) copy-start(f32[768,1280]{1,0:T(8,128)} %copy.148) | copy-start | bytes 11796484
  711.9 42.8 %collective-permute-start.7 = (bf16[384,1280]{1,0:T(8,128)(2,1)S(1)}, bf16[384,1280]{1,0:T(8,128)(2,1)S(1)}, u32[]{:S(2)}, u32[]{:S(2)}) collective-permute-start(bf16[384,1280]{1,0:T(8,128)(2,1)S(1)} %select_convert_fusion.3), channel_id=1, source_target_pairs={{0,2},{2,0},{1,3},{3,1},{4,6},{6,4},{5,7},{7,5},{8,10},{10,8},{9,1... | collective-permute-start | bytes 2949128 | tf_op jit(solution)/shard_map/ppermute | solution.py:25
  753.1 23.1 %collective-permute-start.10 = (bf16[384,1280]{1,0:T(8,128)(2,1)S(1)}, bf16[384,1280]{1,0:T(8,128)(2,1)S(1)}, u32[]{:S(2)}, u32[]{:S(2)}) collective-permute-start(bf16[384,1280]{1,0:T(8,128)(2,1)S(1)} %select_convert_fusion.2), channel_id=1, source_target_pairs={{0,2},{2,0},{1,3},{3,1},{4,6},{6,4},{5,7},{7,5},{8,10},{10,8},{9,1... | collective-permute-start | bytes 2949128 | tf_op jit(solution)/shard_map/ppermute | solution.py:25
  755.0 21.8 %collective-permute-start.8 = (bf16[192,1280]{1,0:T(8,128)(2,1)S(1)}, bf16[192,1280]{1,0:T(8,128)(2,1)S(1)}, u32[]{:S(2)}, u32[]{:S(2)}) collective-permute-start(bf16[192,1280]{1,0:T(8,128)(2,1)S(1)} %select_convert_fusion.5), channel_id=1, source_target_pairs={{0,1},{1,0},{2,3},{3,2},{4,5},{5,4},{6,7},{7,6},{8,9},{9,8},{10,11... | collective-permute-start | bytes 1474568 | tf_op jit(solution)/shard_map/ppermute | solution.py:25
  776.7 4.3 collective-permute-start.11
  777.0 4.0 copy-start.12
  781.2 4.0 copy-start.10
  785.2 3.9 copy-start.19
  799.8 840.7 %reduce-scatter.5.cloned.1.call-start = ((), (), s32[]{:S(2)}) async-start(), calls=%async_computation.9 | async-start | bytes 27033600 | tf_op jit(solution)/shard_map/reduce_scatter | solution.py:211
  799.9 3.9 copy-start.8
  814.7 0.7 copy-start.26
  820.4 8.8 copy-start.13
  820.4 8.8 copy-start.16
  829.1 1.2 copy-start.11
  829.1 2.2 copy-start.17
  831.3 1.4 copy-start.25
  831.3 1.9 copy-start.5
  831.3 1.9 copy-start.9
Sparse Core Ops, SparseCore 0:
  11.5 62.5 all-gather.8
  77.6 58.2 all-gather.10
  139.3 64.6 all-gather.6
  207.3 63.3 all-gather.12
  273.4 96.4 all-gather.14
  372.7 96.2 all-gather.16
  800.0 549.8 reduce-scatter.2
  1352.7 287.7 reduce-scatter.4
where the time goes:
time: 1660 us; the launch traced here: 1650 us
  waiting for transfers between devices  1040 us (63%)
  matrix products  277 us (17%)
  local copies, waits for them, and re-layouts  107 us (6%)
  other arithmetic  102 us (6%)
  blocking collectives  91.6 us (6%)
    reduce_scatter x1, waiting for transfers between devices, on_device(): lax.psum_scatter(jnp.concatenate([jnp.concatenate([outer_sum(normed, grad...  462 us
    reduce_scatter x1, waiting for transfers between devices, on_device(): lax.psum_scatter(outer_sum(activated, cotangent), 'fsdp', scatter_dimensi...  286 us
    ppermute x12, waiting for transfers between devices, swapped(): return lax.ppermute(block, axis, route)  139 us
    dot_general x54, matrix products, times_transposed(): lax.dot_general(left, right, (((1,), (1,)), ((), ())), preferred_element_...  106 us
    dot_general x38, matrix products, outer_sum(): lax.dot_general(left, right, (((0,), (0,)), ((), ())), preferred_element_...  96.2 us
    unnamed x2, blocking collectives  91.6 us
    all_gather x1, waiting for transfers between devices, on_device(): lax.all_gather(w_down.astype(jnp.bfloat16), 'fsdp', axis=0, tiled=True)  86.8 us
    dot_general x38, matrix products, matmul(): return jnp.dot(left, right, preferred_element_type=jnp.float32)  75 us
  transfers between devices with their start and end apart: 20, of which 12 were waited for; matrix products, arithmetic and copies ran while one was open for 16% of the time, Pallas kernels for 0%

commit v1 on v0

v1 whole, which is shorter than its diff:
```python
import functools
import math

import jax
import jax.numpy as jnp
from jax import lax
from jax.experimental import pallas as pl
from jax.experimental.pallas import tpu as pltpu
from jax.sharding import PartitionSpec as P

D = 1280
H = 16
HD = 80
CLIP_LEN = 1536
GROUP = 8
LANES = 128
HEADS_HERE = H // GROUP
HEAD_COLS = HEADS_HERE * HD
SURE = CLIP_LEN * 3 // 4

epsilon = 1e-05
masked_value = -1e30
MESH = pl.DeviceIdType.MESH
VMEM = pltpu.VMEM
DMA = pltpu.SemaphoreType.DMA
bf16 = jnp.bfloat16
f32 = jnp.float32


def matmul(left, right):
    return jnp.dot(left, right, preferred_element_type=f32)


def outer_sum(left, right):
    return lax.dot_general(left, right, (((0,), (0,)), ((), ())), preferred_element_type=f32)


def times_transposed(left, right):
    return lax.dot_general(left, right, (((1,), (1,)), ((), ())), preferred_element_type=f32)


def flip(place, mask):
    for bit in (1, 2, 4):
        if mask & bit:
            place = place + bit - 2 * bit * (place // bit % 2)
    return place


def remote(src, dst, send_sem, recv_sem, target):
    return pltpu.make_async_remote_copy(
        src_ref=src,
        dst_ref=dst,
        send_sem=send_sem,
        recv_sem=recv_sem,
        device_id=(target,),
        device_id_type=MESH,
    )


def greet(targets):
    barrier = pltpu.get_barrier_semaphore()
    for target in targets:
        pl.semaphore_signal(barrier, inc=1, device_id=(target,), device_id_type=MESH)
    pl.semaphore_wait(barrier, len(targets))


def greet_all(me, count):
    barrier = pltpu.get_barrier_semaphore()

    def signal(step, unused):
        pl.semaphore_signal(
            barrier, inc=1, device_id=((me + step) % count,), device_id_type=MESH
        )
        return unused

    lax.fori_loop(1, count, signal, 0)
    pl.semaphore_wait(barrier, count - 1)


def params(collective_id):
    return pltpu.CompilerParams(collective_id=collective_id, has_side_effects=True)


ANYSPEC = pl.BlockSpec(memory_space=pl.ANY)
VSPEC = pl.BlockSpec(memory_space=pltpu.VMEM)


FAR = (2, 4, 6)


def gather_start(place, base, block, out, sems):
    local, send, recv = sems[:3]
    pltpu.make_async_copy(block, out.at[place], local).start()
    for slot, mask in enumerate(FAR + (1,)):
        remote(
            block, out.at[place], send.at[slot], recv.at[slot], base + flip(place, mask)
        ).start()


def gather_finish(place, base, block, out, sems):
    local, send, recv, pass_send, pass_recv = sems
    for slot, mask in enumerate(FAR):
        came = out.at[flip(place, mask)]
        remote(block, came, send.at[slot], recv.at[slot], base + place).wait_recv()
        remote(
            came, came, pass_send.at[slot], pass_recv.at[slot], base + flip(place, 1)
        ).start()
    pltpu.make_async_copy(block, out.at[place], local).wait()
    for slot, mask in enumerate(FAR + (1,)):
        remote(block, out.at[place], send.at[slot], recv.at[slot], base + place).wait_send()
    remote(block, out.at[place], send.at[3], recv.at[3], base + place).wait_recv()
    for slot, mask in enumerate(FAR):
        came = out.at[flip(place, mask)]
        remote(came, came, pass_send.at[slot], pass_recv.at[slot], base + place).wait()


def gather_sems():
    return [DMA, DMA((4,)), DMA((4,)), DMA((3,)), DMA((3,))]


def gather_kernel(x_ref, out_ref, *sems):
    me = lax.axis_index("fsdp")
    place = me % GROUP
    base = me - place
    greet([base + flip(place, mask) for mask in FAR + (1,)])
    gather_start(place, base, x_ref, out_ref, sems)
    gather_finish(place, base, x_ref, out_ref, sems)


def plane_gather(block, collective_id):
    return pl.pallas_call(
        gather_kernel,
        out_shape=jax.ShapeDtypeStruct((GROUP,) + block.shape, block.dtype),
        in_specs=[VSPEC],
        out_specs=ANYSPEC,
        scratch_shapes=gather_sems(),
        compiler_params=params(collective_id),
        name=f"plane_gather_{collective_id}",
    )(block)


def scatter_kernel(count, *refs):
    parts = refs[:count]
    outs = refs[count : 2 * count]
    rest = refs[2 * count :]
    me = lax.axis_index("fsdp")
    place = me % GROUP
    base = me - place
    greet([base + flip(place, mask) for mask in FAR + (1,)])
    held = []
    for which in range(count):
        sib, stage, got, sib_send, sib_recv, send, recv = rest[7 * which : 7 * which + 7]
        part = parts[which]
        for slot, mask in enumerate(FAR + (0,)):
            remote(
                part.at[flip(place, mask ^ 1)],
                sib.at[slot],
                sib_send.at[slot],
                sib_recv.at[slot],
                base + flip(place, 1),
            ).start()
        held.append((part, outs[which], sib, stage, got, sib_send, sib_recv, send, recv))
    rows = parts[0].shape[1]
    step = 32
    for part, out, sib, stage, got, sib_send, sib_recv, send, recv in held:
        for slot, mask in enumerate(FAR):
            remote(
                part.at[0], sib.at[slot], sib_send.at[slot], sib_recv.at[slot], me
            ).wait_recv()
            target = flip(place, mask)

            def add(index, unused, part=part, sib=sib, stage=stage, slot=slot, target=target):
                span = pl.ds(pl.multiple_of(index * step, step), step)
                stage[slot, span, :] = (
                    part[target, span, :].astype(f32) + sib[slot, span, :].astype(f32)
                ).astype(bf16)
                return unused

            lax.fori_loop(0, rows // step, add, 0)
            remote(
                stage.at[slot], got.at[slot], send.at[slot], recv.at[slot], base + target
            ).start()
    for part, out, sib, stage, got, sib_send, sib_recv, send, recv in held:
        remote(part.at[0], sib.at[3], sib_send.at[3], sib_recv.at[3], me).wait_recv()
        for slot in range(3):
            remote(stage.at[slot], got.at[slot], send.at[slot], recv.at[slot], me).wait_recv()

        def total(index, unused, part=part, sib=sib, got=got, out=out):
            span = pl.ds(pl.multiple_of(index * step, step), step)
            value = part[place, span, :].astype(f32) + sib[3, span, :].astype(f32)
            for slot in range(3):
                value = value + got[slot, span, :].astype(f32)
            out[span, :] = value
            return unused

        lax.fori_loop(0, rows // step, total, 0)
    for part, out, sib, stage, got, sib_send, sib_recv, send, recv in held:
        for slot in range(4):
            remote(part.at[0], sib.at[slot], sib_send.at[slot], sib_recv.at[slot], me).wait_send()
        for slot in range(3):
            remote(stage.at[slot], got.at[slot], send.at[slot], recv.at[slot], me).wait_send()


def plane_scatter(parts, collective_id):
    rows, width = parts[0].shape[1:]
    scratch = []
    for part in parts:
        scratch += [
            VMEM((4, rows, width), bf16),
            VMEM((3, rows, width), bf16),
            VMEM((3, rows, width), bf16),
            DMA((4,)),
            DMA((4,)),
            DMA((3,)),
            DMA((3,)),
        ]
    return pl.pallas_call(
        functools.partial(scatter_kernel, len(parts)),
        out_shape=[jax.ShapeDtypeStruct((rows, width), f32) for part in parts],
        in_specs=[VSPEC] * len(parts),
        out_specs=[VSPEC] * len(parts),
        scratch_shapes=scratch,
        compiler_params=params(collective_id),
        name=f"plane_scatter_{collective_id}",
    )(*parts)


def line_gather(me, groups, outs, sems):
    mine = me // GROUP
    for step in range(groups - 1):
        for which, out in enumerate(outs):
            up_send, up_recv, down_send, down_recv = sems[4 * which : 4 * which + 4]

            @pl.when((mine - step >= 0) & (mine + 1 < groups))
            def _(out=out, up_send=up_send, up_recv=up_recv):
                slab = out.at[mine - step]
                remote(slab, slab, up_send.at[step], up_recv.at[step], me + GROUP).start()

            @pl.when((mine + step < groups) & (mine >= 1))
            def _(out=out, down_send=down_send, down_recv=down_recv):
                slab = out.at[mine + step]
                remote(slab, slab, down_send.at[step], down_recv.at[step], me - GROUP).start()

        for which, out in enumerate(outs):
            up_send, up_recv, down_send, down_recv = sems[4 * which : 4 * which + 4]

            @pl.when(mine - 1 - step >= 0)
            def _(out=out, up_send=up_send, up_recv=up_recv):
                slab = out.at[mine - 1 - step]
                remote(slab, slab, up_send.at[step], up_recv.at[step], me).wait_recv()

            @pl.when(mine + 1 + step < groups)
            def _(out=out, down_send=down_send, down_recv=down_recv):
                slab = out.at[mine + 1 + step]
                remote(slab, slab, down_send.at[step], down_recv.at[step], me).wait_recv()


def line_gather_drain(me, groups, outs, sems):
    mine = me // GROUP
    for step in range(groups - 1):
        for which, out in enumerate(outs):
            up_send, up_recv, down_send, down_recv = sems[4 * which : 4 * which + 4]

            @pl.when((mine - step >= 0) & (mine + 1 < groups))
            def _(out=out, up_send=up_send, up_recv=up_recv):
                slab = out.at[0]
                remote(slab, slab, up_send.at[step], up_recv.at[step], me).wait_send()

            @pl.when((mine + step < groups) & (mine >= 1))
            def _(out=out, down_send=down_send, down_recv=down_recv):
                slab = out.at[0]
                remote(slab, slab, down_send.at[step], down_recv.at[step], me).wait_send()


def line_sems(groups, arrays):
    return [DMA((groups,))] * (4 * arrays)


def spread_start(me, place, base, pack, out, local, send, recv):
    slot_of = me // GROUP
    pltpu.make_async_copy(pack.at[place], out.at[slot_of, place], local).start()
    for mask in range(1, GROUP):
        target = flip(place, mask)
        remote(
            pack.at[target],
            out.at[slot_of, place],
            send.at[mask],
            recv.at[mask],
            base + target,
        ).start()


def spread_wait(me, place, base, pack, out, local, send, recv):
    slot_of = me // GROUP
    pltpu.make_async_copy(pack.at[place], out.at[slot_of, place], local).wait()
    for mask in range(1, GROUP):
        source = flip(place, mask)
        remote(
            pack.at[source], out.at[slot_of, source], send.at[mask], recv.at[mask], base + place
        ).wait()


def fetch_kernel(
    count,
    x_ref,
    ct_ref,
    qkv_ref,
    up_ref,
    down_ref,
    out_ref,
    x_all,
    ct_all,
    qkv_all,
    up_all,
    down_all,
    out_all,
    *sems,
):
    groups = count // GROUP
    me = lax.axis_index("fsdp")
    place = me % GROUP
    base = me - place
    mine = me // GROUP
    x_sems, sems = sems[:5], sems[5:]
    ct_sems, sems = sems[:5], sems[5:]
    qkv_sems, sems = sems[:3], sems[3:]
    up_sems, sems = sems[:3], sems[3:]
    line_q, sems = sems[:4], sems[4:]
    line_u, sems = sems[:8], sems[8:]
    down_local, out_local, out_send, out_recv = sems
    greet_all(me, count)
    spread_start(me, place, base, qkv_ref, qkv_all, *qkv_sems)
    gather_start(place, base, x_ref, x_all, x_sems)
    pltpu.make_async_copy(down_ref, down_all.at[mine], down_local).start()
    per = count // GROUP
    wanted = me // per
    slot = me % per
    for group in range(groups):
        target = group * GROUP + wanted

        @pl.when(target != me)
        def _(target=target, group=group):
            remote(
                out_ref, out_all.at[slot], out_send.at[group], out_recv.at[slot], target
            ).start()

        @pl.when(target == me)
        def _(target=target, group=group):
            pltpu.make_async_copy(out_ref, out_all.at[slot], out_local).start()

    spread_wait(me, place, base, qkv_ref, qkv_all, *qkv_sems)
    spread_start(me, place, base, up_ref, up_all, *up_sems)
    line_gather(me, groups, [qkv_all], line_q)
    gather_finish(place, base, x_ref, x_all, x_sems)
    gather_start(place, base, ct_ref, ct_all, ct_sems)
    spread_wait(me, place, base, up_ref, up_all, *up_sems)
    pltpu.make_async_copy(down_ref, down_all.at[mine], down_local).wait()
    line_gather(me, groups, [up_all, down_all], line_u)
    gather_finish(place, base, ct_ref, ct_all, ct_sems)
    line_gather_drain(me, groups, [qkv_all], line_q)
    line_gather_drain(me, groups, [up_all, down_all], line_u)
    for group in range(groups):
        target = group * GROUP + wanted

        @pl.when(target != me)
        def _(group=group):
            remote(
                out_ref, out_all.at[slot], out_send.at[group], out_recv.at[slot], me
            ).wait_send()

        @pl.when(target == me)
        def _():
            pltpu.make_async_copy(out_ref, out_all.at[slot], out_local).wait()

    for index in range(per):
        owner = place * per + index

        @pl.when(owner != me)
        def _(index=index):
            remote(
                out_ref, out_all.at[index], out_send.at[0], out_recv.at[index], me
            ).wait_recv()


def fetch(count, x, ct, qkv, up, down, out, collective_id):
    groups = count // GROUP

    def shaped(*shape):
        return jax.ShapeDtypeStruct(shape, bf16)

    return pl.pallas_call(
        functools.partial(fetch_kernel, count),
        out_shape=[
            shaped(GROUP, *x.shape),
            shaped(GROUP, *ct.shape),
            shaped(groups, *qkv.shape),
            shaped(groups, *up.shape),
            shaped(groups, *down.shape),
            shaped(groups, *out.shape),
        ],
        in_specs=[VSPEC] * 6,
        out_specs=[ANYSPEC] * 6,
        scratch_shapes=gather_sems()
        + gather_sems()
        + [DMA, DMA((GROUP,)), DMA((GROUP,))] * 2
        + line_sems(groups, 1)
        + line_sems(groups, 2)
        + [DMA, DMA, DMA((groups,)), DMA((groups,))],
        compiler_params=params(collective_id),
        name="fetch",
    )(x, ct, qkv, up, down, out)


def add_slabs(blocks, store, *terms):
    def body(index, unused):
        value = terms[0](index).astype(f32)
        for term in terms[1:]:
            value = value + term(index).astype(f32)
        store(index, value)
        return unused

    lax.fori_loop(0, blocks, body, 0)


def line_sum(me, groups, own, stage, from_low, from_high, sems):
    up_send, up_recv, down_send, down_recv = sems
    mine = me // GROUP
    blocks = own.shape[1]

    def add(target, other):
        def store(index, value):
            stage[target, index] = value.astype(bf16)

        add_slabs(blocks, store, lambda index: own[target, index], lambda index: other[target, index])

    for target in range(groups - 1, 0, -1):
        low = groups - 1 - target

        def up(src, target=target):
            return remote(
                src.at[target],
                from_low.at[target],
                up_send.at[target],
                up_recv.at[target],
                me + GROUP,
            )

        def down(src, low=low):
            return remote(
                src.at[low], from_high.at[low], down_send.at[low], down_recv.at[low], me - GROUP
            )

        @pl.when((mine < target) & (mine == 0))
        def _(up=up):
            up(own).start()

        @pl.when((mine > low) & (mine == groups - 1))
        def _(down=down):
            down(own).start()

        @pl.when((mine < target) & (mine > 0))
        def _(up=up, target=target):
            up(own).wait_recv()
            add(target, from_low)
            up(stage).start()

        @pl.when((mine > low) & (mine < groups - 1))
        def _(down=down, low=low):
            down(own).wait_recv()
            add(low, from_high)
            down(stage).start()


def line_sum_finish(me, groups, own, from_low, from_high, total, sems):
    up_send, up_recv, down_send, down_recv = sems
    mine = me // GROUP
    blocks = own.shape[1]

    def store(index, value):
        total[index] = value

    def put(index, value):
        total[index] = total[index] + value

    add_slabs(blocks, store, lambda index: own[mine, index])
    for target in range(groups):
        low_copy = remote(
            own.at[target], from_low.at[target], up_send.at[target], up_recv.at[target], me
        )
        high_copy = remote(
            own.at[target], from_high.at[target], down_send.at[target], down_recv.at[target], me
        )

        @pl.when((mine == target) & (mine > 0))
        def _(low_copy=low_copy, target=target):
            low_copy.wait_recv()
            add_slabs(blocks, put, lambda index: from_low[target, index])

        @pl.when((mine == target) & (mine < groups - 1))
        def _(high_copy=high_copy, target=target):
            high_copy.wait_recv()
            add_slabs(blocks, put, lambda index: from_high[target, index])

        @pl.when(mine < target)
        def _(low_copy=low_copy):
            low_copy.wait_send()

        @pl.when(mine > target)
        def _(high_copy=high_copy):
            high_copy.wait_send()


def return_kernel(
    count,
    cols_ref,
    down_ref,
    out_ref,
    vec_ref,
    cols_all,
    down_total,
    out_all,
    vec_all,
    cols_stage,
    cols_low,
    cols_high,
    cols_total,
    cols_send,
    down_stage,
    down_low,
    down_high,
    *sems,
):
    groups = count // GROUP
    per = count // GROUP
    me = lax.axis_index("fsdp")
    place = me % GROUP
    base = me - place
    mine = me // GROUP
    line_c, line_d = sems[:4], sems[4:8]
    swap_local, swap_send, swap_recv = sems[8:11]
    out_local, out_send, out_recv = sems[11:14]
    vec_local, vec_send, vec_recv = sems[14:17]
    greet_all(me, count)

    def vec_copy(step):
        target = (me + step) % count
        return remote(
            vec_ref.at[target], vec_all.at[me], vec_send.at[step], vec_recv.at[step], target
        )

    def vec_start(step, unused):
        vec_copy(step).start()
        return unused

    lax.fori_loop(1, count, vec_start, 0)
    own_vec = pltpu.make_async_copy(vec_ref.at[me], vec_all.at[me], vec_local)
    own_vec.start()
    for index in range(per):
        owner = place * per + index

        @pl.when(owner != me)
        def _(index=index, owner=owner):
            remote(
                out_ref.at[index], out_all.at[mine], out_send.at[index], out_recv.at[mine], owner
            ).start()

        @pl.when(owner == me)
        def _(index=index):
            pltpu.make_async_copy(out_ref.at[index], out_all.at[mine], out_local).start()

    line_sum(me, groups, cols_ref, cols_stage, cols_low, cols_high, line_c)
    line_sum(me, groups, down_ref, down_stage, down_low, down_high, line_d)
    line_sum_finish(me, groups, cols_ref, cols_low, cols_high, cols_total, line_c)

    def narrow(index, value):
        cols_send[index] = value.astype(bf16)

    add_slabs(GROUP, narrow, lambda index: cols_total[index])
    own_cols = pltpu.make_async_copy(cols_send.at[place], cols_all.at[place], swap_local)
    own_cols.start()
    swaps = []
    for mask in range(1, GROUP):
        target = flip(place, mask)
        swap = remote(
            cols_send.at[target],
            cols_all.at[place],
            swap_send.at[mask],
            swap_recv.at[mask],
            base + target,
        )
        swap.start()
        swaps.append(swap)
    line_sum_finish(me, groups, down_ref, down_low, down_high, down_total, line_d)
    own_cols.wait()
    for swap in swaps:
        swap.wait()
    own_vec.wait()

    def vec_wait(step, unused):
        vec_copy(step).wait()
        return unused

    lax.fori_loop(1, count, vec_wait, 0)
    for index in range(per):
        owner = place * per + index

        @pl.when(owner != me)
        def _(index=index):
            remote(
                out_ref.at[index], out_all.at[mine], out_send.at[index], out_recv.at[mine], me
            ).wait_send()

        @pl.when(owner == me)
        def _(index=index):
            pltpu.make_async_copy(out_ref.at[index], out_all.at[mine], out_local).wait()

    wanted = me // per
    for group in range(groups):

        @pl.when(group * GROUP + wanted != me)
        def _(group=group):
            remote(
                out_ref.at[0], out_all.at[group], out_send.at[0], out_recv.at[group], me
            ).wait_recv()


def give_back(count, cols, down, out, vec, collective_id):
    groups = count // GROUP

    def line(array, kind=bf16):
        return VMEM(array.shape, kind)

    return pl.pallas_call(
        functools.partial(return_kernel, count),
        out_shape=[
            jax.ShapeDtypeStruct(cols.shape[1:], bf16),
            jax.ShapeDtypeStruct(down.shape[1:], f32),
            jax.ShapeDtypeStruct((groups,) + out.shape[1:], bf16),
            jax.ShapeDtypeStruct(vec.shape, f32),
        ],
        in_specs=[VSPEC] * 4,
        out_specs=[VSPEC] * 4,
        scratch_shapes=[
            line(cols),
            line(cols),
            line(cols),
            VMEM(cols.shape[1:], f32),
            VMEM(cols.shape[1:], bf16),
            line(down),
            line(down),
            line(down),
        ]
        + line_sems(groups, 2)
        + [DMA, DMA((GROUP,)), DMA((GROUP,))]
        + [DMA, DMA((groups,)), DMA((groups,))]
        + [DMA, DMA((count,)), DMA((count,))],
        compiler_params=params(collective_id),
        name="give_back",
    )(cols, down, out, vec)


QBLOCK = 256


def attend_kernel(length_ref, query_ref, key_ref, value_ref, mixed_ref, log_ref):
    length = length_ref[0]
    score_scale = 1.0 / math.sqrt(HD)
    scores = times_transposed(query_ref[...], key_ref[...]) * score_scale
    tail = scores[:, SURE:]
    place = SURE + lax.broadcasted_iota(jnp.int32, tail.shape, 1)
    scores = jnp.concatenate(
        [scores[:, :SURE], jnp.where(place < length, tail, masked_value)], axis=1
    )
    largest = jnp.max(scores, axis=-1, keepdims=True)
    exponent = jnp.exp(scores - largest)
    total = jnp.sum(exponent, axis=-1, keepdims=True)
    weights = (exponent * (1.0 / total)).astype(bf16)
    mixed_ref[...] = matmul(weights, value_ref[...]).astype(bf16)
    log_ref[0] = largest + jnp.log(total)


def attend(length, qkv):
    rows = qkv.shape[0]
    heads = HEADS_HERE
    return pl.pallas_call(
        attend_kernel,
        out_shape=[
            jax.ShapeDtypeStruct((rows, heads * LANES), bf16),
            jax.ShapeDtypeStruct((heads, rows, 1), f32),
        ],
        grid=(heads, rows // QBLOCK),
        in_specs=[
            pl.BlockSpec(memory_space=pltpu.SMEM),
            pl.BlockSpec((QBLOCK, LANES), lambda h, i: (i, h)),
            pl.BlockSpec((rows, LANES), lambda h, i: (0, heads + h)),
            pl.BlockSpec((rows, LANES), lambda h, i: (0, 2 * heads + h)),
        ],
        out_specs=[
            pl.BlockSpec((QBLOCK, LANES), lambda h, i: (i, h)),
            pl.BlockSpec((1, QBLOCK, 1), lambda h, i: (h, i, 0)),
        ],
        name="attend",
    )(length, qkv, qkv, qkv)


def attend_back_kernel(
    length_ref,
    query_ref,
    key_ref,
    value_ref,
    grad_ref,
    log_ref,
    grad_query_ref,
    grad_key_ref,
    grad_value_ref,
    key_sum,
    value_sum,
):
    length = length_ref[0]
    block = pl.program_id(1)
    score_scale = 1.0 / math.sqrt(HD)
    query = query_ref[...]
    key = key_ref[...]
    grad = grad_ref[...]
    scores = times_transposed(query, key) * score_scale
    tail = scores[:, SURE:]
    place = SURE + lax.broadcasted_iota(jnp.int32, tail.shape, 1)
    scores = jnp.concatenate(
        [scores[:, :SURE], jnp.where(place < length, tail, masked_value)], axis=1
    )
    weights = jnp.exp(scores - log_ref[0])
    grad_weights = times_transposed(grad, value_ref[...])
    inner = jnp.sum(weights * grad_weights, axis=-1, keepdims=True)
    grad_scores = (weights * (grad_weights - inner)).astype(bf16)
    grad_query_ref[...] = (matmul(grad_scores, key) * score_scale).astype(bf16)

    @pl.when(block == 0)
    def _():
        key_sum[...] = jnp.zeros_like(key_sum)
        value_sum[...] = jnp.zeros_like(value_sum)

    key_sum[...] += outer_sum(grad_scores, query)
    value_sum[...] += outer_sum(weights.astype(bf16), grad)

    @pl.when(block == pl.num_programs(1) - 1)
    def _():
        grad_key_ref[...] = (key_sum[...] * score_scale).astype(bf16)
        grad_value_ref[...] = value_sum[...].astype(bf16)


def attend_back(length, qkv, grad, log):
    rows = qkv.shape[0]
    heads = HEADS_HERE
    shape = jax.ShapeDtypeStruct((rows, heads * LANES), bf16)
    return pl.pallas_call(
        attend_back_kernel,
        out_shape=[shape] * 3,
        grid=(heads, rows // QBLOCK),
        in_specs=[
            pl.BlockSpec(memory_space=pltpu.SMEM),
            pl.BlockSpec((QBLOCK, LANES), lambda h, i: (i, h)),
            pl.BlockSpec((rows, LANES), lambda h, i: (0, heads + h)),
            pl.BlockSpec((rows, LANES), lambda h, i: (0, 2 * heads + h)),
            pl.BlockSpec((QBLOCK, LANES), lambda h, i: (i, h)),
            pl.BlockSpec((1, QBLOCK, 1), lambda h, i: (h, i, 0)),
        ],
        out_specs=[
            pl.BlockSpec((QBLOCK, LANES), lambda h, i: (i, h)),
            pl.BlockSpec((rows, LANES), lambda h, i: (0, h)),
            pl.BlockSpec((rows, LANES), lambda h, i: (0, h)),
        ],
        scratch_shapes=[VMEM((rows, LANES), f32), VMEM((rows, LANES), f32)],
        name="attend_back",
    )(length, qkv, qkv, qkv, grad, log)


def layer_norm(values, gain, offset):
    average = jnp.mean(values, axis=-1, keepdims=True)
    centred = values - average
    variance = jnp.mean(centred * centred, axis=-1, keepdims=True)
    return centred * lax.rsqrt(variance + epsilon) * gain + offset


def norm_backward(values, gain, grad_out):
    average = jnp.mean(values, axis=-1, keepdims=True)
    centred = values - average
    inverse = lax.rsqrt(jnp.mean(centred * centred, axis=-1, keepdims=True) + epsilon)
    xhat = centred * inverse
    scaled = grad_out * gain
    grad_values = inverse * (
        scaled
        - jnp.mean(scaled, axis=-1, keepdims=True)
        - xhat * jnp.mean(scaled * xhat, axis=-1, keepdims=True)
    )
    return grad_values, jnp.sum(grad_out * xhat, axis=0), jnp.sum(grad_out, axis=0)


def gelu_exact(values):
    return jax.nn.gelu(values, approximate=False)


def column_sums(matrix):
    return jnp.sum(matrix.astype(f32), axis=0)


def widen(cols, count):
    lead = cols.shape[:-1]
    split = cols.reshape(lead + (count, HD))
    return jnp.pad(split, [(0, 0)] * (len(lead) + 1) + [(0, LANES - HD)]).reshape(
        lead + (count * LANES,)
    )


def narrow(cols, count):
    lead = cols.shape[:-1]
    return cols.reshape(lead + (count, LANES))[..., :HD].reshape(lead + (count * HD,))


def on_device(
    inputs,
    ln1_gain,
    ln1_bias,
    w_query,
    b_query,
    w_key,
    w_value,
    b_value,
    w_out,
    b_out,
    ln2_gain,
    ln2_bias,
    w_up,
    b_up,
    w_down,
    b_down,
    lengths,
    cotangent,
):
    count = lax.axis_size("fsdp")
    groups = count // GROUP
    me = lax.axis_index("fsdp")
    place = me % GROUP
    few = w_query.shape[0]
    many = w_down.shape[0]
    rows = inputs.shape[0]
    wide = 3 * HEAD_COLS
    ff_here = groups * many

    qkv_pack = (
        jnp.stack([w_query, w_key, w_value], axis=1)
        .astype(bf16)
        .reshape(few, 3, GROUP, HEAD_COLS)
        .transpose(2, 0, 1, 3)
        .reshape(GROUP, few, wide)
    )
    small = (ln1_gain, ln1_bias, b_query, b_value, b_out, ln2_gain, ln2_bias, b_down, b_up)
    small = jnp.concatenate(small).astype(bf16)
    small_pack = jnp.broadcast_to(
        jnp.pad(small, (0, wide - small.shape[0]))[None, None], (GROUP, 1, wide)
    )
    qkv_pack = jnp.concatenate([qkv_pack, small_pack], axis=1)
    up_pack = (
        w_up.astype(bf16)
        .reshape(few, groups, GROUP, many)
        .transpose(2, 0, 1, 3)
        .reshape(GROUP, few, ff_here)
    )
    x_all, ct_all, qkv_all, up_all, down_all, out_all = fetch(
        count,
        inputs,
        cotangent,
        qkv_pack,
        up_pack,
        w_down.astype(bf16),
        w_out.astype(bf16),
        0,
    )
    w_qkv = widen(qkv_all[:, :, :few].reshape(D, wide), 3 * HEADS_HERE)
    small_all = qkv_all[:, :, few].reshape(count, wide).astype(f32)
    whole = [small_all[:, i * few : (i + 1) * few].reshape(D) for i in range(8)]
    g1, o1, bq, bv, bo, g2, o2, bd = whole
    b_up_all = small_all[:, 8 * few : 8 * few + many].reshape(groups, GROUP, many)
    b_up_here = lax.dynamic_index_in_dim(b_up_all, place, 1, keepdims=False).reshape(ff_here)
    w_up_here = up_all.reshape(D, ff_here)
    w_down_here = down_all.reshape(ff_here, D)
    w_out_here = out_all.reshape(HEADS_HERE, HD, D)
    w_out_here = jnp.pad(w_out_here, ((0, 0), (0, LANES - HD), (0, 0))).reshape(
        HEADS_HERE * LANES, D
    )

    def head_slice(vector):
        return lax.dynamic_slice_in_dim(vector, place * HEAD_COLS, HEAD_COLS)

    b_qkv = jnp.concatenate([head_slice(bq), jnp.zeros((HEAD_COLS,), f32), head_slice(bv)])
    b_qkv = widen(b_qkv, 3 * HEADS_HERE)
    length = lax.dynamic_slice_in_dim(lengths, me // GROUP, 1)

    clip = x_all.reshape(GROUP * rows, D).astype(f32)
    normed = layer_norm(clip, g1, o1).astype(bf16)
    qkv = (matmul(normed, w_qkv) + b_qkv).astype(bf16)
    attended, log = attend(length, qkv)
    part = matmul(attended, w_out_here).astype(bf16).reshape(GROUP, rows, D)
    (branch,) = plane_scatter([part], 1)
    source = inputs.astype(f32)
    residual = source + (branch + bo)
    normed_two_rows = layer_norm(residual, g2, o2).astype(bf16)
    normed_two = plane_gather(normed_two_rows, 2).reshape(GROUP * rows, D)
    ct = ct_all.reshape(GROUP * rows, D)
    hidden = matmul(normed_two, w_up_here) + b_up_here
    activated = gelu_exact(hidden).astype(bf16)
    out_part = matmul(activated, w_down_here).astype(bf16).reshape(GROUP, rows, D)

    grad_activated = times_transposed(ct, w_down_here)
    unused, gelu_pullback = jax.vjp(gelu_exact, hidden)
    grad_hidden = gelu_pullback(grad_activated)[0].astype(bf16)
    two_part = times_transposed(grad_hidden, w_up_here).astype(bf16).reshape(GROUP, rows, D)
    branch_two, grad_normed_two = plane_scatter([out_part, two_part], 3)
    output = residual + (branch_two + bd)
    grad_second, grad_g2, grad_o2 = norm_backward(residual, g2, grad_normed_two)
    grad_residual = cotangent.astype(f32) + grad_second
    grad_branch_rows = grad_residual.astype(bf16)
    grad_branch = plane_gather(grad_branch_rows, 4).reshape(GROUP * rows, D)
    grad_attended = times_transposed(grad_branch, w_out_here).astype(bf16)
    grad_parts = attend_back(length, qkv, grad_attended, log)
    grad_qkv = jnp.concatenate(grad_parts, axis=1)
    one_part = times_transposed(grad_qkv, w_qkv).astype(bf16).reshape(GROUP, rows, D)
    (grad_normed,) = plane_scatter([one_part], 5)
    grad_first, grad_g1, grad_o1 = norm_backward(source, g1, grad_normed)
    grad_inputs = grad_residual + grad_first

    grad_w_qkv = narrow(outer_sum(normed, grad_qkv), 3 * HEADS_HERE).astype(bf16)
    grad_w_up = outer_sum(normed_two, grad_hidden).astype(bf16)
    cols = jnp.concatenate([grad_w_qkv, grad_w_up], axis=1).reshape(
        groups, GROUP, few, wide + ff_here
    )
    down = outer_sum(activated, ct).astype(bf16).reshape(groups, many // few, few, D)
    out = outer_sum(attended, grad_branch).astype(bf16)
    out = out.reshape(HEADS_HERE, LANES, D)[:, :HD].reshape(groups, few, D)
    grad_b = narrow(column_sums(grad_qkv), 3 * HEADS_HERE)

    def spread_heads(part):
        return lax.dynamic_update_slice_in_dim(
            jnp.zeros((D,), f32), part, place * HEAD_COLS, 0
        ).reshape(count, few)

    grad_b_up = lax.dynamic_update_slice_in_dim(
        jnp.zeros((groups, GROUP, many), f32),
        column_sums(grad_hidden).reshape(groups, 1, many),
        place,
        1,
    ).reshape(count, many)
    vec = jnp.concatenate(
        [
            grad_g1.reshape(count, few),
            grad_o1.reshape(count, few),
            spread_heads(grad_b[:HEAD_COLS]),
            spread_heads(grad_b[2 * HEAD_COLS :]),
            column_sums(grad_branch_rows).reshape(count, few),
            grad_g2.reshape(count, few),
            grad_o2.reshape(count, few),
            column_sums(cotangent).reshape(count, few),
            grad_b_up,
        ],
        axis=1,
    )
    vec = jnp.pad(vec, ((0, 0), (0, 4 * LANES - vec.shape[1]))).reshape(count, 4, LANES)
    cols_all, down_total, out_got, vec_all = give_back(count, cols, down, out, vec, 6)
    cols_all = cols_all.astype(f32)

    def shard_of(which):
        piece = cols_all[:, :, which * HEAD_COLS : (which + 1) * HEAD_COLS]
        return piece.transpose(1, 0, 2).reshape(few, D)

    shard_w_up = (
        cols_all[:, :, wide:]
        .reshape(GROUP, few, groups, many)
        .transpose(1, 2, 0, 3)
        .reshape(few, groups * GROUP * many)
    )
    shard_w_out = jnp.sum(out_got.astype(f32), axis=0)
    vec_sum = jnp.sum(vec_all, axis=0).reshape(4 * LANES)
    shards = [vec_sum[i * few : (i + 1) * few] for i in range(8)]
    sg1, so1, sbq, sbv, sbo, sg2, so2, sbd = shards
    return (
        output,
        grad_inputs,
        sg1,
        so1,
        shard_of(0),
        sbq,
        shard_of(1),
        shard_of(2),
        sbv,
        shard_w_out,
        sbo,
        sg2,
        so2,
        shard_w_up,
        vec_sum[8 * few : 8 * few + many],
        down_total.reshape(many, D),
        sbd,
    )


def solution(mesh):
    in_specs = (
        P("fsdp", None),
        P("fsdp"),
        P("fsdp"),
        P("fsdp", None),
        P("fsdp"),
        P("fsdp", None),
        P("fsdp", None),
        P("fsdp"),
        P("fsdp", None),
        P("fsdp"),
        P("fsdp"),
        P("fsdp"),
        P("fsdp", None),
        P("fsdp"),
        P("fsdp", None),
        P("fsdp"),
        P(),
        P("fsdp", None),
    )
    out_specs = (
        P("fsdp", None),
        P("fsdp", None),
        P("fsdp"),
        P("fsdp"),
        P("fsdp", None),
        P("fsdp"),
        P("fsdp", None),
        P("fsdp", None),
        P("fsdp"),
        P("fsdp", None),
        P("fsdp"),
        P("fsdp"),
        P("fsdp"),
        P("fsdp", None),
        P("fsdp"),
        P("fsdp", None),
        P("fsdp"),
    )
    return jax.shard_map(
        on_device, mesh=mesh, in_specs=in_specs, out_specs=out_specs, check_vma=False
    )
```

time: 1660 us -> 595 us (0.36)
  the two profiles are of different devices: /device:TPU:0 before, /device:TPU:13 now
where the time goes in v1:
time: 595 us; the launch traced here: 589 us
  Pallas kernels  441 us (74%)
  matrix products  67.5 us (11%)
  other arithmetic  39.8 us (7%)
  local copies, waits for them, and re-layouts  39.4 us (7%)
    pallas_call x1, Pallas kernels, give_back(): pl.pallas_call(functools.partial(return_kernel, count), out_shape=[jax.Sh...  120 us
    pallas_call x3, Pallas kernels, plane_scatter(): pl.pallas_call(functools.partial(scatter_kernel, len(parts)), out_shape=[...  118 us
    pallas_call x1, Pallas kernels, fetch(): pl.pallas_call(functools.partial(fetch_kernel, count), out_shape=[shaped(...  107 us
    pallas_call x2, Pallas kernels, plane_gather(): pl.pallas_call(gather_kernel, out_shape=jax.ShapeDtypeStruct((GROUP,) + b...  56.1 us
    dot_general x4, matrix products, times_transposed(): lax.dot_general(left, right, (((1,), (1,)), ((), ())), preferred_element_...  25.2 us
    pallas_call x1, Pallas kernels, attend_back(): pl.pallas_call(attend_back_kernel, out_shape=[shape] * 3, grid=(heads, ro...  24.5 us
    dot_general x4, matrix products, matmul(): return jnp.dot(left, right, preferred_element_type=f32)  24.4 us
    dot_general x4, matrix products, outer_sum(): lax.dot_general(left, right, (((0,), (0,)), ((), ())), preferred_element_...  17.9 us

profile of v1, /device:TPU:13, one launch (start us, length us, event | category | flops | bytes accessed | tf_op | source)
XLA Modules:
  0.0 589.4 jit_solution(1436401693455445867)
XLA Ops:
  0.7 1.3 dynamic_slice.13.length_ref
  2.0 0.7 convert.46
  3.3 0.7 convert.48
  6.6 0.7 convert.54
  8.1 1.2 convert_reduce_fusion.3
  9.3 0.9 convert.43
  10.5 0.9 convert.44
  11.7 0.9 convert.45
  12.8 1.6 convert_element_type.112.out_ref
  15.2 1.3 maximum_bitcast_fusion
  16.8 0.8 pad_maximum_fusion.1.qkv_ref
  17.7 0.8 reshape.362
  18.8 1.2 reshape.363.up_ref
  19.9 0.8 convert_element_type.111.down_ref
  20.7 106.6 %fetch.1 = (bf16[8,192,1280]{2,1,0:T(8,128)(2,1)}, bf16[8,192,1280]{2,1,0:T(8,128)(2,1)}, bf16[4,8,41,480]{3,2,1,0:T(8,128)(2,1)}, bf16[4,8,40,640]{3,2,1,0:T(8,...) custom-call(bf16[192,1280]{1,0:T(8,128)(2,1)} %x_ref.1, bf16[192,1280]{1,0:T(8,128)(2,1)} %ct_ref.1, ...), custom_call_target="tpu_custom_call" | custom-call | tf_op jit(solution)/shard_map/fetch/pallas_call | solution.py:391
  127.3 2.9 convert_reduce_fusion
  130.6 1.2 fusion.2
  131.8 1.3 slice.97
  134.5 4.5 fusion.5
  139.0 3.7 reshape_reshape.3
  142.7 3.1 copy.54
  145.8 1.4 pad.16.clone
  147.3 1.3 copy-done.6
  148.6 6.8 %add_convert_fusion.query_ref.key_ref.value_ref = bf16[1536,768]{1,0:T(8,128)(2,1)} fusion(bf16[1536,1280]{1,0:T(8,128)(2,1)} %bitcast.79, bf16[1280,768]{0,1:T(8,128)(2,1)S(1)} %bitcast.91, f32[768]{0:T(1024)S(1)} %pad_bitcast_fusion), kind=kOutput, calls=%fused_computation.14 | convolution fusion | flops 3022258176 | bytes 8260608 | tf_op jit(solution)/shard_map/dot_general | solution.py:31
  155.4 15.8 %attend.1 = (bf16[1536,256]{1,0:T(8,128)(2,1)}, f32[2,1536,1]{2,1,0:T(8,128)}) custom-call(s32[1]{0:T(128)} %dynamic_slice.13.length_ref, bf16[1536,768]{1,0:T(8,128)(2,1)} %add_convert_fusion.query_ref.key_ref.value_ref, bf16[1536,768]{1,0:T(8,128)(2,1)} %add_convert_fusion.query_ref.key_ref.value_ref, ...), custom_call_target="tpu_custom_call" | custom-call | tf_op jit(solution)/shard_map/attend/pallas_call | solution.py:685
  171.2 4.2 convolution_convert_fusion.3
  175.4 35.4 %plane_scatter_1.1 = f32[192,1280]{1,0:T(8,128)} custom-call(bf16[8,192,1280]{2,1,0:T(8,128)(2,1)} %bitcast.73), custom_call_target="tpu_custom_call" | custom-call | tf_op jit(solution)/shard_map/plane_scatter_1/pallas_call | solution.py:217
  210.8 1.6 fusion.24
  212.6 1.0 add_convert_fusion.2.x_ref
  213.7 28.0 %plane_gather_2.1 = bf16[8,192,1280]{2,1,0:T(8,128)(2,1)} custom-call(bf16[192,1280]{1,0:T(8,128)(2,1)} %add_convert_fusion.2.x_ref), custom_call_target="tpu_custom_call" | custom-call | tf_op jit(solution)/shard_map/plane_gather_2/pallas_call | solution.py:131
  241.7 6.0 %fusion.28 = f32[1536,640]{1,0:T(8,128)S(1)} fusion(bf16[1536,1280]{1,0:T(8,128)(2,1)} %bitcast.82, bf16[1280,640]{1,0:T(8,128)(2,1)} %bitcast.106), kind=kOutput, calls=%fused_computation.93 | convolution fusion | flops 2516582400 | bytes 9502720 | tf_op jit(solution)/shard_map/dot_general | solution.py:31
  247.8 11.8 %convert_reduce_fusion.2 = (f32[640]{0:T(1024)S(1)}, bf16[1536,640]{1,0:T(8,128)(2,1)S(1)}, f32[1536,640]{1,0:T(8,128)S(1)}) fusion(f32[1536,640]{1,0:T(8,128)S(1)} %fusion.28, f32[640]{0:T(1024)S(1)} %add.149, bf16[1536,1280]{1,0:T(8,128)(2,1)S(1)} %bitcast.104, bf16[640,1280]{1,0:T(8,128)(2,1)S(1)} %bitcast.109), kind=kOutput, calls=%fused_computation.16 | convolution fusion | flops 2590309888 | bytes 15406080 | tf_op jit(solution)/shard_map/dot_general | solution.py:39
  259.7 4.2 convolution_convert_fusion.5
  264.4 4.1 convolution_convert_fusion.4
  268.7 7.3 %convolution_convert_fusion.2 = bf16[1536,1280]{1,0:T(8,128)(2,1)} fusion(bf16[1536,640]{1,0:T(8,128)(2,1)} %copy-done.7, bf16[640,1280]{1,0:T(8,128)(2,1)} %bitcast.108), kind=kOutput, calls=%fused_computation.10 | convolution fusion | flops 2518548480 | bytes 7536640 | tf_op jit(solution)/shard_map/dot_general | solution.py:31
  276.0 4.9 convolution_convert_fusion.1
  280.9 52.7 %plane_scatter_3.1 = (f32[192,1280]{1,0:T(8,128)}, f32[192,1280]{1,0:T(8,128)}) custom-call(bf16[8,192,1280]{2,1,0:T(8,128)(2,1)} %bitcast.81, bf16[8,192,1280]{2,1,0:T(8,128)(2,1)} %bitcast.84), custom_call_target="tpu_custom_call" | custom-call | tf_op jit(solution)/shard_map/plane_scatter_3/pallas_call | solution.py:217
  333.7 1.7 multiply_reduce_fusion
  335.4 3.7 convert_reduce_fusion.5
  339.4 28.0 %plane_gather_4.1 = bf16[8,192,1280]{2,1,0:T(8,128)(2,1)} custom-call(bf16[192,1280]{1,0:T(8,128)(2,1)} %get-tuple-element.63.x_ref), custom_call_target="tpu_custom_call" | custom-call | tf_op jit(solution)/shard_map/plane_gather_4/pallas_call | solution.py:131
  367.5 3.5 convolution_convert_fusion.6
  371.0 2.1 convolution_convert_fusion.7.grad_ref
  373.1 24.5 %attend_back.1 = (bf16[1536,256]{1,0:T(8,128)(2,1)}, bf16[1536,256]{1,0:T(8,128)(2,1)}, bf16[1536,256]{1,0:T(8,128)(2,1)}) custom-call(s32[1]{0:T(128)} %dynamic_slice.13.length_ref, bf16[1536,768]{1,0:T(8,128)(2,1)} %add_convert_fusion.query_ref.key_ref.value_ref, bf16[1536,768]{1,0:T(8,128)(2,1)} %add_convert_fusion.query_ref.key_ref.value_ref, ...), custom_call_target="tpu_custom_call" | custom-call | tf_op jit(solution)/shard_map/attend_back/pallas_call | solution.py:755
  397.6 0.8 slice.134
  398.4 1.2 constant_dynamic-update-slice_fusion.2
  399.6 1.2 constant_dynamic-update-slice_fusion.1
  402.0 6.3 %convolution_convert_fusion = bf16[1536,1280]{1,0:T(8,128)(2,1)} fusion(bf16[1536,768]{1,0:T(8,128)(2,1)S(1)} %constant_dynamic-update-slice_fusion, bf16[1280,768]{0,1:T(8,128)(2,1)} %bitcast.92), kind=kOutput, calls=%fused_computation.8 | convolution fusion | flops 3021864960 | bytes 8257536 | tf_op jit(solution)/shard_map/dot_general | solution.py:39
  408.3 29.9 %plane_scatter_5.1 = f32[192,1280]{1,0:T(8,128)} custom-call(bf16[8,192,1280]{2,1,0:T(8,128)(2,1)} %bitcast.78), custom_call_target="tpu_custom_call" | custom-call | tf_op jit(solution)/shard_map/plane_scatter_5/pallas_call | solution.py:217
  438.2 1.7 fusion.21
  439.9 2.8 fusion.20
  443.7 2.7 copy.47
  446.4 6.2 %fusion.29 = bf16[1280,6,128]{0,2,1:T(8,128)(2,1)S(1)} fusion(bf16[1536,1280,1]{1,0,2:T(8,128)(2,1)} %bitcast.80, bf16[6,128,1536]{2,1,0:T(8,128)(2,1)} %bitcast.90), kind=kOutput, calls=%fused_computation.94 | convolution fusion | flops 3019898880 | bytes 8257536 | tf_op jit(solution)/shard_map/dot_general | solution.py:35
  452.9 3.3 copy.48
  456.2 120.0 %give_back.1 = (bf16[8,40,1120]{2,1,0:T(8,128)(2,1)}, f32[4,40,1280]{2,1,0:T(8,128)}, bf16[4,40,1280]{2,1,0:T(8,128)(2,1)}, f32[32,4,128]{2,1,0:T(4,128)}) custom-call(bf16[4,8,40,1120]{3,2,1,0:T(8,128)(2,1)} %bitcast.75, bf16[4,4,40,1280]{3,2,1,0:T(8,128)(2,1)} %bitcast.94, bf16[4,40,1280]{2,1,0:T(8,128)(2,1)} %bitcast.93, f32[32,4,128]{2,1,0:T(4,128)} %reshape.394.vec_ref), custom_call_target="tpu_custom_call" | custom-call | tf_op jit(solution)/shard_map/give_back/pallas_call | solution.py:633
  576.2 0.9 reduce_sum.206
  578.4 1.8 convert_reduce_fusion.6
  580.1 1.3 slice.138
  581.4 0.9 reshape.399
  582.3 0.8 copy.52
  583.1 1.8 reshape.400
  585.4 0.8 reshape.398
  586.3 0.8 reshape.397
  587.2 0.8 reshape.396
  588.1 0.9 copy.67
  (122 shorter events, 13.7 us)
Async XLA Ops:
  0.7 17.0 %copy-start.10 = (f32[40,5120]{1,0:T(8,128)S(1)}, f32[40,5120]{1,0:T(8,128)}, u32[]{:S(2)}) copy-start(f32[40,5120]{1,0:T(8,128)} %param.30) | copy-start | bytes 2457604
  15.2 4.7 copy-start.11
  127.3 3.3 copy-start
  127.3 4.5 copy-start.9
  134.5 4.5 copy-start.14
  147.3 1.3 copy-start.6
  175.4 35.4 %copy-start.1 = (bf16[192,1280]{1,0:T(8,128)(2,1)S(1)}, bf16[192,1280]{1,0:T(8,128)(2,1)}, u32[]{:S(2)}) copy-start(bf16[192,1280]{1,0:T(8,128)(2,1)} %x_ref.1) | copy-start | bytes 1474564
  241.7 6.1 %copy-start.15 = (bf16[8,192,1280]{2,1,0:T(8,128)(2,1)S(1)}, bf16[8,192,1280]{2,1,0:T(8,128)(2,1)}, u32[]{:S(2)}) copy-start(bf16[8,192,1280]{2,1,0:T(8,128)(2,1)} %get-tuple-element.40) | copy-start | bytes 11796484
  241.7 6.1 %copy-start.17 = (bf16[4,160,1280]{2,1,0:T(8,128)(2,1)S(1)}, bf16[4,160,1280]{2,1,0:T(8,128)(2,1)}, u32[]{:S(2)}) copy-start(bf16[4,160,1280]{2,1,0:T(8,128)(2,1)} %get-tuple-element.39) | copy-start | bytes 4915204
  247.8 11.9 %copy-start.2 = (bf16[8,192,1280]{2,1,0:T(8,128)(2,1)S(1)}, bf16[8,192,1280]{2,1,0:T(8,128)(2,1)}, u32[]{:S(2)}) copy-start(bf16[8,192,1280]{2,1,0:T(8,128)(2,1)} %plane_gather_2.1) | copy-start | bytes 11796484
  259.6 4.2 copy-start.18
  264.4 4.1 copy-start.7
  268.6 7.3 %copy-start.16 = (bf16[4,8,40,640]{3,2,1,0:T(8,128)(2,1)S(1)}, bf16[4,8,40,640]{3,2,1,0:T(8,128)(2,1)}, u32[]{:S(2)}) copy-start(bf16[4,8,40,640]{3,2,1,0:T(8,128)(2,1)} %get-tuple-element.38) | copy-start | bytes 4915204
  268.7 7.3 %copy-start.19 = (bf16[1536,640]{1,0:T(8,128)(2,1)S(1)}, bf16[1536,640]{1,0:T(8,128)(2,1)}, u32[]{:S(2)}) copy-start(bf16[1536,640]{1,0:T(8,128)(2,1)} %copy-done.18) | copy-start | bytes 5898244
  335.4 32.1 %copy-start.5 = (bf16[1536,256]{1,0:T(8,128)(2,1)S(1)}, bf16[1536,256]{1,0:T(8,128)(2,1)}, u32[]{:S(2)}) copy-start(bf16[1536,256]{1,0:T(8,128)(2,1)} %get-tuple-element.36) | copy-start | bytes 2359300
  367.5 3.5 copy-start.3
  397.6 3.2 copy-start.13
  446.4 6.3 %copy-start.8 = (bf16[1280,640]{0,1:T(8,128)(2,1)S(1)}, bf16[1280,640]{0,1:T(8,128)(2,1)}, u32[]{:S(2)}) copy-start(bf16[1280,640]{0,1:T(8,128)(2,1)} %convolution_convert_fusion.5) | copy-start | bytes 4915204
  580.1 4.8 copy-start.4
  584.9 3.2 copy-start.12

commit v2 on v1

v2 whole, which is shorter than its diff:
```python
import functools
import math

import jax
import jax.numpy as jnp
from jax import lax
from jax.experimental import pallas as pl
from jax.experimental.pallas import tpu as pltpu
from jax.sharding import PartitionSpec as P

D = 1280
H = 16
HD = 80
CLIP_LEN = 1536
GROUP = 8
LANES = 128
HEADS_HERE = H // GROUP
HEAD_COLS = HEADS_HERE * HD
SURE = CLIP_LEN * 3 // 4

epsilon = 1e-05
masked_value = -1e30
MESH = pl.DeviceIdType.MESH
VMEM = pltpu.VMEM
DMA = pltpu.SemaphoreType.DMA
bf16 = jnp.bfloat16
f32 = jnp.float32


def matmul(left, right):
    return jnp.dot(left, right, preferred_element_type=f32)


def outer_sum(left, right):
    return lax.dot_general(left, right, (((0,), (0,)), ((), ())), preferred_element_type=f32)


def times_transposed(left, right):
    return lax.dot_general(left, right, (((1,), (1,)), ((), ())), preferred_element_type=f32)


def flip(place, mask):
    for bit in (1, 2, 4):
        if mask & bit:
            place = place + bit - 2 * bit * (place // bit % 2)
    return place


def remote(src, dst, send_sem, recv_sem, target):
    return pltpu.make_async_remote_copy(
        src_ref=src,
        dst_ref=dst,
        send_sem=send_sem,
        recv_sem=recv_sem,
        device_id=(target,),
        device_id_type=MESH,
    )


def greet(targets):
    barrier = pltpu.get_barrier_semaphore()
    for target in targets:
        pl.semaphore_signal(barrier, inc=1, device_id=(target,), device_id_type=MESH)
    pl.semaphore_wait(barrier, len(targets))


def greet_all(me, count):
    barrier = pltpu.get_barrier_semaphore()

    def signal(step, unused):
        pl.semaphore_signal(
            barrier, inc=1, device_id=((me + step) % count,), device_id_type=MESH
        )
        return unused

    lax.fori_loop(1, count, signal, 0)
    pl.semaphore_wait(barrier, count - 1)


def params(collective_id):
    return pltpu.CompilerParams(collective_id=collective_id, has_side_effects=True)


ANYSPEC = pl.BlockSpec(memory_space=pl.ANY)
VSPEC = pl.BlockSpec(memory_space=pltpu.VMEM)


FAR = (2, 4, 6)
PIECES = ((0, 2), (1, 4), (1, 2), (0, 4), (0, 6), (1, 6))


def half_of(ref, owner, half):
    rows = ref.shape[1] // 2
    return ref.at[owner, pl.ds(half * rows, rows)]


def gather_sems():
    return [DMA, DMA, DMA, DMA((6,)), DMA((6,)), DMA((6,)), DMA((6,))]


def gather_piece(place, base, block, out, sems, slot):
    send, recv = sems[3:5]
    half, mask = PIECES[slot]
    rows = block.shape[0] // 2
    if slot < 4:
        src = block.at[pl.ds(half * rows, rows)]
        dst = half_of(out, place, half)
        target = flip(place, mask)
    else:
        near, far = (2, 4) if half == 0 else (4, 2)
        src = half_of(out, flip(place, near), half)
        dst = src
        target = flip(place, far)
    return remote(src, dst, send.at[slot], recv.at[slot], base + target)


def gather_pass(place, base, out, sems, slot):
    pass_send, pass_recv = sems[5:7]
    half, mask = PIECES[slot]
    piece = half_of(out, flip(place, mask), half)
    return remote(piece, piece, pass_send.at[slot], pass_recv.at[slot], base + flip(place, 1))


def gather_own(place, base, block, out, sems):
    return remote(block, out.at[place], sems[1], sems[2], base + flip(place, 1))


def gather_start(place, base, block, out, sems):
    for slot in (0, 1, 2, 3):
        gather_piece(place, base, block, out, sems, slot).start()
    pltpu.make_async_copy(block, out.at[place], sems[0]).start()
    gather_own(place, base, block, out, sems).start()


def gather_relay(place, base, block, out, sems):
    for slot, relay in ((0, 4), (1, 5)):
        gather_piece(place, base, block, out, sems, slot).wait_recv()
        gather_piece(place, base, block, out, sems, relay).start()
        gather_pass(place, base, out, sems, slot).start()


def gather_finish(place, base, block, out, sems):
    for slot in (2, 3, 4, 5):
        gather_piece(place, base, block, out, sems, slot).wait_recv()
        gather_pass(place, base, out, sems, slot).start()
    pltpu.make_async_copy(block, out.at[place], sems[0]).wait()
    gather_own(place, base, block, out, sems).wait()
    for slot in range(6):
        gather_piece(place, base, block, out, sems, slot).wait_send()
        gather_pass(place, base, out, sems, slot).wait()


def gather_kernel(x_ref, out_ref, *sems):
    me = lax.axis_index("fsdp")
    place = me % GROUP
    base = me - place
    greet([base + flip(place, mask) for mask in FAR + (1,)])
    gather_start(place, base, x_ref, out_ref, sems)
    gather_relay(place, base, x_ref, out_ref, sems)
    gather_finish(place, base, x_ref, out_ref, sems)


def plane_gather(block, collective_id):
    return pl.pallas_call(
        gather_kernel,
        out_shape=jax.ShapeDtypeStruct((GROUP,) + block.shape, block.dtype),
        in_specs=[VSPEC],
        out_specs=ANYSPEC,
        scratch_shapes=gather_sems(),
        compiler_params=params(collective_id),
        name=f"plane_gather_{collective_id}",
    )(block)


ORDER = (6, 2, 4, 0)


def row_loop(rows, step, body):
    def run(index, unused):
        body(pl.ds(pl.multiple_of(index * step, step), step))
        return unused

    lax.fori_loop(0, rows // step, run, 0)


def scatter_scratch(rows, width, ready=False):
    half = rows // 2
    return [
        VMEM((4, rows, width) if ready else (4, 2, rows, width), bf16),
        VMEM((4, rows, width), bf16),
        VMEM((2, half, width), bf16),
        VMEM((2, rows, width), bf16),
        DMA((4,)),
        DMA((4,)),
        DMA((4,)),
        DMA((6,)),
        DMA((6,)),
    ]


SCATTER = 9


class Scatter:
    def __init__(self, place, base, scratch, ready=None):
        self.place, self.base, self.ready = place, base, ready
        self.parts, self.sib, self.relay, self.got = scratch[:4]
        self.local, self.sib_send, self.sib_recv, self.send, self.recv = scratch[4:]
        self.rows = self.got.shape[1]
        self.half = self.rows // 2

    def block(self, i, other):
        return flip(flip(self.place, ORDER[i]), 1 if other else 0)

    def keep(self, i):
        return self.parts.at[i, 1] if self.ready is None else self.parts.at[i]

    def sibling(self, i):
        if self.ready is None:
            src = self.parts.at[i, 0]
        else:
            src = self.ready.at[self.block(i, True)]
        return remote(
            src,
            self.sib.at[i],
            self.sib_send.at[i],
            self.sib_recv.at[i],
            self.base + flip(self.place, 1),
        )

    def load(self, i):
        return pltpu.make_async_copy(
            self.ready.at[self.block(i, False)], self.keep(i), self.local.at[i]
        )

    def begin(self):
        for i in range(4):
            self.sibling(i).start()
            self.load(i).start()

    def link(self, slot):
        half = slot % 2
        span = pl.ds(half * self.half, self.half)
        if slot < 2:
            i, mask, dst = 0, (2, 4)[half], self.relay.at[half]
        else:
            i = slot // 2
            mask, dst = ORDER[i], self.got.at[i - 1, span]
        return remote(
            self.keep(i).at[span],
            dst,
            self.send.at[slot],
            self.recv.at[slot],
            self.base + flip(self.place, mask),
        )

    def merge(self, i):
        if self.ready is not None:
            self.load(i).wait()
        self.sibling(i).wait_recv()
        keep = self.keep(i)

        def body(span):
            keep[span, :] = (
                keep[span, :].astype(f32) + self.sib[i, span, :].astype(f32)
            ).astype(bf16)

        row_loop(self.rows, 32, body)

    def merge_relay(self, i, half):
        self.link(half).wait_recv()
        start = half * self.half
        keep = self.keep(i)

        def run(index, unused):
            here = pl.multiple_of(index * 32, 32)
            span = pl.ds(start + here, 32)
            keep[span, :] = (
                keep[span, :].astype(f32) + self.relay[half, pl.ds(here, 32), :].astype(f32)
            ).astype(bf16)
            return unused

        lax.fori_loop(0, self.half // 32, run, 0)

    def after(self, i):
        if i < 3:
            self.merge(i)
        if i == 0:
            self.link(0).start()
            self.link(1).start()
        if i == 1:
            self.link(2).start()
        if i == 2:
            self.link(5).start()
            self.merge_relay(1, 1)
            self.link(3).start()
            self.merge_relay(2, 0)
            self.link(4).start()

    def finish(self, use):
        if self.ready is not None:
            self.load(3).wait()
        self.sibling(3).wait_recv()
        for slot in range(2, 6):
            self.link(slot).wait_recv()
        keep = self.keep(3)

        def body(span):
            value = keep[span, :].astype(f32) + self.sib[3, span, :].astype(f32)
            value = value + self.got[0, span, :].astype(f32)
            use(span, value + self.got[1, span, :].astype(f32))

        row_loop(self.rows, 32, body)

    def drain(self):
        for i in range(4):
            self.sibling(i).wait_send()
        for slot in range(6):
            self.link(slot).wait_send()


def line_send(me, groups, outs, sems, step):
    mine = me // GROUP
    for which, out in enumerate(outs):
        up_send, up_recv, down_send, down_recv = sems[4 * which : 4 * which + 4]

        @pl.when((mine - step >= 0) & (mine + 1 < groups))
        def _(out=out, up_send=up_send, up_recv=up_recv):
            slab = out.at[mine - step]
            remote(slab, slab, up_send.at[step], up_recv.at[step], me + GROUP).start()

        @pl.when((mine + step < groups) & (mine >= 1))
        def _(out=out, down_send=down_send, down_recv=down_recv):
            slab = out.at[mine + step]
            remote(slab, slab, down_send.at[step], down_recv.at[step], me - GROUP).start()


def line_wait(me, groups, outs, sems, step):
    mine = me // GROUP
    for which, out in enumerate(outs):
        up_send, up_recv, down_send, down_recv = sems[4 * which : 4 * which + 4]

        @pl.when(mine - 1 - step >= 0)
        def _(out=out, up_send=up_send, up_recv=up_recv):
            slab = out.at[mine - 1 - step]
            remote(slab, slab, up_send.at[step], up_recv.at[step], me).wait_recv()

        @pl.when(mine + 1 + step < groups)
        def _(out=out, down_send=down_send, down_recv=down_recv):
            slab = out.at[mine + 1 + step]
            remote(slab, slab, down_send.at[step], down_recv.at[step], me).wait_recv()


def line_gather(me, groups, outs, sems):
    for step in range(groups - 1):
        line_send(me, groups, outs, sems, step)
        line_wait(me, groups, outs, sems, step)


def line_gather_drain(me, groups, outs, sems):
    mine = me // GROUP
    for step in range(groups - 1):
        for which, out in enumerate(outs):
            up_send, up_recv, down_send, down_recv = sems[4 * which : 4 * which + 4]

            @pl.when((mine - step >= 0) & (mine + 1 < groups))
            def _(out=out, up_send=up_send, up_recv=up_recv):
                slab = out.at[0]
                remote(slab, slab, up_send.at[step], up_recv.at[step], me).wait_send()

            @pl.when((mine + step < groups) & (mine >= 1))
            def _(out=out, down_send=down_send, down_recv=down_recv):
                slab = out.at[0]
                remote(slab, slab, down_send.at[step], down_recv.at[step], me).wait_send()


def line_sems(groups, arrays):
    return [DMA((groups,))] * (4 * arrays)


def spread_start(me, place, base, pack, out, local, send, recv):
    slot_of = me // GROUP
    pltpu.make_async_copy(pack.at[place], out.at[slot_of, place], local).start()
    for mask in range(1, GROUP):
        target = flip(place, mask)
        remote(
            pack.at[target],
            out.at[slot_of, place],
            send.at[mask],
            recv.at[mask],
            base + target,
        ).start()


def spread_wait(me, place, base, pack, out, local, send, recv):
    slot_of = me // GROUP
    pltpu.make_async_copy(pack.at[place], out.at[slot_of, place], local).wait()
    for mask in range(1, GROUP):
        source = flip(place, mask)
        remote(
            pack.at[source], out.at[slot_of, source], send.at[mask], recv.at[mask], base + place
        ).wait()


def greet_near(me, place, base, groups, masks):
    barrier = pltpu.get_barrier_semaphore()
    mine = me // GROUP
    for mask in masks:
        pl.semaphore_signal(
            barrier, inc=1, device_id=(base + flip(place, mask),), device_id_type=MESH
        )

    @pl.when(mine > 0)
    def _():
        pl.semaphore_signal(barrier, inc=1, device_id=(me - GROUP,), device_id_type=MESH)

    @pl.when(mine < groups - 1)
    def _():
        pl.semaphore_signal(barrier, inc=1, device_id=(me + GROUP,), device_id_type=MESH)

    both = jnp.where(mine > 0, 1, 0) + jnp.where(mine < groups - 1, 1, 0)
    pl.semaphore_wait(barrier, len(masks) + both)


def fetch_kernel(count, x_ref, qkv_ref, out_ref, x_all, qkv_all, out_all, *sems):
    groups = count // GROUP
    me = lax.axis_index("fsdp")
    place = me % GROUP
    base = me - place
    x_sems, sems = sems[:7], sems[7:]
    qkv_sems, sems = sems[:3], sems[3:]
    line_q, sems = sems[:4], sems[4:]
    out_local, out_send, out_recv = sems
    greet_all(me, count)
    spread_start(me, place, base, qkv_ref, qkv_all, *qkv_sems)
    gather_start(place, base, x_ref, x_all, x_sems)
    spread_wait(me, place, base, qkv_ref, qkv_all, *qkv_sems)
    line_send(me, groups, [qkv_all], line_q, 0)
    per = count // GROUP
    wanted = me // per
    slot = me % per
    for group in range(groups):
        target = group * GROUP + wanted

        @pl.when(target != me)
        def _(target=target, group=group):
            remote(
                out_ref, out_all.at[slot], out_send.at[group], out_recv.at[slot], target
            ).start()

        @pl.when(target == me)
        def _(target=target, group=group):
            pltpu.make_async_copy(out_ref, out_all.at[slot], out_local).start()

    line_wait(me, groups, [qkv_all], line_q, 0)
    gather_relay(place, base, x_ref, x_all, x_sems)
    for step in range(1, groups - 1):
        line_send(me, groups, [qkv_all], line_q, step)
        line_wait(me, groups, [qkv_all], line_q, step)
    gather_finish(place, base, x_ref, x_all, x_sems)
    line_gather_drain(me, groups, [qkv_all], line_q)
    for group in range(groups):
        target = group * GROUP + wanted

        @pl.when(target != me)
        def _(group=group):
            remote(
                out_ref, out_all.at[slot], out_send.at[group], out_recv.at[slot], me
            ).wait_send()

        @pl.when(target == me)
        def _():
            pltpu.make_async_copy(out_ref, out_all.at[slot], out_local).wait()

    for index in range(per):
        owner = place * per + index

        @pl.when(owner != me)
        def _(index=index):
            remote(
                out_ref, out_all.at[index], out_send.at[0], out_recv.at[index], me
            ).wait_recv()


def shaped(*shape, kind=bf16):
    return jax.ShapeDtypeStruct(shape, kind)


def fetch(count, x, qkv, out, collective_id):
    groups = count // GROUP
    return pl.pallas_call(
        functools.partial(fetch_kernel, count),
        out_shape=[
            shaped(GROUP, *x.shape),
            shaped(groups, *qkv.shape),
            shaped(groups, *out.shape),
        ],
        in_specs=[VSPEC] * 3,
        out_specs=[ANYSPEC] * 3,
        scratch_shapes=gather_sems()
        + [DMA, DMA((GROUP,)), DMA((GROUP,))]
        + line_sems(groups, 1)
        + [DMA, DMA((groups,)), DMA((groups,))],
        compiler_params=params(collective_id),
        name="fetch",
    )(x, qkv, out)


def add_slabs(blocks, store, *terms):
    def body(index, unused):
        value = terms[0](index).astype(f32)
        for term in terms[1:]:
            value = value + term(index).astype(f32)
        store(index, value)
        return unused

    lax.fori_loop(0, blocks, body, 0)


def line_sum_scratch(groups, slabs, rows, width):
    return [
        VMEM((groups + 1, slabs, rows, width), bf16),
        VMEM((slabs, rows, width), f32),
    ] + line_sems(groups, 1)


LINE_SUM = 6


class LineSum:
    def __init__(self, me, groups, own, scratch):
        self.me, self.groups, self.own = me, groups, own
        self.came, self.total = scratch[:2]
        self.up_send, self.up_recv, self.down_send, self.down_recv = scratch[2:]
        self.mine = me // GROUP
        self.blocks = own.shape[1]

    def up(self, target, src):
        return remote(
            src.at[target],
            self.came.at[target],
            self.up_send.at[target],
            self.up_recv.at[target],
            self.me + GROUP,
        )

    def down(self, target, src):
        last = jnp.where(self.mine - 1 == target, self.groups, target)
        return remote(
            src.at[target],
            self.came.at[last],
            self.down_send.at[target],
            self.down_recv.at[target],
            self.me - GROUP,
        )

    def add(self, target):
        def store(index, value):
            self.came[target, index] = value.astype(bf16)

        add_slabs(
            self.blocks,
            store,
            lambda index: self.own[target, index],
            lambda index: self.came[target, index],
        )

    def begin(self):
        for target in range(self.groups - 1, 0, -1):
            low = self.groups - 1 - target

            @pl.when((self.mine == 0))
            def _(target=target):
                self.up(target, self.own).start()

            @pl.when(self.mine == self.groups - 1)
            def _(low=low):
                self.down(low, self.own).start()

    def tasks(self):
        def step(target):
            low = self.groups - 1 - target

            @pl.when((self.mine < target) & (self.mine > 0))
            def _():
                self.up(target, self.own).wait_recv()
                self.add(target)
                self.up(target, self.came).start()

            @pl.when((self.mine > low) & (self.mine < self.groups - 1))
            def _():
                self.down(low, self.own).wait_recv()
                self.add(low)
                self.down(low, self.came).start()

        return [functools.partial(step, target) for target in range(self.groups - 1, 0, -1)]

    def finish(self):
        def store(index, value):
            self.total[index] = value

        def put(index, value):
            self.total[index] = self.total[index] + value

        add_slabs(self.blocks, store, lambda index: self.own[self.mine, index])
        for target in range(self.groups):

            @pl.when((self.mine == target) & (target > 0))
            def _(target=target):
                self.up(target, self.own).wait_recv()
                add_slabs(self.blocks, put, lambda index: self.came[target, index])

            @pl.when((self.mine == target) & (target < self.groups - 1))
            def _(target=target):
                self.down(target, self.own).wait_recv()
                add_slabs(self.blocks, put, lambda index: self.came[self.groups, index])

    def drain(self):
        for target in range(self.groups):

            @pl.when(self.mine < target)
            def _(target=target):
                self.up(target, self.own).wait_send()

            @pl.when(self.mine > target)
            def _(target=target):
                self.down(target, self.own).wait_send()


def swap_scratch(rows, width):
    return [VMEM((GROUP, rows, width), bf16), DMA, DMA((GROUP,)), DMA((GROUP,))]


SWAP = 4


class Swap:
    def __init__(self, place, base, got, scratch):
        self.place, self.base, self.got = place, base, got
        self.give, self.local, self.send, self.recv = scratch

    def copy(self, mask):
        target = flip(self.place, mask)
        return remote(
            self.give.at[target],
            self.got.at[self.place],
            self.send.at[mask],
            self.recv.at[mask],
            self.base + target,
        )

    def own(self):
        return pltpu.make_async_copy(
            self.give.at[self.place], self.got.at[self.place], self.local
        )

    def begin(self, total):
        def store(index, value):
            self.give[index] = value.astype(bf16)

        add_slabs(GROUP, store, lambda index: total[index])
        for mask in range(1, GROUP):
            self.copy(mask).start()
        self.own().start()

    def finish(self):
        self.own().wait()
        for mask in range(1, GROUP):
            self.copy(mask).wait()


class Mail:
    def __init__(self, me, count, given, got, local, send, recv):
        self.me, self.count, self.given, self.got = me, count, given, got
        self.local, self.send, self.recv = local, send, recv

    def copy(self, step):
        target = (self.me + step) % self.count
        return remote(
            self.given.at[target],
            self.got.at[self.me],
            self.send.at[step],
            self.recv.at[step],
            target,
        )

    def own(self):
        return pltpu.make_async_copy(self.given.at[self.me], self.got.at[self.me], self.local)

    def begin(self):
        self.own().start()

        def run(step, unused):
            self.copy(step).start()
            return unused

        lax.fori_loop(1, self.count, run, 0)

    def finish(self, total):
        self.own().wait()

        def run(step, unused):
            self.copy(step).wait()
            return unused

        lax.fori_loop(1, self.count, run, 0)

        def add(index, value):
            return value + self.got[index]

        total[...] = lax.fori_loop(
            0, self.count, add, jnp.zeros(self.got.shape[1:], f32)
        )


def masked_scores(length, query, key):
    scores = times_transposed(query, key) * (1.0 / math.sqrt(HD))
    tail = scores[:, SURE:]
    place = SURE + lax.broadcasted_iota(jnp.int32, tail.shape, 1)
    return jnp.concatenate(
        [scores[:, :SURE], jnp.where(place < length, tail, masked_value)], axis=1
    )


def norm_rows(value):
    average = jnp.mean(value, axis=-1, keepdims=True)
    centred = value - average
    inverse = lax.rsqrt(jnp.mean(centred * centred, axis=-1, keepdims=True) + epsilon)
    return centred * inverse


def forward_kernel(
    count,
    length_ref,
    qkv_ref,
    w_out_ref,
    x_ref,
    vec_ref,
    ct_ref,
    up_ref,
    down_ref,
    mixed_ref,
    log_ref,
    residual_ref,
    two_all,
    ct_all,
    up_all,
    down_all,
    two_rows,
    *rest,
):
    groups = count // GROUP
    me = lax.axis_index("fsdp")
    place = me % GROUP
    base = me - place
    mine = me // GROUP
    scatter, rest = Scatter(place, base, rest[:SCATTER]), rest[SCATTER:]
    two_sems, rest = rest[:7], rest[7:]
    ct_sems, rest = rest[:7], rest[7:]
    up_sems, rest = rest[:3], rest[3:]
    line_u, (down_local,) = rest[:8], rest[8:]
    length = length_ref[0]
    rows = x_ref.shape[0]
    greet_near(me, place, base, groups, range(1, GROUP))
    spread_start(me, place, base, up_ref, up_all, *up_sems)
    own_down = pltpu.make_async_copy(down_ref, down_all.at[mine], down_local)
    own_down.start()
    gather_start(place, base, ct_ref, ct_all, ct_sems)
    line = [up_all, down_all]

    def first():
        spread_wait(me, place, base, up_ref, up_all, *up_sems)
        own_down.wait()
        line_send(me, groups, line, line_u, 0)
        gather_relay(place, base, ct_ref, ct_all, ct_sems)

    tasks = [first]
    for step in range(groups - 1):

        def task(step=step):
            line_wait(me, groups, line, line_u, step)
            if step < groups - 2:
                line_send(me, groups, line, line_u, step + 1)

        tasks.append(task)

    def attend_rows(block):
        here = pl.ds(pl.multiple_of(block * rows, rows), rows)
        for head in range(HEADS_HERE):
            cols = pl.ds(head * LANES, LANES)
            scores = masked_scores(
                length, qkv_ref[here, cols], qkv_ref[:, pl.ds((HEADS_HERE + head) * LANES, LANES)]
            )
            largest = jnp.max(scores, axis=-1, keepdims=True)
            exponent = jnp.exp(scores - largest)
            total = jnp.sum(exponent, axis=-1, keepdims=True)
            weights = (exponent * (1.0 / total)).astype(bf16)
            value = qkv_ref[:, pl.ds((2 * HEADS_HERE + head) * LANES, LANES)]
            mixed_ref[here, cols] = matmul(weights, value).astype(bf16)
            log_ref[head, here, :] = largest + jnp.log(total)
        return matmul(mixed_ref[here, :], w_out_ref[...]).astype(bf16)

    for i in range(4):

        def pair(turn, unused, i=i):
            block = jnp.where(turn == 0, scatter.block(i, True), scatter.block(i, False))
            scatter.parts[i, turn] = attend_rows(block)

            @pl.when(turn == 0)
            def _():
                scatter.sibling(i).start()

            return unused

        lax.fori_loop(0, 2, pair, 0)
        scatter.after(i)
        if tasks:
            tasks.pop(0)()

    def normalize(span, value):
        total = x_ref[span, :].astype(f32) + (value + vec_ref[0:1, :])
        residual_ref[span, :] = total
        two_rows[span, :] = (norm_rows(total) * vec_ref[1:2, :] + vec_ref[2:3, :]).astype(bf16)

    scatter.finish(normalize)
    gather_start(place, base, two_rows, two_all, two_sems)
    gather_finish(place, base, ct_ref, ct_all, ct_sems)
    for task in tasks:
        task()
    gather_relay(place, base, two_rows, two_all, two_sems)
    scatter.drain()
    gather_finish(place, base, two_rows, two_all, two_sems)
    line_gather_drain(me, groups, line, line_u)


def forward(count, length, qkv, w_out, x, vec, ct, up, down, collective_id):
    groups = count // GROUP
    rows, width = x.shape
    clip = qkv.shape[0]
    return pl.pallas_call(
        functools.partial(forward_kernel, count),
        out_shape=[
            shaped(clip, HEADS_HERE * LANES),
            shaped(HEADS_HERE, clip, 1, kind=f32),
            shaped(rows, width, kind=f32),
            shaped(GROUP, rows, width),
            shaped(GROUP, rows, width),
            shaped(groups, *up.shape),
            shaped(groups, *down.shape),
        ],
        in_specs=[pl.BlockSpec(memory_space=pltpu.SMEM)] + [VSPEC] * 7,
        out_specs=[VSPEC] * 3 + [ANYSPEC] * 4,
        scratch_shapes=[VMEM((rows, width), bf16)]
        + scatter_scratch(rows, width)
        + gather_sems()
        + gather_sems()
        + [DMA, DMA((GROUP,)), DMA((GROUP,))]
        + line_sems(groups, 2)
        + [DMA],
        compiler_params=params(collective_id),
        name="forward",
    )(length, qkv, w_out, x, vec, ct, up, down)


def norm_back_rows(value, gain, grad):
    average = jnp.mean(value, axis=-1, keepdims=True)
    centred = value - average
    inverse = lax.rsqrt(jnp.mean(centred * centred, axis=-1, keepdims=True) + epsilon)
    xhat = centred * inverse
    scaled = grad * gain
    moved = inverse * (
        scaled
        - jnp.mean(scaled, axis=-1, keepdims=True)
        - xhat * jnp.mean(scaled * xhat, axis=-1, keepdims=True)
    )
    return moved, grad * xhat


def fold(value):
    total = value[0:8]
    for index in range(1, value.shape[0] // 8):
        total = total + value[index * 8 : index * 8 + 8]
    return total


def middle_kernel(
    count,
    length_ref,
    two_ref,
    part_ref,
    residual_ref,
    ct_ref,
    vec_ref,
    w_out_ref,
    qkv_ref,
    log_ref,
    mixed_ref,
    up_ref,
    down_ref,
    output_ref,
    grad_ref,
    grad_qkv_ref,
    grad_out_ref,
    sums_ref,
    up_got,
    down_total,
    branch_rows,
    branch_all,
    key_sum,
    value_sum,
    grad_two,
    folded,
    *rest,
):
    groups = count // GROUP
    me = lax.axis_index("fsdp")
    place = me % GROUP
    base = me - place
    two, rest = Scatter(place, base, rest[:SCATTER], two_ref), rest[SCATTER:]
    last, rest = Scatter(place, base, rest[:SCATTER], part_ref), rest[SCATTER:]
    sems, rest = rest[:7], rest[7:]
    up_line, rest = LineSum(me, groups, up_ref, rest[:LINE_SUM]), rest[LINE_SUM:]
    down_line, rest = LineSum(me, groups, down_ref, rest[:LINE_SUM]), rest[LINE_SUM:]
    up_swap = Swap(place, base, up_got, rest)
    length = length_ref[0]
    rows = ct_ref.shape[0]
    score_scale = 1.0 / math.sqrt(HD)
    greet_near(me, place, base, groups, range(1, GROUP))
    two.begin()
    up_line.begin()
    down_line.begin()
    last.begin()
    tasks = up_line.tasks() + down_line.tasks()
    for i in range(3):
        two.after(i)
    tasks.pop(0)()
    key_sum[...] = jnp.zeros_like(key_sum)
    value_sum[...] = jnp.zeros_like(value_sum)
    folded[...] = jnp.zeros_like(folded)

    def through_norm(span, value):
        moved, by_xhat = norm_back_rows(residual_ref[span, :], vec_ref[0:1, :], value)
        cotangent = ct_ref[span, :].astype(f32)
        total = cotangent + moved
        grad_ref[span, :] = total
        branch = total.astype(bf16)
        branch_rows[span, :] = branch
        for index, term in enumerate((by_xhat, value, branch.astype(f32), cotangent)):
            folded[index] = folded[index] + fold(term)

    two.finish(through_norm)
    gather_start(place, base, branch_rows, branch_all, sems)
    for index in range(4):
        sums_ref[index : index + 1, :] = jnp.sum(folded[index], axis=0, keepdims=True)
    sums_ref[4:8, :] = jnp.zeros((4, sums_ref.shape[1]), f32)

    def attend_back(block):
        here = pl.ds(pl.multiple_of(block * rows, rows), rows)
        grads = times_transposed(branch_all[block], w_out_ref[...]).astype(bf16)
        for head in range(HEADS_HERE):
            cols = pl.ds(head * LANES, LANES)
            query = qkv_ref[here, cols]
            key = qkv_ref[:, pl.ds((HEADS_HERE + head) * LANES, LANES)]
            value = qkv_ref[:, pl.ds((2 * HEADS_HERE + head) * LANES, LANES)]
            grad = grads[:, head * LANES : (head + 1) * LANES]
            weights = jnp.exp(masked_scores(length, query, key) - log_ref[head, here, :])
            grad_weights = times_transposed(grad, value)
            inner = jnp.sum(weights * grad_weights, axis=-1, keepdims=True)
            grad_scores = (weights * (grad_weights - inner)).astype(bf16)
            grad_qkv_ref[here, cols] = (matmul(grad_scores, key) * score_scale).astype(bf16)
            key_sum[:, cols] += outer_sum(grad_scores, query)
            value_sum[:, cols] += outer_sum(weights.astype(bf16), grad)

    def attend_pair(first, second):
        def run(turn, unused):
            attend_back(jnp.where(turn == 0, flip(place, first), flip(place, second)))
            return unused

        lax.fori_loop(0, 2, run, 0)

    args = (place, base, branch_rows, branch_all, sems)
    pltpu.make_async_copy(branch_rows, branch_all.at[place], sems[0]).wait()
    gather_own(*args).wait_recv()
    attend_pair(0, 1)
    gather_relay(*args)
    for slot in (2, 3):
        gather_piece(*args, slot).wait_recv()
        gather_pass(place, base, branch_all, sems, slot).start()
    tasks.pop(0)()
    attend_pair(2, 4)
    for slot in (4, 5):
        gather_piece(*args, slot).wait_recv()
        gather_pass(place, base, branch_all, sems, slot).start()
    for slot in range(4):
        gather_pass(place, base, branch_all, sems, slot).wait_recv()
    last.after(0)
    tasks.pop(0)()
    attend_pair(3, 5)
    last.after(1)
    if tasks:
        tasks.pop(0)()
    for slot in (4, 5):
        gather_pass(place, base, branch_all, sems, slot).wait_recv()
    attend_pair(6, 7)
    last.after(2)
    for task in tasks:
        task()
    up_line.finish()
    up_swap.begin(up_line.total)
    cols = pl.ds(HEADS_HERE * LANES, HEADS_HERE * LANES)
    grad_qkv_ref[:, cols] = (key_sum[...] * score_scale).astype(bf16)
    cols = pl.ds(2 * HEADS_HERE * LANES, HEADS_HERE * LANES)
    grad_qkv_ref[:, cols] = value_sum[...].astype(bf16)
    grad_out = jnp.zeros(grad_out_ref.shape, f32)
    for block in range(GROUP):
        grad_out = grad_out + outer_sum(
            mixed_ref[block * rows : (block + 1) * rows, :], branch_all[block]
        )
    grad_out_ref[...] = grad_out.astype(bf16)

    def residual_and(span, value):
        output_ref[span, :] = residual_ref[span, :] + (value + vec_ref[1:2, :])

    last.finish(residual_and)
    down_line.finish()
    add_slabs(
        down_total.shape[0],
        lambda index, value: down_total.__setitem__(index, value),
        lambda index: down_line.total[index],
    )
    up_swap.finish()
    gather_own(*args).wait_send()
    for slot in range(6):
        gather_piece(*args, slot).wait_send()
        gather_pass(place, base, branch_all, sems, slot).wait_send()
    two.drain()
    last.drain()
    up_line.drain()
    down_line.drain()


def middle(count, length, two, part, residual, ct, vec, w_out, qkv, log, mixed, up, down, cid):
    groups = count // GROUP
    rows, width = ct.shape
    clip = qkv.shape[0]
    wide = HEADS_HERE * LANES
    return pl.pallas_call(
        functools.partial(middle_kernel, count),
        out_shape=[
            shaped(rows, width, kind=f32),
            shaped(rows, width, kind=f32),
            shaped(clip, 3 * wide),
            shaped(wide, width),
            shaped(8, width, kind=f32),
            shaped(*up.shape[1:]),
            shaped(*down.shape[1:], kind=f32),
        ],
        in_specs=[pl.BlockSpec(memory_space=pltpu.SMEM)] + [ANYSPEC] * 2 + [VSPEC] * 9,
        out_specs=[VSPEC] * 7,
        scratch_shapes=[
            VMEM((rows, width), bf16),
            VMEM((GROUP, rows, width), bf16),
            VMEM((clip, wide), f32),
            VMEM((clip, wide), f32),
            VMEM((8, width), f32),
            VMEM((4, 8, width), f32),
        ]
        + scatter_scratch(rows, width, True)
        + scatter_scratch(rows, width, True)
        + gather_sems()
        + line_sum_scratch(groups, *up.shape[1:])
        + line_sum_scratch(groups, *down.shape[1:])
        + swap_scratch(*up.shape[2:]),
        compiler_params=params(cid),
        name="middle",
    )(length, two, part, residual, ct, vec, w_out, qkv, log, mixed, up, down)


def last_kernel(
    count,
    x_ref,
    normed_ref,
    grad_qkv_ref,
    w_qkv_ref,
    grad_ref,
    gain_ref,
    early_ref,
    out_ref,
    grad_inputs_ref,
    qkv_got,
    out_total,
    early_total,
    late_total,
    own_cols,
    cols,
    folded,
    late,
    early_got,
    late_got,
    out_got,
    *rest,
):
    groups = count // GROUP
    per = groups
    me = lax.axis_index("fsdp")
    place = me % GROUP
    base = me - place
    mine = me // GROUP
    rows, width = x_ref.shape
    few = own_cols.shape[2]
    one, rest = Scatter(place, base, rest[:SCATTER]), rest[SCATTER:]
    line, rest = LineSum(me, groups, own_cols, rest[:LINE_SUM]), rest[LINE_SUM:]
    swap, rest = Swap(place, base, qkv_got, rest[:SWAP]), rest[SWAP:]
    early_mail = Mail(me, count, early_ref, early_got, *rest[:3])
    late_mail = Mail(me, count, late, late_got, *rest[3:6])
    out_local, out_send, out_recv = rest[6:]
    greet_all(me, count)
    early_mail.begin()
    for index in range(per):
        owner = place * per + index

        @pl.when(owner != me)
        def _(index=index, owner=owner):
            remote(
                out_ref.at[index], out_got.at[mine], out_send.at[index], out_recv.at[mine], owner
            ).start()

        @pl.when(owner == me)
        def _(index=index):
            pltpu.make_async_copy(out_ref.at[index], out_got.at[mine], out_local).start()

    padded = 3 * HEADS_HERE * LANES
    packed = 3 * HEAD_COLS
    row = lax.broadcasted_iota(jnp.int32, (padded, packed), 0)
    col = lax.broadcasted_iota(jnp.int32, (padded, packed), 1)
    pick = jnp.where(
        (row // LANES == col // HD) & (row % LANES == col % HD), 1.0, 0.0
    ).astype(bf16)

    def weight_grad(index, unused):
        tile = pl.ds(pl.multiple_of(index * 256, 256), 256)
        grad = outer_sum(normed_ref[:, tile], grad_qkv_ref[...]).astype(bf16)
        cols[tile, :] = matmul(grad, pick)
        return unused

    lax.fori_loop(0, width // 256, weight_grad, 0)
    for owner in range(count):
        own_cols[owner // GROUP, owner % GROUP] = cols[owner * few : (owner + 1) * few, :].astype(
            bf16
        )
    line.begin()
    tasks = line.tasks()
    for i in range(4):

        def pair(turn, unused, i=i):
            block = jnp.where(turn == 0, one.block(i, True), one.block(i, False))
            here = pl.ds(pl.multiple_of(block * rows, rows), rows)
            one.parts[i, turn] = times_transposed(grad_qkv_ref[here, :], w_qkv_ref[...]).astype(
                bf16
            )

            @pl.when(turn == 0)
            def _():
                one.sibling(i).start()

            return unused

        lax.fori_loop(0, 2, pair, 0)
        one.after(i)
        if tasks and i > 0:
            tasks.pop(0)()
    for task in tasks:
        task()
    folded[...] = jnp.zeros_like(folded)

    def through_norm(span, value):
        moved, by_xhat = norm_back_rows(x_ref[span, :].astype(f32), gain_ref[0:1, :], value)
        grad_inputs_ref[span, :] = grad_ref[span, :] + moved
        folded[0] = folded[0] + fold(by_xhat)
        folded[1] = folded[1] + fold(value)

    one.finish(through_norm)
    line.finish()
    swap.begin(line.total)

    wide = HEADS_HERE * LANES

    def bias_sum(which):
        def add(index, value):
            span = pl.ds(pl.multiple_of(index * 64, 64), 64)
            return value + fold(grad_qkv_ref[span, which * wide : (which + 1) * wide].astype(f32))

        total = lax.fori_loop(
            0, grad_qkv_ref.shape[0] // 64, add, jnp.zeros((8, wide), f32)
        )
        row = lax.broadcasted_iota(jnp.int32, (wide, width), 0)
        col = lax.broadcasted_iota(jnp.int32, (wide, width), 1) - place * HEAD_COLS
        fits = (col >= 0) & (col < HEAD_COLS) & (row % LANES < HD)
        spot = jnp.where(fits & (row // LANES * HD + row % LANES == col), 1.0, 0.0)
        return jnp.sum(
            jnp.dot(total, spot, precision=lax.Precision.HIGHEST, preferred_element_type=f32),
            axis=0,
            keepdims=True,
        )

    vectors = jnp.concatenate(
        [
            jnp.sum(folded[0], axis=0, keepdims=True),
            jnp.sum(folded[1], axis=0, keepdims=True),
            bias_sum(0),
            bias_sum(2),
            jnp.zeros((4, width), f32),
        ],
        axis=0,
    )
    stretch = lax.broadcasted_iota(jnp.int32, (1, width), 1)
    row = lax.broadcasted_iota(jnp.int32, (width, LANES), 0)
    lane = lax.broadcasted_iota(jnp.int32, (width, LANES), 1)
    spot = jnp.where(row % few == lane, 1.0, 0.0)
    many = 8

    def owners(index, unused):
        terms = [
            jnp.where(stretch // few == index * many + k, vectors, 0.0) for k in range(many)
        ]
        slabs = jnp.dot(
            jnp.concatenate(terms, axis=0),
            spot,
            precision=lax.Precision.HIGHEST,
            preferred_element_type=f32,
        )
        for k in range(many):
            late[index * many + k] = slabs[k * 8 : k * 8 + 8]
        return unused

    lax.fori_loop(0, count // many, owners, 0)
    late_mail.begin()
    early_mail.finish(early_total)
    for index in range(per):
        owner = place * per + index

        @pl.when(owner != me)
        def _(index=index):
            remote(
                out_ref.at[index], out_got.at[mine], out_send.at[index], out_recv.at[mine], me
            ).wait_send()

        @pl.when(owner == me)
        def _(index=index):
            pltpu.make_async_copy(out_ref.at[index], out_got.at[mine], out_local).wait()

    for group in range(groups):

        @pl.when(group * GROUP + me // per != me)
        def _(group=group):
            remote(
                out_ref.at[0], out_got.at[group], out_send.at[0], out_recv.at[group], me
            ).wait_recv()

    total = out_got[0].astype(f32)
    for group in range(1, groups):
        total = total + out_got[group].astype(f32)
    out_total[...] = total
    swap.finish()
    late_mail.finish(late_total)
    one.drain()
    line.drain()


def last(count, x, normed, grad_qkv, w_qkv, grad, gain, early, out, collective_id):
    groups = count // GROUP
    rows, width = x.shape
    few = width // count
    packed = 3 * HEAD_COLS

    def mail(shape):
        return [DMA, DMA((count,)), DMA((count,))]

    return pl.pallas_call(
        functools.partial(last_kernel, count),
        out_shape=[
            shaped(rows, width, kind=f32),
            shaped(GROUP, few, packed),
            shaped(few, width, kind=f32),
            shaped(*early.shape[1:], kind=f32),
            shaped(8, LANES, kind=f32),
        ],
        in_specs=[VSPEC] * 8,
        out_specs=[VSPEC] * 5,
        scratch_shapes=[
            VMEM((groups, GROUP, few, packed), bf16),
            VMEM((width, packed), f32),
            VMEM((2, 8, width), f32),
            VMEM((count, 8, LANES), f32),
            VMEM(early.shape, f32),
            VMEM((count, 8, LANES), f32),
            VMEM((groups, few, width), bf16),
        ]
        + scatter_scratch(rows, width)
        + line_sum_scratch(groups, GROUP, few, packed)
        + swap_scratch(few, packed)
        + mail(early)
        + mail(early)
        + [DMA, DMA((groups,)), DMA((groups,))],
        compiler_params=params(collective_id),
        name="last",
    )(x, normed, grad_qkv, w_qkv, grad, gain, early, out)


def layer_norm(values, gain, offset):
    average = jnp.mean(values, axis=-1, keepdims=True)
    centred = values - average
    variance = jnp.mean(centred * centred, axis=-1, keepdims=True)
    return centred * lax.rsqrt(variance + epsilon) * gain + offset


def gelu_exact(values):
    return jax.nn.gelu(values, approximate=False)


def column_sums(matrix):
    return jnp.sum(matrix.astype(f32), axis=0)


def widen(cols, count):
    lead = cols.shape[:-1]
    split = cols.reshape(lead + (count, HD))
    return jnp.pad(split, [(0, 0)] * (len(lead) + 1) + [(0, LANES - HD)]).reshape(
        lead + (count * LANES,)
    )


def on_device(
    inputs,
    ln1_gain,
    ln1_bias,
    w_query,
    b_query,
    w_key,
    w_value,
    b_value,
    w_out,
    b_out,
    ln2_gain,
    ln2_bias,
    w_up,
    b_up,
    w_down,
    b_down,
    lengths,
    cotangent,
):
    count = lax.axis_size("fsdp")
    groups = count // GROUP
    me = lax.axis_index("fsdp")
    place = me % GROUP
    few = w_query.shape[0]
    many = w_down.shape[0]
    rows = inputs.shape[0]
    wide = 3 * HEAD_COLS
    ff_here = groups * many

    qkv_pack = (
        jnp.stack([w_query, w_key, w_value], axis=1)
        .astype(bf16)
        .reshape(few, 3, GROUP, HEAD_COLS)
        .transpose(2, 0, 1, 3)
        .reshape(GROUP, few, wide)
    )
    small = (ln1_gain, ln1_bias, b_query, b_value, b_out, ln2_gain, ln2_bias, b_down, b_up)
    small = jnp.concatenate(small).astype(bf16)
    small_pack = jnp.broadcast_to(
        jnp.pad(small, (0, wide - small.shape[0]))[None, None], (GROUP, 1, wide)
    )
    qkv_pack = jnp.concatenate([qkv_pack, small_pack], axis=1)
    up_pack = (
        w_up.astype(bf16)
        .reshape(few, groups, GROUP, many)
        .transpose(2, 0, 1, 3)
        .reshape(GROUP, few, ff_here)
    )
    x_all, qkv_all, out_all = fetch(count, inputs, qkv_pack, w_out.astype(bf16), 0)
    w_qkv = widen(qkv_all[:, :, :few].reshape(D, wide), 3 * HEADS_HERE)
    small_all = qkv_all[:, :, few].reshape(count, wide).astype(f32)
    whole = [small_all[:, i * few : (i + 1) * few].reshape(D) for i in range(8)]
    g1, o1, bq, bv, bo, g2, o2, bd = whole
    b_up_all = small_all[:, 8 * few : 8 * few + many].reshape(groups, GROUP, many)
    b_up_here = lax.dynamic_index_in_dim(b_up_all, place, 1, keepdims=False).reshape(ff_here)
    w_out_here = out_all.reshape(HEADS_HERE, HD, D)
    w_out_here = jnp.pad(w_out_here, ((0, 0), (0, LANES - HD), (0, 0))).reshape(
        HEADS_HERE * LANES, D
    )

    def head_slice(vector):
        return lax.dynamic_slice_in_dim(vector, place * HEAD_COLS, HEAD_COLS)

    b_qkv = jnp.concatenate([head_slice(bq), jnp.zeros((HEAD_COLS,), f32), head_slice(bv)])
    b_qkv = widen(b_qkv, 3 * HEADS_HERE)
    length = lax.dynamic_slice_in_dim(lengths, me // GROUP, 1)

    clip = x_all.reshape(GROUP * rows, D).astype(f32)
    normed = layer_norm(clip, g1, o1).astype(bf16)
    qkv = (matmul(normed, w_qkv) + b_qkv).astype(bf16)
    source = inputs.astype(f32)
    norm_vec = jnp.pad(jnp.stack([bo, g2, o2]), ((0, 5), (0, 0)))
    attended, log, residual, two_all, ct_all, up_all, down_all = forward(
        count,
        length,
        qkv,
        w_out_here,
        inputs,
        norm_vec,
        cotangent,
        up_pack,
        w_down.astype(bf16),
        1,
    )
    w_up_here = up_all.reshape(D, ff_here)
    w_down_here = down_all.reshape(ff_here, D)
    normed_two = two_all.reshape(GROUP * rows, D)
    ct = ct_all.reshape(GROUP * rows, D)
    hidden = matmul(normed_two, w_up_here) + b_up_here
    activated = gelu_exact(hidden).astype(bf16)
    out_part = matmul(activated, w_down_here).astype(bf16).reshape(GROUP, rows, D)

    grad_activated = times_transposed(ct, w_down_here)
    unused, gelu_pullback = jax.vjp(gelu_exact, hidden)
    grad_hidden = gelu_pullback(grad_activated)[0].astype(bf16)
    two_part = times_transposed(grad_hidden, w_up_here).astype(bf16).reshape(GROUP, rows, D)
    grad_w_up = outer_sum(normed_two, grad_hidden).astype(bf16)
    grad_w_down = outer_sum(activated, ct).astype(bf16)
    back_vec = jnp.pad(jnp.stack([g2, bd]), ((0, 6), (0, 0)))
    output, grad_residual, grad_qkv, grad_out, sums, up_got, down_total = middle(
        count,
        length,
        two_part,
        out_part,
        residual,
        cotangent,
        back_vec,
        w_out_here,
        qkv,
        log,
        attended,
        grad_w_up.reshape(groups, GROUP, few, ff_here),
        grad_w_down.reshape(groups, many // few, few, D),
        2,
    )
    grad_out = grad_out.reshape(HEADS_HERE, LANES, D)[:, :HD].reshape(groups, few, D)
    up_lanes = -(-many // LANES)
    grad_b_up = jnp.pad(
        column_sums(grad_hidden).reshape(groups, 1, many),
        ((0, 0), (0, 0), (0, up_lanes * LANES - many)),
    ).reshape(groups, 1, up_lanes, LANES)
    grad_b_up = jnp.where(
        (jnp.arange(GROUP) == place)[None, :, None, None], grad_b_up, 0.0
    ).reshape(count, up_lanes, LANES)
    early = jnp.pad(
        sums[:4].reshape(4, count, few).transpose(1, 0, 2), ((0, 0), (0, 0), (0, LANES - few))
    )
    early = jnp.concatenate(
        [early, grad_b_up, jnp.zeros((count, 4 - up_lanes, LANES), f32)], axis=1
    )
    grad_inputs, qkv_got, shard_w_out, early_sum, late_sum = last(
        count,
        inputs,
        normed,
        grad_qkv,
        w_qkv,
        grad_residual,
        jnp.pad(g1[None], ((0, 7), (0, 0))),
        early,
        grad_out,
        3,
    )

    def shard_of(which):
        piece = qkv_got[:, :, which * HEAD_COLS : (which + 1) * HEAD_COLS]
        return piece.transpose(1, 0, 2).reshape(few, D).astype(f32)

    shard_w_up = (
        up_got.reshape(GROUP, few, groups, many)
        .transpose(1, 2, 0, 3)
        .reshape(few, groups * GROUP * many)
        .astype(f32)
    )
    return (
        output,
        grad_inputs,
        late_sum[0, :few],
        late_sum[1, :few],
        shard_of(0),
        late_sum[2, :few],
        shard_of(1),
        shard_of(2),
        late_sum[3, :few],
        shard_w_out,
        early_sum[2, :few],
        early_sum[0, :few],
        early_sum[1, :few],
        shard_w_up,
        early_sum[4 : 4 + up_lanes].reshape(up_lanes * LANES)[:many],
        down_total.reshape(many, D),
        early_sum[3, :few],
    )


def solution(mesh):
    in_specs = (
        P("fsdp", None),
        P("fsdp"),
        P("fsdp"),
        P("fsdp", None),
        P("fsdp"),
        P("fsdp", None),
        P("fsdp", None),
        P("fsdp"),
        P("fsdp", None),
        P("fsdp"),
        P("fsdp"),
        P("fsdp"),
        P("fsdp", None),
        P("fsdp"),
        P("fsdp", None),
        P("fsdp"),
        P(),
        P("fsdp", None),
    )
    out_specs = (
        P("fsdp", None),
        P("fsdp", None),
        P("fsdp"),
        P("fsdp"),
        P("fsdp", None),
        P("fsdp"),
        P("fsdp", None),
        P("fsdp", None),
        P("fsdp"),
        P("fsdp", None),
        P("fsdp"),
        P("fsdp"),
        P("fsdp"),
        P("fsdp", None),
        P("fsdp"),
        P("fsdp", None),
        P("fsdp"),
    )
    return jax.shard_map(
        on_device, mesh=mesh, in_specs=in_specs, out_specs=out_specs, check_vma=False
    )
```

time: 595 us -> 445 us (0.75)
  the two profiles are of different devices: /device:TPU:13 before, /device:TPU:0 now
where the time goes in v2:
time: 445 us; the launch traced here: 440 us
  Pallas kernels  329 us (74%)
  matrix products  42 us (9%)
  local copies, waits for them, and re-layouts  38.3 us (9%)
  other arithmetic  29 us (7%)
    pallas_call x1, Pallas kernels, forward(): pl.pallas_call(functools.partial(forward_kernel, count), out_shape=[shape...  96 us
    pallas_call x1, Pallas kernels, middle(): pl.pallas_call(functools.partial(middle_kernel, count), out_shape=[shaped...  92.7 us
    pallas_call x1, Pallas kernels, last(): pl.pallas_call(functools.partial(last_kernel, count), out_shape=[shaped(r...  84.7 us
    pallas_call x1, Pallas kernels, fetch(): pl.pallas_call(functools.partial(fetch_kernel, count), out_shape=[shaped(...  55.8 us
    dot_general x3, matrix products, matmul(): return jnp.dot(left, right, preferred_element_type=f32)  16.9 us
    dot_general x2, matrix products, times_transposed(): lax.dot_general(left, right, (((1,), (1,)), ((), ())), preferred_element_...  16.6 us
    unnamed x34, local copies, waits for them, and re-layouts  9.22 us

profile of v2, /device:TPU:0, one launch (start us, length us, event | category | flops | bytes accessed | tf_op | source)
XLA Modules:
  0.0 440.1 jit_solution(15223694588598705762)
XLA Ops:
  0.8 1.3 dynamic_slice.13.length_ref
  2.1 0.7 convert.53
  2.8 0.7 convert.54
  3.4 0.7 convert.55
  4.1 0.7 convert.56
  4.8 0.7 convert.57
  5.4 0.7 convert.58
  6.1 0.7 convert.59
  6.7 0.7 convert.61
  7.4 0.7 convert.60
  8.3 0.9 convert.50
  9.4 0.9 convert.51
  10.6 0.9 convert.52
  11.8 1.6 convert_element_type.119.out_ref
  13.4 0.3 copy.42
  13.6 0.3 copy.41
  13.9 0.3 copy.40
  14.1 1.3 maximum_bitcast_fusion
  15.4 0.3 reshape.270
  15.8 0.8 pad_maximum_fusion.qkv_ref
  16.6 0.8 reshape.276
  17.4 0.3 copy.56
  17.7 1.2 reshape.277.up_ref
  18.8 0.8 convert_element_type.127.down_ref
  19.6 55.8 %fetch.1 = (bf16[8,192,1280]{2,1,0:T(8,128)(2,1)}, bf16[4,8,41,480]{3,2,1,0:T(8,128)(2,1)}, bf16[4,40,1280]{2,1,0:T(8,128)(2,1)}) custom-call(bf16[192,1280]{1,0:T(8,128)(2,1)} %x_ref.5, bf16[8,41,480]{2,1,0:T(8,128)(2,1)} %pad_maximum_fusion.qkv_ref, bf16[40,1280]{1,0:T(8,128)(2,1)} %convert_element_type.119.out_ref), custom_call_target="tpu_custom_call" | custom-call | tf_op jit(solution)/shard_map/fetch/pallas_call | solution.py:491
  75.4 2.8 convert_reduce_fusion
  78.3 3.3 multiply_reduce_fusion
  81.8 1.2 slice.81
  84.5 0.6 pad.37.gain_ref
  85.2 0.7 select_maximum_fusion.1
  85.8 0.9 pad.34
  86.7 3.7 reshape_reshape.3
  90.4 3.2 copy.52
  93.6 1.4 pad.32.clone
  95.0 2.4 copy.46.w_qkv_ref
  97.4 4.6 %fusion.3.normed_ref = bf16[1536,1280]{1,0:T(8,128)(2,1)} fusion(bf16[8,192,1280]{2,1,0:T(8,128)(2,1)} %get-tuple-element.39, f32[1280]{0:T(1024)S(1)} %add.83, f32[1280]{0:T(1024)S(1)} %mul.71, f32[1536]{0:T(1024)S(1)} %rsqrt.13, f32[1536]{0:T(1024)S(1)} %div.21), kind=kLoop, calls=%fused_computation.4 | loop fusion | flops 11796480 | bytes 7886848 | tf_op jit(solution)/shard_map/convert_element_type | solution.py:1402
  102.0 1.6 add_convert_fusion
  103.6 4.6 %add_convert_fusion.1.qkv_ref = bf16[1536,768]{1,0:T(8,128)(2,1)} fusion(bf16[1536,1280]{1,0:T(8,128)(2,1)S(1)} %bitcast.95, bf16[1280,768]{0,1:T(8,128)(2,1)S(1)} %bitcast.89, f32[768]{0:T(1024)S(1)} %pad_bitcast_fusion), kind=kOutput, calls=%fused_computation.11 | convolution fusion | flops 3022258176 | bytes 8260608 | tf_op jit(solution)/shard_map/dot_general | solution.py:31
  108.2 96.0 %forward.1 = (bf16[1536,256]{1,0:T(8,128)(2,1)}, f32[2,1536,1]{2,1,0:T(8,128)}, f32[192,1280]{1,0:T(8,128)}, bf16[8,192,1280]{2,1,0:T(8,128)(2,1)}, bf16[8,192,1...) custom-call(s32[1]{0:T(128)} %dynamic_slice.13.length_ref, ...), custom_call_target="tpu_custom_call" | custom-call | tf_op jit(solution)/shard_map/forward/pallas_call | solution.py:840
  204.2 6.0 %fusion.13 = f32[1536,640]{1,0:T(8,128)S(1)} fusion(bf16[1536,1280]{1,0:T(8,128)(2,1)} %bitcast.109, bf16[1280,640]{1,0:T(8,128)(2,1)} %bitcast.111), kind=kOutput, calls=%fused_computation.66 | convolution fusion | flops 2516582400 | bytes 9502720 | tf_op jit(solution)/shard_map/dot_general | solution.py:31
  210.3 11.9 %convert_reduce_fusion.1 = (f32[640]{0:T(1024)S(1)}, bf16[1536,640]{1,0:T(8,128)(2,1)S(1)}, f32[1536,640]{1,0:T(8,128)S(1)}) fusion(f32[1536,640]{1,0:T(8,128)S(1)} %fusion.13, f32[640]{0:T(1024)S(1)} %add.92, bf16[1536,1280]{1,0:T(8,128)(2,1)S(1)} %bitcast.107, bf16[640,1280]{1,0:T(8,128)(2,1)S(1)} %bitcast.114), kind=kOutput, calls=%fused_computation.13 | convolution fusion | flops 2590309888 | bytes 15406080 | tf_op jit(solution)/shard_map/dot_general | solution.py:39
  222.1 4.5 %convolution_convert_fusion.3 = bf16[1280,640]{1,0:T(8,128)(2,1)} fusion(bf16[1536,1280]{1,0:T(8,128)(2,1)S(1)} %bitcast.110, bf16[1536,640]{1,0:T(8,128)(2,1)S(1)} %get-tuple-element.62), kind=kOutput, calls=%fused_computation.30 | convolution fusion | flops 2517401600 | bytes 7536640 | tf_op jit(solution)/shard_map/dot_general | solution.py:35
  226.6 0.5 multiply_convert_fusion
  227.2 4.1 convolution_convert_fusion.2
  231.5 6.3 %convolution_convert_fusion = bf16[1536,1280]{1,0:T(8,128)(2,1)} fusion(bf16[1536,640]{1,0:T(8,128)(2,1)S(1)} %multiply_convert_fusion, bf16[640,1280]{1,0:T(8,128)(2,1)} %bitcast.113), kind=kOutput, calls=%fused_computation.7 | convolution fusion | flops 2518548480 | bytes 7536640 | tf_op jit(solution)/shard_map/dot_general | solution.py:31
  237.8 4.7 %convolution_convert_fusion.1 = bf16[1536,1280]{1,0:T(8,128)(2,1)} fusion(bf16[1536,640]{1,0:T(8,128)(2,1)S(1)} %copy-done.13, bf16[1280,640]{1,0:T(8,128)(2,1)S(1)} %bitcast.112), kind=kOutput, calls=%fused_computation.8 | convolution fusion | flops 2518548480 | bytes 7536640 | tf_op jit(solution)/shard_map/dot_general | solution.py:39
  242.5 92.7 %middle.1 = (f32[192,1280]{1,0:T(8,128)}, f32[192,1280]{1,0:T(8,128)}, bf16[1536,768]{1,0:T(8,128)(2,1)}, bf16[256,1280]{1,0:T(8,128)(2,1)}, f32[8,1280]{1,0:T(8...) custom-call(s32[1]{0:T(128)} %dynamic_slice.13.length_ref, bf16[8,192,1280]{2,1,0:T(8,128)(2,1)} %bitcast.94, ...), custom_call_target="tpu_custom_call" | custom-call | tf_op jit(solution)/shard_map/middle/pallas_call | solution.py:1047
  335.2 0.8 slice.89
  336.1 0.7 fusion.10.early_ref
  336.9 1.8 slice.113
  338.6 84.7 %last.1 = (f32[192,1280]{1,0:T(8,128)}, bf16[8,40,480]{2,1,0:T(8,128)(2,1)}, f32[40,1280]{1,0:T(8,128)}, f32[8,128]{1,0:T(8,128)}, f32[8,128]{1,0:T(8,128)}) custom-call(bf16[192,1280]{1,0:T(8,128)(2,1)} %x_ref.5, bf16[1536,1280]{1,0:T(8,128)(2,1)} %fusion.3.normed_ref, bf16[1536,768]{1,0:T(8,128)(2,1)} %get-tuple-element.50.grad_qkv_ref, ...), custom_call_target="tpu_custom_call" | custom-call | tf_op jit(solution)/shard_map/last/pallas_call | solution.py:1279
  423.3 1.3 slice_bitcast_fusion.1
  424.6 1.4 slice_bitcast_fusion.2
  426.0 1.3 convert_bitcast_fusion
  427.4 0.8 reshape.297
  428.3 0.8 reshape.296
  429.3 0.8 reshape.295
  430.1 0.9 reshape.299
  431.1 0.8 copy.50
  431.9 1.8 reshape.298
  433.6 2.2 copy.63
  435.9 2.2 copy.64
  438.1 0.7 copy.65
  438.7 0.9 copy.66
  (74 shorter events, 3.4 us)
Async XLA Ops:
  0.7 15.9 %copy-start.2 = (f32[40,5120]{1,0:T(8,128)S(1)}, f32[40,5120]{1,0:T(8,128)}, u32[]{:S(2)}) copy-start(f32[40,5120]{1,0:T(8,128)} %param.30) | copy-start | bytes 2457604
  14.1 4.7 %copy-start.3 = (f32[160,1280]{1,0:T(8,128)S(1)}, f32[160,1280]{1,0:T(8,128)}, u32[]{:S(2)}) copy-start(f32[160,1280]{1,0:T(8,128)} %param.32) | copy-start | bytes 2457604
  75.4 6.4 %copy-start.1 = (bf16[4,8,41,480]{3,2,1,0:T(8,128)(2,1)S(1)}, bf16[4,8,41,480]{3,2,1,0:T(8,128)(2,1)}, u32[]{:S(2)}) copy-start(bf16[4,8,41,480]{3,2,1,0:T(8,128)(2,1)} %get-tuple-element.40) | copy-start | bytes 3778564
  78.2 7.6 %copy-start.5 = (bf16[4,40,1280]{2,1,0:T(8,128)(2,1)S(1)}, bf16[4,40,1280]{2,1,0:T(8,128)(2,1)}, u32[]{:S(2)}) copy-start(bf16[4,40,1280]{2,1,0:T(8,128)(2,1)} %get-tuple-element.41) | copy-start | bytes 1228804
  97.4 4.6 %copy-start = (bf16[8,192,1280]{2,1,0:T(8,128)(2,1)S(1)}, bf16[8,192,1280]{2,1,0:T(8,128)(2,1)}, u32[]{:S(2)}) copy-start(bf16[8,192,1280]{2,1,0:T(8,128)(2,1)} %get-tuple-element.39) | copy-start | bytes 11796484
  204.2 6.1 %copy-start.8 = (bf16[8,192,1280]{2,1,0:T(8,128)(2,1)S(1)}, bf16[8,192,1280]{2,1,0:T(8,128)(2,1)}, u32[]{:S(2)}) copy-start(bf16[8,192,1280]{2,1,0:T(8,128)(2,1)} %get-tuple-element.44) | copy-start | bytes 11796484
  204.2 6.1 %copy-start.11 = (bf16[4,160,1280]{2,1,0:T(8,128)(2,1)S(1)}, bf16[4,160,1280]{2,1,0:T(8,128)(2,1)}, u32[]{:S(2)}) copy-start(bf16[4,160,1280]{2,1,0:T(8,128)(2,1)} %get-tuple-element.45) | copy-start | bytes 4915204
  210.3 11.9 %copy-start.9 = (bf16[8,192,1280]{2,1,0:T(8,128)(2,1)S(1)}, bf16[8,192,1280]{2,1,0:T(8,128)(2,1)}, u32[]{:S(2)}) copy-start(bf16[8,192,1280]{2,1,0:T(8,128)(2,1)} %get-tuple-element.42) | copy-start | bytes 11796484
  222.1 4.5 %copy-start.12 = (bf16[1536,640]{1,0:T(8,128)(2,1)}, bf16[1536,640]{1,0:T(8,128)(2,1)S(1)}, u32[]{:S(2)}) copy-start(bf16[1536,640]{1,0:T(8,128)(2,1)S(1)} %get-tuple-element.62) | copy-start | bytes 5898244
  231.5 6.3 %copy-start.10 = (bf16[4,8,40,640]{3,2,1,0:T(8,128)(2,1)S(1)}, bf16[4,8,40,640]{3,2,1,0:T(8,128)(2,1)}, u32[]{:S(2)}) copy-start(bf16[4,8,40,640]{3,2,1,0:T(8,128)(2,1)} %get-tuple-element.43) | copy-start | bytes 4915204
  231.5 6.3 %copy-start.13 = (bf16[1536,640]{1,0:T(8,128)(2,1)S(1)}, bf16[1536,640]{1,0:T(8,128)(2,1)}, u32[]{:S(2)}) copy-start(bf16[1536,640]{1,0:T(8,128)(2,1)} %copy-done.12) | copy-start | bytes 5898244
  423.3 6.8 %copy-start.6 = (bf16[8,40,640]{2,1,0:T(8,128)(2,1)S(1)}, bf16[8,40,640]{2,1,0:T(8,128)(2,1)}, u32[]{:S(2)}) copy-start(bf16[8,40,640]{2,1,0:T(8,128)(2,1)} %get-tuple-element.59) | copy-start | bytes 1228804
  431.1 7.7 %copy-start.4 = (f32[4,40,1280]{2,1,0:T(8,128)S(1)}, f32[4,40,1280]{2,1,0:T(8,128)}, u32[]{:S(2)}) copy-start(f32[4,40,1280]{2,1,0:T(8,128)} %get-tuple-element.60) | copy-start | bytes 2457604
  431.8 6.2 %copy-start.7 = (f32[40,1280]{1,0:T(8,128)S(1)}, f32[40,1280]{1,0:T(8,128)}, u32[]{:S(2)}) copy-start(f32[40,1280]{1,0:T(8,128)} %get-tuple-element.115) | copy-start | bytes 614404

commit v3 on v2

--- a/solution.py
+++ b/solution.py
@@ -150,28 +150,6 @@
         gather_pass(place, base, out, sems, slot).wait()
 
 
-def gather_kernel(x_ref, out_ref, *sems):
-    me = lax.axis_index("fsdp")
-    place = me % GROUP
-    base = me - place
-    greet([base + flip(place, mask) for mask in FAR + (1,)])
-    gather_start(place, base, x_ref, out_ref, sems)
-    gather_relay(place, base, x_ref, out_ref, sems)
-    gather_finish(place, base, x_ref, out_ref, sems)
-
-
-def plane_gather(block, collective_id):
-    return pl.pallas_call(
-        gather_kernel,
-        out_shape=jax.ShapeDtypeStruct((GROUP,) + block.shape, block.dtype),
-        in_specs=[VSPEC],
-        out_specs=ANYSPEC,
-        scratch_shapes=gather_sems(),
-        compiler_params=params(collective_id),
-        name=f"plane_gather_{collective_id}",
-    )(block)
-
-
 ORDER = (6, 2, 4, 0)
 
 
@@ -378,28 +356,45 @@
     return [DMA((groups,))] * (4 * arrays)
 
 
-def spread_start(me, place, base, pack, out, local, send, recv):
-    slot_of = me // GROUP
-    pltpu.make_async_copy(pack.at[place], out.at[slot_of, place], local).start()
-    for mask in range(1, GROUP):
-        target = flip(place, mask)
-        remote(
-            pack.at[target],
-            out.at[slot_of, place],
-            send.at[mask],
-            recv.at[mask],
-            base + target,
-        ).start()
-
-
-def spread_wait(me, place, base, pack, out, local, send, recv):
-    slot_of = me // GROUP
-    pltpu.make_async_copy(pack.at[place], out.at[slot_of, place], local).wait()
-    for mask in range(1, GROUP):
-        source = flip(place, mask)
-        remote(
-            pack.at[source], out.at[slot_of, source], send.at[mask], recv.at[mask], base + place
-        ).wait()
+class Spread:
+    def __init__(self, place, base, pack, out, scratch, one=False):
+        self.place, self.base, self.pack, self.out, self.one = place, base, pack, out, one
+        self.local, self.send, self.recv = scratch
+
+    def slab(self, target):
+        return self.pack if self.one else self.pack.at[target]
+
+    def copy(self, mask):
+        target = flip(self.place, mask)
+        return remote(
+            self.slab(target),
+            self.out.at[self.place],
+            self.send.at[mask],
+            self.recv.at[mask],
+            self.base + target,
+        )
+
+    def own(self):
+        return pltpu.make_async_copy(
+            self.slab(self.place), self.out.at[self.place], self.local
+        )
+
+    def begin(self):
+        for mask in (6, 2, 4, 7, 3, 5, 1):
+            self.copy(mask).start()
+        self.own().start()
+
+    def finish(self):
+        self.own().wait()
+        for mask in range(1, GROUP):
+            self.copy(mask).wait()
+
+
+SPREAD = 3
+
+
+def spread_sems():
+    return [DMA, DMA((GROUP,)), DMA((GROUP,))]
 
 
 def greet_near(me, place, base, groups, masks):
@@ -422,88 +417,8 @@
     pl.semaphore_wait(barrier, len(masks) + both)
 
 
-def fetch_kernel(count, x_ref, qkv_ref, out_ref, x_all, qkv_all, out_all, *sems):
-    groups = count // GROUP
-    me = lax.axis_index("fsdp")
-    place = me % GROUP
-    base = me - place
-    x_sems, sems = sems[:7], sems[7:]
-    qkv_sems, sems = sems[:3], sems[3:]
-    line_q, sems = sems[:4], sems[4:]
-    out_local, out_send, out_recv = sems
-    greet_all(me, count)
-    spread_start(me, place, base, qkv_ref, qkv_all, *qkv_sems)
-    gather_start(place, base, x_ref, x_all, x_sems)
-    spread_wait(me, place, base, qkv_ref, qkv_all, *qkv_sems)
-    line_send(me, groups, [qkv_all], line_q, 0)
-    per = count // GROUP
-    wanted = me // per
-    slot = me % per
-    for group in range(groups):
-        target = group * GROUP + wanted
-
-        @pl.when(target != me)
-        def _(target=target, group=group):
-            remote(
-                out_ref, out_all.at[slot], out_send.at[group], out_recv.at[slot], target
-            ).start()
-
-        @pl.when(target == me)
-        def _(target=target, group=group):
-            pltpu.make_async_copy(out_ref, out_all.at[slot], out_local).start()
-
-    line_wait(me, groups, [qkv_all], line_q, 0)
-    gather_relay(place, base, x_ref, x_all, x_sems)
-    for step in range(1, groups - 1):
-        line_send(me, groups, [qkv_all], line_q, step)
-        line_wait(me, groups, [qkv_all], line_q, step)
-    gather_finish(place, base, x_ref, x_all, x_sems)
-    line_gather_drain(me, groups, [qkv_all], line_q)
-    for group in range(groups):
-        target = group * GROUP + wanted
-
-        @pl.when(target != me)
-        def _(group=group):
-            remote(
-                out_ref, out_all.at[slot], out_send.at[group], out_recv.at[slot], me
-            ).wait_send()
-
-        @pl.when(target == me)
-        def _():
-            pltpu.make_async_copy(out_ref, out_all.at[slot], out_local).wait()
-
-    for index in range(per):
-        owner = place * per + index
-
-        @pl.when(owner != me)
-        def _(index=index):
-            remote(
-                out_ref, out_all.at[index], out_send.at[0], out_recv.at[index], me
-            ).wait_recv()
-
-
 def shaped(*shape, kind=bf16):
     return jax.ShapeDtypeStruct(shape, kind)
-
-
-def fetch(count, x, qkv, out, collective_id):
-    groups = count // GROUP
-    return pl.pallas_call(
-        functools.partial(fetch_kernel, count),
-        out_shape=[
-            shaped(GROUP, *x.shape),
-            shaped(groups, *qkv.shape),
-            shaped(groups, *out.shape),
-        ],
-        in_specs=[VSPEC] * 3,
-        out_specs=[ANYSPEC] * 3,
-        scratch_shapes=gather_sems()
-        + [DMA, DMA((GROUP,)), DMA((GROUP,))]
-        + line_sems(groups, 1)
-        + [DMA, DMA((groups,)), DMA((groups,))],
-        compiler_params=params(collective_id),
-        name="fetch",
-    )(x, qkv, out)
 
 
 def add_slabs(blocks, store, *terms):
@@ -729,52 +644,147 @@
     return centred * inverse
 
 
-def forward_kernel(
+def head_pick(rows, cols):
+    row = lax.broadcasted_iota(jnp.int32, (rows, cols), 0)
+    col = lax.broadcasted_iota(jnp.int32, (rows, cols), 1)
+    return jnp.where((col // LANES == row // HD) & (col % LANES == row % HD), 1.0, 0.0).astype(bf16)
+
+
+def front_kernel(
     count,
     length_ref,
-    qkv_ref,
+    x_ref,
+    ct_ref,
+    wq_ref,
+    wk_ref,
+    wv_ref,
+    wo_ref,
+    wu_ref,
+    wd_ref,
+    small_ref,
+    normed_out,
+    w_qkv_out,
+    qkv_out,
     w_out_ref,
-    x_ref,
-    vec_ref,
-    ct_ref,
-    up_ref,
-    down_ref,
     mixed_ref,
     log_ref,
     residual_ref,
+    vec_ref,
+    small_all,
     two_all,
     ct_all,
     up_all,
     down_all,
+    x_all,
+    normed_ref,
+    w_qkv_ref,
+    qkv_ref,
     two_rows,
+    pack_qkv,
+    pack_up,
+    down_ref,
+    out_ref,
+    qkv_slabs,
+    out_slabs,
+    wide_w,
+    wide_out,
     *rest,
 ):
     groups = count // GROUP
+    per = groups
     me = lax.axis_index("fsdp")
     place = me % GROUP
     base = me - place
     mine = me // GROUP
+    rows, width = x_ref.shape
+    few = wq_ref.shape[0]
+    many = wd_ref.shape[0]
+    packed = 3 * HEAD_COLS
+    wide = HEADS_HERE * LANES
     scatter, rest = Scatter(place, base, rest[:SCATTER]), rest[SCATTER:]
+    x_sems, rest = rest[:7], rest[7:]
     two_sems, rest = rest[:7], rest[7:]
     ct_sems, rest = rest[:7], rest[7:]
-    up_sems, rest = rest[:3], rest[3:]
-    line_u, (down_local,) = rest[:8], rest[8:]
-    length = length_ref[0]
-    rows = x_ref.shape[0]
-    greet_near(me, place, base, groups, range(1, GROUP))
-    spread_start(me, place, base, up_ref, up_all, *up_sems)
+    qkv_spread, rest = (
+        Spread(place, base, pack_qkv, qkv_slabs.at[mine], rest[:SPREAD]),
+        rest[SPREAD:],
+    )
+    small_spread, rest = (
+        Spread(place, base, small_ref, small_all.at[mine], rest[:SPREAD], True),
+        rest[SPREAD:],
+    )
+    up_spread, rest = (
+        Spread(place, base, pack_up, up_all.at[mine], rest[:SPREAD]),
+        rest[SPREAD:],
+    )
+    line_q, rest = rest[:8], rest[8:]
+    line_u, rest = rest[:8], rest[8:]
+    down_local, out_local, out_send, out_recv, keep_normed, keep_w, keep_qkv = rest
+    length = length_ref[me // GROUP]
+
+    for other in range(GROUP):
+        cols = slice(other * HEAD_COLS, (other + 1) * HEAD_COLS)
+        for index, ref in enumerate((wq_ref, wk_ref, wv_ref)):
+            pack_qkv[other, :, index * HEAD_COLS : (index + 1) * HEAD_COLS] = ref[:, cols].astype(
+                bf16
+            )
+    greet_all(me, count)
+    qkv_spread.begin()
+    small_spread.begin()
+    x_args = (place, base, x_ref, x_all, x_sems)
+    ct_args = (place, base, ct_ref, ct_all, ct_sems)
+    two_args = (place, base, two_rows, two_all, two_sems)
+    gather_start(*x_args)
+    for other in range(GROUP):
+        for group in range(groups):
+            start = (group * GROUP + other) * many
+            pack_up[other, :, group * many : (group + 1) * many] = wu_ref[
+                :, start : start + many
+            ].astype(bf16)
+    down_ref[...] = wd_ref[...].astype(bf16)
+    out_ref[...] = wo_ref[...].astype(bf16)
     own_down = pltpu.make_async_copy(down_ref, down_all.at[mine], down_local)
     own_down.start()
-    gather_start(place, base, ct_ref, ct_all, ct_sems)
+    qkv_spread.finish()
+    small_spread.finish()
+    first_line = [qkv_slabs, small_all]
+    line_send(me, groups, first_line, line_q, 0)
+    up_spread.begin()
+    gather_relay(*x_args)
+    line_wait(me, groups, first_line, line_q, 0)
+    line_send(me, groups, first_line, line_q, 1)
+    gather_finish(*x_args)
+    gather_start(*ct_args)
+    for step in range(1, groups - 1):
+        if step > 1:
+            line_send(me, groups, first_line, line_q, step)
+        line_wait(me, groups, first_line, line_q, step)
+
+    wanted = me // per
+    slot = me % per
+    for group in range(groups):
+        target = group * GROUP + wanted
+
+        @pl.when(target != me)
+        def _(target=target, group=group):
+            remote(
+                out_ref, out_slabs.at[slot], out_send.at[group], out_recv.at[slot], target
+            ).start()
+
+        @pl.when(target == me)
+        def _(target=target, group=group):
+            pltpu.make_async_copy(out_ref, out_slabs.at[slot], out_local).start()
+
+    up_spread.finish()
+    own_down.wait()
     line = [up_all, down_all]
-
-    def first():
-        spread_wait(me, place, base, up_ref, up_all, *up_sems)
-        own_down.wait()
-        line_send(me, groups, line, line_u, 0)
-        gather_relay(place, base, ct_ref, ct_all, ct_sems)
-
-    tasks = [first]
+    line_send(me, groups, line, line_u, 0)
+    gather_relay(*ct_args)
+
+    def ct_end():
+        gather_finish(*ct_args)
+
+    tasks = [ct_end]
     for step in range(groups - 1):
 
         def task(step=step):
@@ -783,6 +793,94 @@
                 line_send(me, groups, line, line_u, step + 1)
 
         tasks.append(task)
+
+    row = lax.broadcasted_iota(jnp.int32, (LANES, width), 0)
+    lane = lax.broadcasted_iota(jnp.int32, (LANES, width), 1)
+    tile = jnp.where((lane % few == row) & (row < few), 1.0, 0.0).astype(bf16)
+    owner = lax.broadcasted_iota(jnp.int32, (1, width), 1) // few
+
+    def lay(group, value):
+        for other in range(GROUP):
+            spot = matmul(small_all[group, other], tile)
+            value = value + jnp.where(owner == group * GROUP + other, spot, 0.0)
+        return value
+
+    vectors = lax.fori_loop(0, groups, lay, jnp.zeros((small_ref.shape[0], width), f32))
+    vec_ref[...] = vectors[:8]
+    gain, offset = vec_ref[0:1, :], vec_ref[1:2, :]
+
+    def first_norm(index, unused):
+        for part in range(rows // 32):
+            span = pl.ds(part * 32, 32)
+            value = x_all[index, span, :].astype(f32)
+            normed_ref[
+                pl.ds(pl.multiple_of(index * rows, rows) + part * 32, 32), :
+            ] = (norm_rows(value) * gain + offset).astype(bf16)
+        return unused
+
+    lax.fori_loop(0, GROUP, first_norm, 0)
+    keep = pltpu.make_async_copy(normed_ref, normed_out, keep_normed)
+    keep.start()
+
+    for source in range(count):
+        wide_w[source * few : (source + 1) * few, :] = qkv_slabs[
+            source // GROUP, source % GROUP
+        ].astype(f32)
+    pick = head_pick(packed, 3 * wide)
+
+    def widen_rows(span):
+        w_qkv_ref[span, :] = matmul(wide_w[span, :].astype(bf16), pick).astype(bf16)
+
+    row_loop(width, 256, widen_rows)
+    keep_two = pltpu.make_async_copy(w_qkv_ref, w_qkv_out, keep_w)
+    keep_two.start()
+    row = lax.broadcasted_iota(jnp.int32, (width, wide), 0) - place * HEAD_COLS
+    col = lax.broadcasted_iota(jnp.int32, (width, wide), 1)
+    spot = jnp.where(
+        (col % LANES < HD) & (row == col // LANES * HD + col % LANES), 1.0, 0.0
+    ).astype(bf16)
+    biases = matmul(vectors.astype(bf16), spot)
+    bias = jnp.concatenate(
+        [biases[2:3], jnp.zeros((1, wide), f32), biases[3:4]], axis=1
+    )
+
+    def project(index, unused):
+        span = pl.ds(pl.multiple_of(index * rows, rows), rows)
+        qkv_ref[span, :] = (matmul(normed_ref[span, :], w_qkv_ref[...]) + bias).astype(bf16)
+        return unused
+
+    lax.fori_loop(0, GROUP, project, 0)
+    keep_three = pltpu.make_async_copy(qkv_ref, qkv_out, keep_qkv)
+    keep_three.start()
+
+    for group in range(groups):
+        target = group * GROUP + wanted
+
+        @pl.when(target != me)
+        def _(group=group):
+            remote(
+                out_ref, out_slabs.at[slot], out_send.at[group], out_recv.at[slot], me
+            ).wait_send()
+
+        @pl.when(target == me)
+        def _():
+            pltpu.make_async_copy(out_ref, out_slabs.at[slot], out_local).wait()
+
+    for index in range(per):
+        sender = place * per + index
+
+        @pl.when(sender != me)
+        def _(index=index):
+            remote(
+                out_ref, out_slabs.at[index], out_send.at[0], out_recv.at[index], me
+            ).wait_recv()
+
+    wide_out[...] = jnp.zeros_like(wide_out)
+    for index in range(per):
+        start = index * few
+        start = start // HD * LANES + start % HD
+        wide_out[start : start + few, :] = out_slabs[index].astype(f32)
+    w_out_ref[...] = wide_out[...].astype(bf16)
 
     def attend_rows(block):
         here = pl.ds(pl.multiple_of(block * rows, rows), rows)
@@ -818,48 +916,74 @@
             tasks.pop(0)()
 
     def normalize(span, value):
-        total = x_ref[span, :].astype(f32) + (value + vec_ref[0:1, :])
+        total = x_ref[span, :].astype(f32) + (value + vec_ref[4:5, :])
         residual_ref[span, :] = total
-        two_rows[span, :] = (norm_rows(total) * vec_ref[1:2, :] + vec_ref[2:3, :]).astype(bf16)
+        two_rows[span, :] = (norm_rows(total) * vec_ref[5:6, :] + vec_ref[6:7, :]).astype(bf16)
 
     scatter.finish(normalize)
-    gather_start(place, base, two_rows, two_all, two_sems)
-    gather_finish(place, base, ct_ref, ct_all, ct_sems)
+    gather_start(*two_args)
     for task in tasks:
         task()
-    gather_relay(place, base, two_rows, two_all, two_sems)
+    gather_relay(*two_args)
     scatter.drain()
-    gather_finish(place, base, two_rows, two_all, two_sems)
+    line_gather_drain(me, groups, first_line, line_q)
     line_gather_drain(me, groups, line, line_u)
-
-
-def forward(count, length, qkv, w_out, x, vec, ct, up, down, collective_id):
+    gather_finish(*two_args)
+    keep.wait()
+    keep_two.wait()
+    keep_three.wait()
+
+
+def front(count, lengths, x, ct, wq, wk, wv, wo, wu, wd, small, collective_id):
     groups = count // GROUP
     rows, width = x.shape
-    clip = qkv.shape[0]
+    clip = GROUP * rows
+    few = wq.shape[0]
+    many = wd.shape[0]
+    packed = 3 * HEAD_COLS
+    wide = HEADS_HERE * LANES
     return pl.pallas_call(
-        functools.partial(forward_kernel, count),
+        functools.partial(front_kernel, count),
         out_shape=[
-            shaped(clip, HEADS_HERE * LANES),
+            shaped(clip, width),
+            shaped(width, 3 * wide),
+            shaped(clip, 3 * wide),
+            shaped(wide, width),
+            shaped(clip, wide),
             shaped(HEADS_HERE, clip, 1, kind=f32),
             shaped(rows, width, kind=f32),
+            shaped(8, width, kind=f32),
+            shaped(groups, GROUP, *small.shape),
             shaped(GROUP, rows, width),
             shaped(GROUP, rows, width),
-            shaped(groups, *up.shape),
-            shaped(groups, *down.shape),
+            shaped(groups, GROUP, few, groups * many),
+            shaped(groups, many, width),
         ],
-        in_specs=[pl.BlockSpec(memory_space=pltpu.SMEM)] + [VSPEC] * 7,
-        out_specs=[VSPEC] * 3 + [ANYSPEC] * 4,
-        scratch_shapes=[VMEM((rows, width), bf16)]
+        in_specs=[pl.BlockSpec(memory_space=pltpu.SMEM)] + [VSPEC] * 9,
+        out_specs=[ANYSPEC] * 3 + [VSPEC] * 6 + [ANYSPEC] * 4,
+        scratch_shapes=[
+            VMEM((GROUP, rows, width), bf16),
+            VMEM((clip, width), bf16),
+            VMEM((width, 3 * wide), bf16),
+            VMEM((clip, 3 * wide), bf16),
+            VMEM((rows, width), bf16),
+            VMEM((GROUP, few, packed), bf16),
+            VMEM((GROUP, few, groups * many), bf16),
+            VMEM((many, width), bf16),
+            VMEM((few, width), bf16),
+            VMEM((groups, GROUP, few, packed), bf16),
+            VMEM((groups, few, width), bf16),
+            VMEM((width, packed), f32),
+            VMEM((wide, width), f32),
+        ]
         + scatter_scratch(rows, width)
-        + gather_sems()
-        + gather_sems()
-        + [DMA, DMA((GROUP,)), DMA((GROUP,))]
-        + line_sems(groups, 2)
-        + [DMA],
+        + gather_sems() * 3
+        + spread_sems() * 3
+        + line_sems(groups, 2) * 2
+        + [DMA, DMA, DMA((groups,)), DMA((groups,)), DMA, DMA, DMA],
         compiler_params=params(collective_id),
-        name="forward",
-    )(length, qkv, w_out, x, vec, ct, up, down)
+        name="front",
+    )(lengths, x, ct, wq, wk, wv, wo, wu, wd, small)
 
 
 def norm_back_rows(value, gain, grad):
@@ -939,7 +1063,7 @@
     folded[...] = jnp.zeros_like(folded)
 
     def through_norm(span, value):
-        moved, by_xhat = norm_back_rows(residual_ref[span, :], vec_ref[0:1, :], value)
+        moved, by_xhat = norm_back_rows(residual_ref[span, :], vec_ref[5:6, :], value)
         cotangent = ct_ref[span, :].astype(f32)
         total = cotangent + moved
         grad_ref[span, :] = total
@@ -1019,7 +1143,7 @@
     grad_out_ref[...] = grad_out.astype(bf16)
 
     def residual_and(span, value):
-        output_ref[span, :] = residual_ref[span, :] + (value + vec_ref[1:2, :])
+        output_ref[span, :] = residual_ref[span, :] + (value + vec_ref[7:8, :])
 
     last.finish(residual_and)
     down_line.finish()
@@ -1307,27 +1431,12 @@
     )(x, normed, grad_qkv, w_qkv, grad, gain, early, out)
 
 
-def layer_norm(values, gain, offset):
-    average = jnp.mean(values, axis=-1, keepdims=True)
-    centred = values - average
-    variance = jnp.mean(centred * centred, axis=-1, keepdims=True)
-    return centred * lax.rsqrt(variance + epsilon) * gain + offset
-
-
 def gelu_exact(values):
     return jax.nn.gelu(values, approximate=False)
 
 
 def column_sums(matrix):
     return jnp.sum(matrix.astype(f32), axis=0)
-
-
-def widen(cols, count):
-    lead = cols.shape[:-1]
-    split = cols.reshape(lead + (count, HD))
-    return jnp.pad(split, [(0, 0)] * (len(lead) + 1) + [(0, LANES - HD)]).reshape(
-        lead + (count * LANES,)
-    )
 
 
 def on_device(
@@ -1357,67 +1466,53 @@
     few = w_query.shape[0]
     many = w_down.shape[0]
     rows = inputs.shape[0]
-    wide = 3 * HEAD_COLS
     ff_here = groups * many
 
-    qkv_pack = (
-        jnp.stack([w_query, w_key, w_value], axis=1)
-        .astype(bf16)
-        .reshape(few, 3, GROUP, HEAD_COLS)
-        .transpose(2, 0, 1, 3)
-        .reshape(GROUP, few, wide)
-    )
-    small = (ln1_gain, ln1_bias, b_query, b_value, b_out, ln2_gain, ln2_bias, b_down, b_up)
-    small = jnp.concatenate(small).astype(bf16)
-    small_pack = jnp.broadcast_to(
-        jnp.pad(small, (0, wide - small.shape[0]))[None, None], (GROUP, 1, wide)
-    )
-    qkv_pack = jnp.concatenate([qkv_pack, small_pack], axis=1)
-    up_pack = (
-        w_up.astype(bf16)
-        .reshape(few, groups, GROUP, many)
-        .transpose(2, 0, 1, 3)
-        .reshape(GROUP, few, ff_here)
-    )
-    x_all, qkv_all, out_all = fetch(count, inputs, qkv_pack, w_out.astype(bf16), 0)
-    w_qkv = widen(qkv_all[:, :, :few].reshape(D, wide), 3 * HEADS_HERE)
-    small_all = qkv_all[:, :, few].reshape(count, wide).astype(f32)
-    whole = [small_all[:, i * few : (i + 1) * few].reshape(D) for i in range(8)]
-    g1, o1, bq, bv, bo, g2, o2, bd = whole
-    b_up_all = small_all[:, 8 * few : 8 * few + many].reshape(groups, GROUP, many)
-    b_up_here = lax.dynamic_index_in_dim(b_up_all, place, 1, keepdims=False).reshape(ff_here)
-    w_out_here = out_all.reshape(HEADS_HERE, HD, D)
-    w_out_here = jnp.pad(w_out_here, ((0, 0), (0, LANES - HD), (0, 0))).reshape(
-        HEADS_HERE * LANES, D
-    )
-
-    def head_slice(vector):
-        return lax.dynamic_slice_in_dim(vector, place * HEAD_COLS, HEAD_COLS)
-
-    b_qkv = jnp.concatenate([head_slice(bq), jnp.zeros((HEAD_COLS,), f32), head_slice(bv)])
-    b_qkv = widen(b_qkv, 3 * HEADS_HERE)
-    length = lax.dynamic_slice_in_dim(lengths, me // GROUP, 1)
-
-    clip = x_all.reshape(GROUP * rows, D).astype(f32)
-    normed = layer_norm(clip, g1, o1).astype(bf16)
-    qkv = (matmul(normed, w_qkv) + b_qkv).astype(bf16)
-    source = inputs.astype(f32)
-    norm_vec = jnp.pad(jnp.stack([bo, g2, o2]), ((0, 5), (0, 0)))
-    attended, log, residual, two_all, ct_all, up_all, down_all = forward(
-        count,
-        length,
+    up_lanes = -(-many // LANES)
+    small = jnp.stack([ln1_gain, ln1_bias, b_query, b_value, b_out, ln2_gain, ln2_bias, b_down])
+    small = jnp.concatenate(
+        [
+            jnp.pad(small, ((0, 0), (0, LANES - few))),
+            jnp.pad(b_up, (0, up_lanes * LANES - many)).reshape(up_lanes, LANES),
+            jnp.zeros((8 - up_lanes, LANES), f32),
+        ]
+    ).astype(bf16)
+    (
+        normed,
+        w_qkv,
         qkv,
         w_out_here,
+        attended,
+        log,
+        residual,
+        vectors,
+        small_all,
+        two_all,
+        ct_all,
+        up_all,
+        down_all,
+    ) = front(
+        count,
+        lengths,
         inputs,
-        norm_vec,
         cotangent,
-        up_pack,
-        w_down.astype(bf16),
-        1,
-    )
+        w_query,
+        w_key,
+        w_value,
+        w_out,
+        w_up,
+        w_down,
+        small,
+        0,
+    )
+    b_up_here = lax.dynamic_index_in_dim(small_all, place, 1, keepdims=False)
+    b_up_here = b_up_here[:, 8 : 8 + up_lanes].astype(f32)
+    b_up_here = b_up_here.reshape(groups, up_lanes * LANES)[:, :many].reshape(ff_here)
     w_up_here = up_all.reshape(D, ff_here)
     w_down_here = down_all.reshape(ff_here, D)
     normed_two = two_all.reshape(GROUP * rows, D)
+    length = lax.dynamic_slice_in_dim(lengths, me // GROUP, 1)
+
     ct = ct_all.reshape(GROUP * rows, D)
     hidden = matmul(normed_two, w_up_here) + b_up_here
     activated = gelu_exact(hidden).astype(bf16)
@@ -1429,7 +1524,6 @@
     two_part = times_transposed(grad_hidden, w_up_here).astype(bf16).reshape(GROUP, rows, D)
     grad_w_up = outer_sum(normed_two, grad_hidden).astype(bf16)
     grad_w_down = outer_sum(activated, ct).astype(bf16)
-    back_vec = jnp.pad(jnp.stack([g2, bd]), ((0, 6), (0, 0)))
     output, grad_residual, grad_qkv, grad_out, sums, up_got, down_total = middle(
         count,
         length,
@@ -1437,7 +1531,7 @@
         out_part,
         residual,
         cotangent,
-        back_vec,
+        vectors,
         w_out_here,
         qkv,
         log,
@@ -1447,7 +1541,6 @@
         2,
     )
     grad_out = grad_out.reshape(HEADS_HERE, LANES, D)[:, :HD].reshape(groups, few, D)
-    up_lanes = -(-many // LANES)
     grad_b_up = jnp.pad(
         column_sums(grad_hidden).reshape(groups, 1, many),
         ((0, 0), (0, 0), (0, up_lanes * LANES - many)),
@@ -1468,7 +1561,7 @@
         grad_qkv,
         w_qkv,
         grad_residual,
-        jnp.pad(g1[None], ((0, 7), (0, 0))),
+        vectors,
         early,
         grad_out,
         3,

time: 445 us -> 387 us (0.87)
  other arithmetic: 29 us -> 6.69 us
  local copies, waits for them, and re-layouts: 38.3 us -> 21.4 us
  Pallas kernels: 329 us -> 313 us
  matrix products: 42 us -> 37.5 us
    pallas_call x2 -> x1, Pallas kernels: 152 us -> 135 us  [front(): pl.pallas_call(functools.partial(front_kernel, count), out_shape=[shaped(...]
    convert_element_type x6 -> x0, other arithmetic: 8.66 us -> none  [the longest x2 6.2 us: on_device(): normed = layer_norm(clip, g1, o1).astype(bf16)]
    reduce_sum x2 -> x0, other arithmetic: 6.17 us -> none  [the longest x1 3.34 us: layer_norm(): variance = jnp.mean(centred * centred, axis=-1, keepdims=True)]
    another operation x13 -> x5, other arithmetic: 9.43 us -> 3.38 us  [the longest x4 2.7 us: on_device(): jnp.stack([ln1_gain, ln1_bias, b_query, b_value, b_out, ln2_gain, ln2_bia...]
    another operation x12 -> x1, local copies, waits for them, and re-layouts: 5.54 us -> 0.03 us  [on_device(): jnp.stack([ln1_gain, ln1_bias, b_query, b_value, b_out, ln2_gain, ln2_bia...]
    reshape x8 -> x1, local copies, waits for them, and re-layouts: 5.21 us -> 0.01 us  [on_device(): jnp.pad(b_up, (0, up_lanes * LANES - many)).reshape(up_lanes, LANES)]
    dot_general x3 -> x2, matrix products: 16.9 us -> 12.4 us  [matmul(): return jnp.dot(left, right, preferred_element_type=f32)]
    unnamed x34 -> x24, local copies, waits for them, and re-layouts: 9.22 us -> 6.04 us
where the time goes in v3:
time: 387 us; the launch traced here: 380 us
  Pallas kernels  313 us (81%)
  matrix products  37.5 us (10%)
  local copies, waits for them, and re-layouts  21.4 us (6%)
  other arithmetic  6.69 us (2%)
    pallas_call x1, Pallas kernels, front(): pl.pallas_call(functools.partial(front_kernel, count), out_shape=[shaped(...  135 us
    pallas_call x1, Pallas kernels, middle(): pl.pallas_call(functools.partial(middle_kernel, count), out_shape=[shaped...  92.5 us
    pallas_call x1, Pallas kernels, last(): pl.pallas_call(functools.partial(last_kernel, count), out_shape=[shaped(r...  84.9 us
    dot_general x2, matrix products, times_transposed(): lax.dot_general(left, right, (((1,), (1,)), ((), ())), preferred_element_...  16.6 us
    dot_general x2, matrix products, matmul(): return jnp.dot(left, right, preferred_element_type=f32)  12.4 us
    dot_general x2, matrix products, outer_sum(): lax.dot_general(left, right, (((0,), (0,)), ((), ())), preferred_element_...  8.56 us

profile of v3, /device:TPU:0, one launch (start us, length us, event | category | flops | bytes accessed | tf_op | source)
XLA Modules:
  0.0 379.9 jit_solution(6169167646793204018)
XLA Ops:
  0.7 1.2 dynamic_slice.7.length_ref
  1.9 0.1 broadcast_in_dim.35
  2.0 0.7 convert.63
  2.7 0.1 pad.27.clone
  2.8 0.7 convert_bitcast_fusion.9
  3.5 0.7 convert_bitcast_fusion.7
  4.2 0.7 convert_bitcast_fusion.5
  4.8 0.7 convert_bitcast_fusion.3
  5.5 0.7 fusion.9.small_ref
  6.2 135.4 %front.1 = (bf16[1536,1280]{1,0:T(8,128)(2,1)}, bf16[1280,768]{1,0:T(8,128)(2,1)}, bf16[1536,768]{1,0:T(8,128)(2,1)}, bf16[256,1280]{1,0:T(8,128)(2,1)}, bf16[15...) custom-call(s32[4]{0:T(128)} %length_ref.1, ...), custom_call_target="tpu_custom_call" | custom-call | tf_op jit(solution)/shard_map/front/pallas_call | solution.py:945
  141.6 0.7 dynamic-slice_bitcast_fusion
  142.4 0.1 reshape.125
  142.5 0.0 copy-start.3
  142.5 0.0 copy-start.6
  142.5 6.0 %fusion.11 = f32[1536,640]{1,0:T(8,128)S(1)} fusion(bf16[1536,1280]{1,0:T(8,128)(2,1)} %bitcast.96, bf16[1280,640]{1,0:T(8,128)(2,1)} %bitcast.98), kind=kOutput, calls=%fused_computation.57 | convolution fusion | flops 2516582400 | bytes 9502720 | tf_op jit(solution)/shard_map/dot_general | solution.py:31
  148.5 0.0 copy-done.3
  148.5 0.0 copy-done.6
  148.6 0.0 copy-start.4
  148.6 11.9 %convert_reduce_fusion = (f32[640]{0:T(1024)S(1)}, bf16[1536,640]{1,0:T(8,128)(2,1)S(1)}, f32[1536,640]{1,0:T(8,128)S(1)}) fusion(f32[1536,640]{1,0:T(8,128)S(1)} %fusion.11, f32[640]{0:T(1024)S(1)} %reshape.125, bf16[1536,1280]{1,0:T(8,128)(2,1)S(1)} %bitcast.94, bf16[640,1280]{1,0:T(8,128)(2,1)S(1)} %bitcast.101), kind=kOutput, calls=%fused_computation.4 | convolution fusion | flops 2590309888 | bytes 15406080 | tf_op jit(solution)/shard_map/dot_general | solution.py:39
  160.4 0.0 copy-start.7
  160.4 0.0 copy-done.4
  160.4 4.5 %convolution_convert_fusion.3 = bf16[1280,640]{1,0:T(8,128)(2,1)} fusion(bf16[1536,1280]{1,0:T(8,128)(2,1)S(1)} %bitcast.97, bf16[1536,640]{1,0:T(8,128)(2,1)S(1)} %get-tuple-element.68), kind=kOutput, calls=%fused_computation.21 | convolution fusion | flops 2517401600 | bytes 7536640 | tf_op jit(solution)/shard_map/dot_general | solution.py:35
  164.9 0.0 copy-done.7
  164.9 0.5 multiply_convert_fusion
  165.5 4.1 %convolution_convert_fusion.2 = bf16[640,1280]{1,0:T(8,128)(2,1)} fusion(bf16[1536,640]{1,0:T(8,128)(2,1)S(1)} %multiply_convert_fusion, bf16[1536,1280]{1,0:T(8,128)(2,1)S(1)} %bitcast.95), kind=kOutput, calls=%fused_computation.20 | convolution fusion | flops 2517401600 | bytes 7536640 | tf_op jit(solution)/shard_map/dot_general | solution.py:35
  169.6 0.1 reshape.120
  169.7 0.1 bitcast_select_fusion
  169.8 0.0 copy-start.5
  169.8 0.0 copy-start.8
  169.8 6.3 %convolution_convert_fusion = bf16[1536,1280]{1,0:T(8,128)(2,1)} fusion(bf16[1536,640]{1,0:T(8,128)(2,1)S(1)} %multiply_convert_fusion, bf16[640,1280]{1,0:T(8,128)(2,1)} %bitcast.100), kind=kOutput, calls=%fused_computation | convolution fusion | flops 2518548480 | bytes 7536640 | tf_op jit(solution)/shard_map/dot_general | solution.py:31
  176.1 0.0 copy-done.5
  176.1 0.0 copy-done.8
  176.1 4.7 %convolution_convert_fusion.1 = bf16[1536,1280]{1,0:T(8,128)(2,1)} fusion(bf16[1536,640]{1,0:T(8,128)(2,1)S(1)} %copy-done.8, bf16[1280,640]{1,0:T(8,128)(2,1)S(1)} %bitcast.99), kind=kOutput, calls=%fused_computation.1 | convolution fusion | flops 2518548480 | bytes 7536640 | tf_op jit(solution)/shard_map/dot_general | solution.py:39
  180.9 92.5 %middle.1 = (f32[192,1280]{1,0:T(8,128)}, f32[192,1280]{1,0:T(8,128)}, bf16[1536,768]{1,0:T(8,128)(2,1)}, bf16[256,1280]{1,0:T(8,128)(2,1)}, f32[8,1280]{1,0:T(8...) custom-call(s32[1]{0:T(128)} %dynamic_slice.7.length_ref, bf16[8,192,1280]{2,1,0:T(8,128)(2,1)} %bitcast.85, ...), custom_call_target="tpu_custom_call" | custom-call | tf_op jit(solution)/shard_map/middle/pallas_call | solution.py:1171
  273.3 0.8 slice.54
  274.1 0.1 reshape.119
  274.3 0.7 fusion.6.early_ref
  275.0 1.8 slice.71
  276.8 84.9 %last.1 = (f32[192,1280]{1,0:T(8,128)}, bf16[8,40,480]{2,1,0:T(8,128)(2,1)}, f32[40,1280]{1,0:T(8,128)}, f32[8,128]{1,0:T(8,128)}, f32[8,128]{1,0:T(8,128)}) custom-call(bf16[192,1280]{1,0:T(8,128)(2,1)} %x_ref.3, bf16[1536,1280]{1,0:T(8,128)(2,1)} %get-tuple-element.54.normed_ref, bf16[1536,768]{1,0:T(8,128)(2,1)} %get-tuple-element.55.grad_qkv_ref, ...), custom_call_target="tpu_custom_call" | custom-call | tf_op jit(solution)/shard_map/last/pallas_call | solution.py:1403
  361.7 0.0 copy-start.1
  361.7 1.3 slice_bitcast_fusion.1
  363.0 1.4 slice_bitcast_fusion.2
  364.4 1.3 slice_bitcast_fusion.6
  365.7 1.3 convert_bitcast_fusion
  367.0 0.1 copy.39
  367.1 0.8 reshape.128
  367.9 0.1 copy.38
  368.0 0.8 reshape.127
  368.9 0.1 copy.37
  369.0 0.8 reshape.126
  369.8 0.0 copy-done.1
  369.8 0.9 reshape.130
  370.8 0.0 copy-start
  370.8 0.8 copy.40
  371.6 0.0 copy-start.2
  371.6 1.8 reshape.129
  373.4 2.2 copy.50
  375.6 2.2 copy.51
  377.8 0.0 copy-done.2
  377.8 0.7 copy.52
  378.5 0.0 copy-done
  378.5 0.9 copy.53
  (12 shorter events, 0.2 us)
Async XLA Ops:
  142.5 6.1 %copy-start.3 = (bf16[8,192,1280]{2,1,0:T(8,128)(2,1)S(1)}, bf16[8,192,1280]{2,1,0:T(8,128)(2,1)}, u32[]{:S(2)}) copy-start(bf16[8,192,1280]{2,1,0:T(8,128)(2,1)} %get-tuple-element.45) | copy-start | bytes 11796484
  142.5 6.1 %copy-start.6 = (bf16[4,160,1280]{2,1,0:T(8,128)(2,1)S(1)}, bf16[4,160,1280]{2,1,0:T(8,128)(2,1)}, u32[]{:S(2)}) copy-start(bf16[4,160,1280]{2,1,0:T(8,128)(2,1)} %get-tuple-element.46) | copy-start | bytes 4915204
  148.6 11.9 %copy-start.4 = (bf16[8,192,1280]{2,1,0:T(8,128)(2,1)S(1)}, bf16[8,192,1280]{2,1,0:T(8,128)(2,1)}, u32[]{:S(2)}) copy-start(bf16[8,192,1280]{2,1,0:T(8,128)(2,1)} %get-tuple-element.42) | copy-start | bytes 11796484
  160.4 4.5 %copy-start.7 = (bf16[1536,640]{1,0:T(8,128)(2,1)}, bf16[1536,640]{1,0:T(8,128)(2,1)S(1)}, u32[]{:S(2)}) copy-start(bf16[1536,640]{1,0:T(8,128)(2,1)S(1)} %get-tuple-element.68) | copy-start | bytes 5898244
  169.8 6.4 %copy-start.5 = (bf16[4,8,40,640]{3,2,1,0:T(8,128)(2,1)S(1)}, bf16[4,8,40,640]{3,2,1,0:T(8,128)(2,1)}, u32[]{:S(2)}) copy-start(bf16[4,8,40,640]{3,2,1,0:T(8,128)(2,1)} %get-tuple-element.43) | copy-start | bytes 4915204
  169.8 6.4 %copy-start.8 = (bf16[1536,640]{1,0:T(8,128)(2,1)S(1)}, bf16[1536,640]{1,0:T(8,128)(2,1)}, u32[]{:S(2)}) copy-start(bf16[1536,640]{1,0:T(8,128)(2,1)} %copy-done.7) | copy-start | bytes 5898244
  361.7 8.1 %copy-start.1 = (bf16[8,40,640]{2,1,0:T(8,128)(2,1)S(1)}, bf16[8,40,640]{2,1,0:T(8,128)(2,1)}, u32[]{:S(2)}) copy-start(bf16[8,40,640]{2,1,0:T(8,128)(2,1)} %get-tuple-element.65) | copy-start | bytes 1228804
  370.8 7.7 %copy-start = (f32[4,40,1280]{2,1,0:T(8,128)S(1)}, f32[4,40,1280]{2,1,0:T(8,128)}, u32[]{:S(2)}) copy-start(f32[4,40,1280]{2,1,0:T(8,128)} %get-tuple-element.66) | copy-start | bytes 2457604
  371.6 6.2 %copy-start.2 = (f32[40,1280]{1,0:T(8,128)S(1)}, f32[40,1280]{1,0:T(8,128)}, u32[]{:S(2)}) copy-start(f32[40,1280]{1,0:T(8,128)} %get-tuple-element.115) | copy-start | bytes 614404

commit v4 on v3

--- a/solution.py
+++ b/solution.py
@@ -44,6 +44,14 @@
         if mask & bit:
             place = place + bit - 2 * bit * (place // bit % 2)
     return place
+
+
+def head_of(place, index):
+    return place // 2 + H // 4 * (HEADS_HERE * (place % 2) + index)
+
+
+def place_of(head):
+    return 2 * (head % (H // 4)) + head // (H // 2)
 
 
 def remote(src, dst, send_sem, recv_sem, target):
@@ -190,6 +198,13 @@
     def block(self, i, other):
         return flip(flip(self.place, ORDER[i]), 1 if other else 0)
 
+    def block_at(self, step):
+        i = step // 2
+        place = self.place
+        place = place + (1 - i // 2) * (2 - 4 * (place // 2 % 2))
+        place = place + (1 - i % 2) * (4 - 8 * (place // 4 % 2))
+        return place + (1 - step % 2) * (1 - 2 * (place % 2))
+
     def keep(self, i):
         return self.parts.at[i, 1] if self.ready is None else self.parts.at[i]
 
@@ -492,23 +507,27 @@
             def _(low=low):
                 self.down(low, self.own).start()
 
+    def pass_up(self, target):
+        self.up(target, self.own).wait_recv()
+        self.add(target)
+        self.up(target, self.came).start()
+
+    def pass_down(self, target):
+        self.down(target, self.own).wait_recv()
+        self.add(target)
+        self.down(target, self.came).start()
+
     def tasks(self):
-        def step(target):
-            low = self.groups - 1 - target
-
-            @pl.when((self.mine < target) & (self.mine > 0))
-            def _():
-                self.up(target, self.own).wait_recv()
-                self.add(target)
-                self.up(target, self.came).start()
-
-            @pl.when((self.mine > low) & (self.mine < self.groups - 1))
-            def _():
-                self.down(low, self.own).wait_recv()
-                self.add(low)
-                self.down(low, self.came).start()
-
-        return [functools.partial(step, target) for target in range(self.groups - 1, 0, -1)]
+        top = self.groups - 1
+
+        def step(hops):
+            for order in range(top):
+                passed = hops - order
+                if 1 <= passed < top - order:
+                    pl.when(self.mine == passed)(functools.partial(self.pass_up, top - order))
+                    pl.when(self.mine == top - passed)(functools.partial(self.pass_down, order))
+
+        return [functools.partial(step, hops) for hops in range(1, top)]
 
     def finish(self):
         def store(index, value):
@@ -585,14 +604,17 @@
 
 
 class Mail:
-    def __init__(self, me, count, given, got, local, send, recv):
-        self.me, self.count, self.given, self.got = me, count, given, got
+    def __init__(self, me, count, given, got, local, send, recv, one=False):
+        self.me, self.count, self.given, self.got, self.one = me, count, given, got, one
         self.local, self.send, self.recv = local, send, recv
+
+    def slab(self, target):
+        return self.given if self.one else self.given.at[target]
 
     def copy(self, step):
         target = (self.me + step) % self.count
         return remote(
-            self.given.at[target],
+            self.slab(target),
             self.got.at[self.me],
             self.send.at[step],
             self.recv.at[step],
@@ -600,7 +622,7 @@
         )
 
     def own(self):
-        return pltpu.make_async_copy(self.given.at[self.me], self.got.at[self.me], self.local)
+        return pltpu.make_async_copy(self.slab(self.me), self.got.at[self.me], self.local)
 
     def begin(self):
         self.own().start()
@@ -611,7 +633,7 @@
 
         lax.fori_loop(1, self.count, run, 0)
 
-    def finish(self, total):
+    def wait(self):
         self.own().wait()
 
         def run(step, unused):
@@ -619,6 +641,9 @@
             return unused
 
         lax.fori_loop(1, self.count, run, 0)
+
+    def finish(self, total):
+        self.wait()
 
         def add(index, value):
             return value + self.got[index]
@@ -642,6 +667,98 @@
     centred = value - average
     inverse = lax.rsqrt(jnp.mean(centred * centred, axis=-1, keepdims=True) + epsilon)
     return centred * inverse
+
+
+class DirectOut:
+    def __init__(self, me, count, shard, slabs, local, send, recv):
+        self.me, self.groups, self.shard, self.slabs = me, count // GROUP, shard, slabs
+        self.local, self.send, self.recv = local, send, recv
+        self.each = self.groups // HEADS_HERE
+        head = me // self.each
+        self.wanted = place_of(head)
+        self.slot = head // (H // 4) % HEADS_HERE * self.each + me % self.each
+
+    def owner(self, place, index):
+        return head_of(place, index // self.each) * self.each + index % self.each
+
+    def copy(self, group):
+        return remote(
+            self.shard,
+            self.slabs.at[self.slot],
+            self.send.at[group],
+            self.recv.at[self.slot],
+            group * GROUP + self.wanted,
+        )
+
+    def own(self):
+        return pltpu.make_async_copy(self.shard, self.slabs.at[self.slot], self.local)
+
+    def begin(self):
+        for group in range(self.groups):
+            mine = group * GROUP + self.wanted == self.me
+            pl.when(jnp.logical_not(mine))(self.copy(group).start)
+            pl.when(mine)(self.own().start)
+
+    def finish(self, place):
+        for group in range(self.groups):
+            mine = group * GROUP + self.wanted == self.me
+            pl.when(jnp.logical_not(mine))(self.copy(group).wait_send)
+            pl.when(mine)(self.own().wait)
+        for index in range(self.groups):
+            copy = remote(
+                self.shard, self.slabs.at[index], self.send.at[0], self.recv.at[index], self.me
+            )
+            pl.when(self.owner(place, index) != self.me)(copy.wait_recv)
+
+
+class DirectBack:
+    def __init__(self, me, count, given, got, local, send, recv):
+        self.me, self.groups, self.given, self.got = me, count // GROUP, given, got
+        self.local, self.send, self.recv = local, send, recv
+        self.each = self.groups // HEADS_HERE
+        self.mine = me // GROUP
+
+    def owner(self, index):
+        head = head_of(self.me % GROUP, index // self.each)
+        return head * self.each + index % self.each
+
+    def copy(self, index):
+        return remote(
+            self.given.at[index],
+            self.got.at[self.mine],
+            self.send.at[index],
+            self.recv.at[self.mine],
+            self.owner(index),
+        )
+
+    def own(self, index):
+        return pltpu.make_async_copy(self.given.at[index], self.got.at[self.mine], self.local)
+
+    def begin(self):
+        for index in range(self.groups):
+            mine = self.owner(index) == self.me
+            pl.when(jnp.logical_not(mine))(self.copy(index).start)
+            pl.when(mine)(self.own(index).start)
+
+    def finish(self, total_ref):
+        for index in range(self.groups):
+            mine = self.owner(index) == self.me
+            pl.when(jnp.logical_not(mine))(self.copy(index).wait_send)
+            pl.when(mine)(self.own(index).wait)
+        sender = place_of(self.me // self.each)
+        for group in range(self.groups):
+            copy = remote(
+                self.given.at[0], self.got.at[group], self.send.at[0], self.recv.at[group], self.me
+            )
+            pl.when(group * GROUP + sender != self.me)(copy.wait_recv)
+        total = self.got[0].astype(f32)
+        for group in range(1, self.groups):
+            total = total + self.got[group].astype(f32)
+        total_ref[...] = total
+
+
+def on_lines(count):
+    return count == 2 * H
 
 
 def head_pick(rows, cols):
@@ -686,6 +803,8 @@
     out_ref,
     qkv_slabs,
     out_slabs,
+    out_sib,
+    small_flat,
     wide_w,
     wide_out,
     *rest,
@@ -709,28 +828,28 @@
         Spread(place, base, pack_qkv, qkv_slabs.at[mine], rest[:SPREAD]),
         rest[SPREAD:],
     )
-    small_spread, rest = (
-        Spread(place, base, small_ref, small_all.at[mine], rest[:SPREAD], True),
-        rest[SPREAD:],
-    )
     up_spread, rest = (
         Spread(place, base, pack_up, up_all.at[mine], rest[:SPREAD]),
         rest[SPREAD:],
     )
-    line_q, rest = rest[:8], rest[8:]
+    line_q, rest = rest[:4], rest[4:]
     line_u, rest = rest[:8], rest[8:]
-    down_local, out_local, out_send, out_recv, keep_normed, keep_w, keep_qkv = rest
+    line_o, rest = rest[:4], rest[4:]
+    small_mail, rest = Mail(me, count, small_ref, small_flat, *rest[:3], one=True), rest[3:]
+    down_local, out_local, out_send, out_recv, keep_normed, keep_w, keep_qkv, keep_small = rest
     length = length_ref[me // GROUP]
+    core = place % 2
+    fast = on_lines(count)
 
     for other in range(GROUP):
-        cols = slice(other * HEAD_COLS, (other + 1) * HEAD_COLS)
-        for index, ref in enumerate((wq_ref, wk_ref, wv_ref)):
-            pack_qkv[other, :, index * HEAD_COLS : (index + 1) * HEAD_COLS] = ref[:, cols].astype(
-                bf16
-            )
+        for head in range(HEADS_HERE):
+            cols = slice(head_of(other, head) * HD, (head_of(other, head) + 1) * HD)
+            for index, ref in enumerate((wq_ref, wk_ref, wv_ref)):
+                start = index * HEAD_COLS + head * HD
+                pack_qkv[other, :, start : start + HD] = ref[:, cols].astype(bf16)
     greet_all(me, count)
     qkv_spread.begin()
-    small_spread.begin()
+    small_mail.begin()
     x_args = (place, base, x_ref, x_all, x_sems)
     ct_args = (place, base, ct_ref, ct_all, ct_sems)
     two_args = (place, base, two_rows, two_all, two_sems)
@@ -746,66 +865,26 @@
     own_down = pltpu.make_async_copy(down_ref, down_all.at[mine], down_local)
     own_down.start()
     qkv_spread.finish()
-    small_spread.finish()
-    first_line = [qkv_slabs, small_all]
-    line_send(me, groups, first_line, line_q, 0)
-    up_spread.begin()
-    gather_relay(*x_args)
-    line_wait(me, groups, first_line, line_q, 0)
-    line_send(me, groups, first_line, line_q, 1)
-    gather_finish(*x_args)
-    gather_start(*ct_args)
-    for step in range(1, groups - 1):
-        if step > 1:
-            line_send(me, groups, first_line, line_q, step)
-        line_wait(me, groups, first_line, line_q, step)
-
-    wanted = me // per
-    slot = me % per
-    for group in range(groups):
-        target = group * GROUP + wanted
-
-        @pl.when(target != me)
-        def _(target=target, group=group):
-            remote(
-                out_ref, out_slabs.at[slot], out_send.at[group], out_recv.at[slot], target
-            ).start()
-
-        @pl.when(target == me)
-        def _(target=target, group=group):
-            pltpu.make_async_copy(out_ref, out_slabs.at[slot], out_local).start()
-
-    up_spread.finish()
-    own_down.wait()
-    line = [up_all, down_all]
-    line_send(me, groups, line, line_u, 0)
-    gather_relay(*ct_args)
-
-    def ct_end():
-        gather_finish(*ct_args)
-
-    tasks = [ct_end]
-    for step in range(groups - 1):
-
-        def task(step=step):
-            line_wait(me, groups, line, line_u, step)
-            if step < groups - 2:
-                line_send(me, groups, line, line_u, step + 1)
-
-        tasks.append(task)
-
+    line_send(me, groups, [qkv_slabs], line_q, 0)
+    small_mail.wait()
+    keep_four = pltpu.make_async_copy(small_flat, small_all, keep_small)
+    keep_four.start()
+
+    kinds = small_ref.shape[0]
     row = lax.broadcasted_iota(jnp.int32, (LANES, width), 0)
     lane = lax.broadcasted_iota(jnp.int32, (LANES, width), 1)
     tile = jnp.where((lane % few == row) & (row < few), 1.0, 0.0).astype(bf16)
     owner = lax.broadcasted_iota(jnp.int32, (1, width), 1) // few
 
     def lay(group, value):
+        slabs = small_flat[pl.ds(pl.multiple_of(group * GROUP, GROUP), GROUP)]
+        spots = matmul(slabs.reshape(GROUP * kinds, LANES), tile)
         for other in range(GROUP):
-            spot = matmul(small_all[group, other], tile)
+            spot = spots[other * kinds : (other + 1) * kinds]
             value = value + jnp.where(owner == group * GROUP + other, spot, 0.0)
         return value
 
-    vectors = lax.fori_loop(0, groups, lay, jnp.zeros((small_ref.shape[0], width), f32))
+    vectors = lax.fori_loop(0, groups, lay, jnp.zeros((kinds, width), f32))
     vec_ref[...] = vectors[:8]
     gain, offset = vec_ref[0:1, :], vec_ref[1:2, :]
 
@@ -818,9 +897,32 @@
             ] = (norm_rows(value) * gain + offset).astype(bf16)
         return unused
 
-    lax.fori_loop(0, GROUP, first_norm, 0)
+    gather_relay(*x_args)
+    line_wait(me, groups, [qkv_slabs], line_q, 0)
+    line_send(me, groups, [qkv_slabs], line_q, 1)
+    gather_finish(*x_args)
+    up_spread.begin()
+    gather_start(*ct_args)
+    lax.fori_loop(0, GROUP // 2, first_norm, 0)
+    line_wait(me, groups, [qkv_slabs], line_q, 1)
+    for step in range(2, groups - 1):
+        line_send(me, groups, [qkv_slabs], line_q, step)
+        if step < groups - 2:
+            line_wait(me, groups, [qkv_slabs], line_q, step)
+    lax.fori_loop(GROUP // 2, GROUP, first_norm, 0)
     keep = pltpu.make_async_copy(normed_ref, normed_out, keep_normed)
     keep.start()
+    line_wait(me, groups, [qkv_slabs], line_q, groups - 2)
+
+    line = [up_all, down_all]
+    if fast:
+        keep_out = pltpu.make_async_copy(out_ref, out_slabs.at[mine], out_local)
+        keep_out.start()
+        keep_out.wait()
+        line_send(me, groups, [out_slabs], line_o, 0)
+    else:
+        direct = DirectOut(me, count, out_ref, out_slabs, out_local, out_send, out_recv)
+        direct.begin()
 
     for source in range(count):
         wide_w[source * few : (source + 1) * few, :] = qkv_slabs[
@@ -832,55 +934,77 @@
         w_qkv_ref[span, :] = matmul(wide_w[span, :].astype(bf16), pick).astype(bf16)
 
     row_loop(width, 256, widen_rows)
+    if fast:
+        line_wait(me, groups, [out_slabs], line_o, 0)
+        line_send(me, groups, [out_slabs], line_o, 1)
     keep_two = pltpu.make_async_copy(w_qkv_ref, w_qkv_out, keep_w)
     keep_two.start()
-    row = lax.broadcasted_iota(jnp.int32, (width, wide), 0) - place * HEAD_COLS
+    row = lax.broadcasted_iota(jnp.int32, (width, wide), 0)
     col = lax.broadcasted_iota(jnp.int32, (width, wide), 1)
     spot = jnp.where(
-        (col % LANES < HD) & (row == col // LANES * HD + col % LANES), 1.0, 0.0
+        (col % LANES < HD) & (row == head_of(place, col // LANES) * HD + col % LANES), 1.0, 0.0
     ).astype(bf16)
     biases = matmul(vectors.astype(bf16), spot)
-    bias = jnp.concatenate(
-        [biases[2:3], jnp.zeros((1, wide), f32), biases[3:4]], axis=1
-    )
+    bias = jnp.concatenate([biases[2:3], jnp.zeros((1, wide), f32), biases[3:4]], axis=1)
 
     def project(index, unused):
         span = pl.ds(pl.multiple_of(index * rows, rows), rows)
         qkv_ref[span, :] = (matmul(normed_ref[span, :], w_qkv_ref[...]) + bias).astype(bf16)
         return unused
 
-    lax.fori_loop(0, GROUP, project, 0)
+    gather_relay(*ct_args)
+    up_spread.finish()
+    own_down.wait()
+    lax.fori_loop(0, GROUP // 2, project, 0)
+    if fast:
+        line_wait(me, groups, [out_slabs], line_o, 1)
+        line_send(me, groups, [out_slabs], line_o, 2)
+    line_send(me, groups, line[:1], line_u[:4], 0)
+    line_send(me, groups, line[1:], line_u[4:], 0)
+    lax.fori_loop(GROUP // 2, GROUP, project, 0)
     keep_three = pltpu.make_async_copy(qkv_ref, qkv_out, keep_qkv)
     keep_three.start()
 
-    for group in range(groups):
-        target = group * GROUP + wanted
-
-        @pl.when(target != me)
-        def _(group=group):
-            remote(
-                out_ref, out_slabs.at[slot], out_send.at[group], out_recv.at[slot], me
-            ).wait_send()
-
-        @pl.when(target == me)
-        def _():
-            pltpu.make_async_copy(out_ref, out_slabs.at[slot], out_local).wait()
-
-    for index in range(per):
-        sender = place * per + index
-
-        @pl.when(sender != me)
-        def _(index=index):
-            remote(
-                out_ref, out_slabs.at[index], out_send.at[0], out_recv.at[index], me
-            ).wait_recv()
-
     wide_out[...] = jnp.zeros_like(wide_out)
-    for index in range(per):
-        start = index * few
-        start = start // HD * LANES + start % HD
-        wide_out[start : start + few, :] = out_slabs[index].astype(f32)
+    if fast:
+        line_wait(me, groups, [out_slabs], line_o, 2)
+        crossing = []
+        for head in range(HEADS_HERE):
+            copy = remote(
+                out_slabs.at[HEADS_HERE * (1 - core) + head],
+                out_sib.at[head],
+                out_send.at[head],
+                out_recv.at[head],
+                base + flip(place, 1),
+            )
+            copy.start()
+            crossing.append(copy)
+        for head in range(HEADS_HERE):
+            here = pl.multiple_of(head * LANES + few * core, 8)
+            wide_out[pl.ds(here, few), :] = out_slabs[HEADS_HERE * core + head].astype(f32)
+        for head, copy in enumerate(crossing):
+            copy.wait()
+            here = pl.multiple_of(head * LANES + few * (1 - core), 8)
+            wide_out[pl.ds(here, few), :] = out_sib[head].astype(f32)
+    else:
+        direct.finish(place)
+        for index in range(per):
+            start = index * few
+            start = start // HD * LANES + start % HD
+            wide_out[start : start + few, :] = out_slabs[index].astype(f32)
     w_out_ref[...] = wide_out[...].astype(bf16)
+
+    tasks = []
+    for step in range(groups - 1):
+        for which in range(2):
+
+            def task(step=step, which=which):
+                sems = line_u[4 * which : 4 * which + 4]
+                line_wait(me, groups, [line[which]], sems, step)
+                if step < groups - 2:
+                    line_send(me, groups, [line[which]], sems, step + 1)
+
+            tasks.append(task)
 
     def attend_rows(block):
         here = pl.ds(pl.multiple_of(block * rows, rows), rows)
@@ -898,22 +1022,24 @@
             log_ref[head, here, :] = largest + jnp.log(total)
         return matmul(mixed_ref[here, :], w_out_ref[...]).astype(bf16)
 
-    for i in range(4):
-
-        def pair(turn, unused, i=i):
-            block = jnp.where(turn == 0, scatter.block(i, True), scatter.block(i, False))
-            scatter.parts[i, turn] = attend_rows(block)
-
-            @pl.when(turn == 0)
-            def _():
-                scatter.sibling(i).start()
-
-            return unused
-
-        lax.fori_loop(0, 2, pair, 0)
-        scatter.after(i)
-        if tasks:
-            tasks.pop(0)()
+    def attend_step(step, unused):
+        i, turn = step // 2, step % 2
+        scatter.parts[i, turn] = attend_rows(scatter.block_at(step))
+        pl.when(turn == 0)(lambda: scatter.sibling(i).start())
+        for k in range(8):
+
+            @pl.when(step == k)
+            def _(k=k):
+                if k % 2:
+                    scatter.after(k // 2)
+                if k == 4:
+                    gather_finish(*ct_args)
+                if k == 6:
+                    tasks[0]()
+
+        return unused
+
+    lax.fori_loop(0, 8, attend_step, 0)
 
     def normalize(span, value):
         total = x_ref[span, :].astype(f32) + (value + vec_ref[4:5, :])
@@ -922,16 +1048,21 @@
 
     scatter.finish(normalize)
     gather_start(*two_args)
-    for task in tasks:
+    tasks[1]()
+    gather_relay(*two_args)
+    tasks[2]()
+    gather_finish(*two_args)
+    for task in tasks[3:]:
         task()
-    gather_relay(*two_args)
     scatter.drain()
-    line_gather_drain(me, groups, first_line, line_q)
+    line_gather_drain(me, groups, [qkv_slabs], line_q)
     line_gather_drain(me, groups, line, line_u)
-    gather_finish(*two_args)
+    if fast:
+        line_gather_drain(me, groups, [out_slabs], line_o)
     keep.wait()
     keep_two.wait()
     keep_three.wait()
+    keep_four.wait()
 
 
 def front(count, lengths, x, ct, wq, wk, wv, wo, wu, wd, small, collective_id):
@@ -953,7 +1084,7 @@
             shaped(HEADS_HERE, clip, 1, kind=f32),
             shaped(rows, width, kind=f32),
             shaped(8, width, kind=f32),
-            shaped(groups, GROUP, *small.shape),
+            shaped(count, *small.shape),
             shaped(GROUP, rows, width),
             shaped(GROUP, rows, width),
             shaped(groups, GROUP, few, groups * many),
@@ -973,14 +1104,19 @@
             VMEM((few, width), bf16),
             VMEM((groups, GROUP, few, packed), bf16),
             VMEM((groups, few, width), bf16),
+            VMEM((HEADS_HERE, few, width), bf16),
+            VMEM((count, *small.shape), bf16),
             VMEM((width, packed), f32),
             VMEM((wide, width), f32),
         ]
         + scatter_scratch(rows, width)
         + gather_sems() * 3
-        + spread_sems() * 3
-        + line_sems(groups, 2) * 2
-        + [DMA, DMA, DMA((groups,)), DMA((groups,)), DMA, DMA, DMA],
+        + spread_sems() * 2
+        + line_sems(groups, 1)
+        + line_sems(groups, 2)
+        + line_sems(groups, 1)
+        + [DMA, DMA((count,)), DMA((count,))]
+        + [DMA, DMA, DMA((groups,)), DMA((groups,)), DMA, DMA, DMA, DMA],
         compiler_params=params(collective_id),
         name="front",
     )(lengths, x, ct, wq, wk, wv, wo, wu, wd, small)
@@ -1057,7 +1193,10 @@
     tasks = up_line.tasks() + down_line.tasks()
     for i in range(3):
         two.after(i)
-    tasks.pop(0)()
+    early = len(tasks) // 4
+    for task in tasks[:early]:
+        task()
+    tasks = tasks[early:]
     key_sum[...] = jnp.zeros_like(key_sum)
     value_sum[...] = jnp.zeros_like(value_sum)
     folded[...] = jnp.zeros_like(folded)
@@ -1095,38 +1234,58 @@
             key_sum[:, cols] += outer_sum(grad_scores, query)
             value_sum[:, cols] += outer_sum(weights.astype(bf16), grad)
 
-    def attend_pair(first, second):
-        def run(turn, unused):
-            attend_back(jnp.where(turn == 0, flip(place, first), flip(place, second)))
-            return unused
-
-        lax.fori_loop(0, 2, run, 0)
-
     args = (place, base, branch_rows, branch_all, sems)
-    pltpu.make_async_copy(branch_rows, branch_all.at[place], sems[0]).wait()
-    gather_own(*args).wait_recv()
-    attend_pair(0, 1)
-    gather_relay(*args)
-    for slot in (2, 3):
-        gather_piece(*args, slot).wait_recv()
-        gather_pass(place, base, branch_all, sems, slot).start()
-    tasks.pop(0)()
-    attend_pair(2, 4)
-    for slot in (4, 5):
-        gather_piece(*args, slot).wait_recv()
-        gather_pass(place, base, branch_all, sems, slot).start()
-    for slot in range(4):
-        gather_pass(place, base, branch_all, sems, slot).wait_recv()
-    last.after(0)
-    tasks.pop(0)()
-    attend_pair(3, 5)
-    last.after(1)
-    if tasks:
-        tasks.pop(0)()
-    for slot in (4, 5):
-        gather_pass(place, base, branch_all, sems, slot).wait_recv()
-    attend_pair(6, 7)
-    last.after(2)
+
+    def passed(slots):
+        for slot in slots:
+            gather_piece(*args, slot).wait_recv()
+            gather_pass(place, base, branch_all, sems, slot).start()
+
+    def arrived(slots):
+        for slot in slots:
+            gather_pass(place, base, branch_all, sems, slot).wait_recv()
+
+    def task():
+        if tasks:
+            tasks.pop(0)()
+
+    def before(step):
+        if step == 0:
+            pltpu.make_async_copy(branch_rows, branch_all.at[place], sems[0]).wait()
+        if step == 1:
+            gather_own(*args).wait_recv()
+            gather_relay(*args)
+        if step == 2:
+            passed((2, 3))
+            last.after(0)
+            task()
+        if step == 3:
+            last.after(1)
+        if step == 4:
+            passed((4, 5))
+            arrived(range(4))
+            task()
+        if step == 5:
+            last.after(2)
+        if step == 6:
+            arrived((4, 5))
+        if step == 7:
+            task()
+
+    def attend_step(step, unused):
+        for k in range(8):
+
+            @pl.when(step == k)
+            def _(k=k):
+                before(k)
+
+        far = step + jnp.where(step == 3, 1, 0) - jnp.where(step == 4, 1, 0)
+        block = place + far % 2 * (1 - 2 * (place % 2))
+        block = block + far // 2 % 2 * (2 - 4 * (place // 2 % 2))
+        attend_back(block + far // 4 * (4 - 8 * (place // 4 % 2)))
+        return unused
+
+    lax.fori_loop(0, 8, attend_step, 0)
     for task in tasks:
         task()
     up_line.finish()
@@ -1140,7 +1299,7 @@
         grad_out = grad_out + outer_sum(
             mixed_ref[block * rows : (block + 1) * rows, :], branch_all[block]
         )
-    grad_out_ref[...] = grad_out.astype(bf16)
+    grad_out_ref[...] = grad_out
 
     def residual_and(span, value):
         output_ref[span, :] = residual_ref[span, :] + (value + vec_ref[7:8, :])
@@ -1174,7 +1333,7 @@
             shaped(rows, width, kind=f32),
             shaped(rows, width, kind=f32),
             shaped(clip, 3 * wide),
-            shaped(wide, width),
+            shaped(wide, width, kind=f32),
             shaped(8, width, kind=f32),
             shaped(*up.shape[1:]),
             shaped(*down.shape[1:], kind=f32),
@@ -1222,10 +1381,10 @@
     early_got,
     late_got,
     out_got,
+    out_sib,
     *rest,
 ):
     groups = count // GROUP
-    per = groups
     me = lax.axis_index("fsdp")
     place = me % GROUP
     base = me - place
@@ -1237,21 +1396,32 @@
     swap, rest = Swap(place, base, qkv_got, rest[:SWAP]), rest[SWAP:]
     early_mail = Mail(me, count, early_ref, early_got, *rest[:3])
     late_mail = Mail(me, count, late, late_got, *rest[3:6])
-    out_local, out_send, out_recv = rest[6:]
+    rest = rest[6:]
+    fast = on_lines(count)
+    core = place % 2
     greet_all(me, count)
     early_mail.begin()
-    for index in range(per):
-        owner = place * per + index
-
-        @pl.when(owner != me)
-        def _(index=index, owner=owner):
-            remote(
-                out_ref.at[index], out_got.at[mine], out_send.at[index], out_recv.at[mine], owner
-            ).start()
-
-        @pl.when(owner == me)
-        def _(index=index):
-            pltpu.make_async_copy(out_ref.at[index], out_got.at[mine], out_local).start()
+    if fast:
+        out_line = LineSum(me, groups, out_got, rest[3 : 3 + LINE_SUM])
+        crossing = []
+        for head in range(HEADS_HERE):
+            slab = HEADS_HERE * core + head
+            here = pl.multiple_of(head * LANES + few * core, 8)
+            out_got[slab, 0] = out_ref[pl.ds(here, few), :].astype(bf16)
+            there = pl.multiple_of(head * LANES + few * (1 - core), 8)
+            out_sib[head, 0] = out_ref[pl.ds(there, few), :].astype(bf16)
+            copy = remote(
+                out_sib.at[head],
+                out_got.at[slab],
+                rest[1].at[head],
+                rest[2].at[head],
+                base + flip(place, 1),
+            )
+            copy.start()
+            crossing.append(copy)
+    else:
+        direct = DirectBack(me, count, out_ref, out_got, *rest[:3])
+        direct.begin()
 
     padded = 3 * HEADS_HERE * LANES
     packed = 3 * HEAD_COLS
@@ -1267,6 +1437,10 @@
         cols[tile, :] = matmul(grad, pick)
         return unused
 
+    if fast:
+        for copy in crossing:
+            copy.wait()
+        out_line.begin()
     lax.fori_loop(0, width // 256, weight_grad, 0)
     for owner in range(count):
         own_cols[owner // GROUP, owner % GROUP] = cols[owner * few : (owner + 1) * few, :].astype(
@@ -1274,6 +1448,7 @@
         )
     line.begin()
     tasks = line.tasks()
+    out_tasks = out_line.tasks() if fast else []
     for i in range(4):
 
         def pair(turn, unused, i=i):
@@ -1291,8 +1466,32 @@
 
         lax.fori_loop(0, 2, pair, 0)
         one.after(i)
-        if tasks and i > 0:
+        if fast and 1 <= i <= 2:
+            out_tasks[i - 1]()
+        if i == 2:
             tasks.pop(0)()
+
+    wide = HEADS_HERE * LANES
+
+    def bias_sum(which):
+        def add(index, value):
+            span = pl.ds(pl.multiple_of(index * 64, 64), 64)
+            return value + fold(grad_qkv_ref[span, which * wide : (which + 1) * wide].astype(f32))
+
+        total = lax.fori_loop(
+            0, grad_qkv_ref.shape[0] // 64, add, jnp.zeros((8, wide), f32)
+        )
+        row = lax.broadcasted_iota(jnp.int32, (wide, width), 0)
+        col = lax.broadcasted_iota(jnp.int32, (wide, width), 1)
+        home = head_of(place, row // LANES) * HD + row % LANES
+        spot = jnp.where((row % LANES < HD) & (home == col), 1.0, 0.0)
+        return jnp.sum(
+            jnp.dot(total, spot, precision=lax.Precision.HIGHEST, preferred_element_type=f32),
+            axis=0,
+            keepdims=True,
+        )
+
+    biases = [bias_sum(0), bias_sum(2)]
     for task in tasks:
         task()
     folded[...] = jnp.zeros_like(folded)
@@ -1307,32 +1506,11 @@
     line.finish()
     swap.begin(line.total)
 
-    wide = HEADS_HERE * LANES
-
-    def bias_sum(which):
-        def add(index, value):
-            span = pl.ds(pl.multiple_of(index * 64, 64), 64)
-            return value + fold(grad_qkv_ref[span, which * wide : (which + 1) * wide].astype(f32))
-
-        total = lax.fori_loop(
-            0, grad_qkv_ref.shape[0] // 64, add, jnp.zeros((8, wide), f32)
-        )
-        row = lax.broadcasted_iota(jnp.int32, (wide, width), 0)
-        col = lax.broadcasted_iota(jnp.int32, (wide, width), 1) - place * HEAD_COLS
-        fits = (col >= 0) & (col < HEAD_COLS) & (row % LANES < HD)
-        spot = jnp.where(fits & (row // LANES * HD + row % LANES == col), 1.0, 0.0)
-        return jnp.sum(
-            jnp.dot(total, spot, precision=lax.Precision.HIGHEST, preferred_element_type=f32),
-            axis=0,
-            keepdims=True,
-        )
-
     vectors = jnp.concatenate(
         [
             jnp.sum(folded[0], axis=0, keepdims=True),
             jnp.sum(folded[1], axis=0, keepdims=True),
-            bias_sum(0),
-            bias_sum(2),
+            *biases,
             jnp.zeros((4, width), f32),
         ],
         axis=0,
@@ -1360,31 +1538,12 @@
     lax.fori_loop(0, count // many, owners, 0)
     late_mail.begin()
     early_mail.finish(early_total)
-    for index in range(per):
-        owner = place * per + index
-
-        @pl.when(owner != me)
-        def _(index=index):
-            remote(
-                out_ref.at[index], out_got.at[mine], out_send.at[index], out_recv.at[mine], me
-            ).wait_send()
-
-        @pl.when(owner == me)
-        def _(index=index):
-            pltpu.make_async_copy(out_ref.at[index], out_got.at[mine], out_local).wait()
-
-    for group in range(groups):
-
-        @pl.when(group * GROUP + me // per != me)
-        def _(group=group):
-            remote(
-                out_ref.at[0], out_got.at[group], out_send.at[0], out_recv.at[group], me
-            ).wait_recv()
-
-    total = out_got[0].astype(f32)
-    for group in range(1, groups):
-        total = total + out_got[group].astype(f32)
-    out_total[...] = total
+    if fast:
+        out_line.finish()
+        out_total[...] = out_line.total[0]
+        out_line.drain()
+    else:
+        direct.finish(out_total)
     swap.finish()
     late_mail.finish(late_total)
     one.drain()
@@ -1396,6 +1555,7 @@
     rows, width = x.shape
     few = width // count
     packed = 3 * HEAD_COLS
+    fast = on_lines(count)
 
     def mail(shape):
         return [DMA, DMA((count,)), DMA((count,))]
@@ -1418,17 +1578,96 @@
             VMEM((count, 8, LANES), f32),
             VMEM(early.shape, f32),
             VMEM((count, 8, LANES), f32),
-            VMEM((groups, few, width), bf16),
+            VMEM((groups, 1, few, width) if fast else (groups, few, width), bf16),
+            VMEM((HEADS_HERE, 1, few, width), bf16),
         ]
         + scatter_scratch(rows, width)
         + line_sum_scratch(groups, GROUP, few, packed)
         + swap_scratch(few, packed)
         + mail(early)
         + mail(early)
-        + [DMA, DMA((groups,)), DMA((groups,))],
+        + [DMA, DMA((groups,)), DMA((groups,))]
+        + (line_sum_scratch(groups, 1, few, width) if fast else []),
         compiler_params=params(collective_id),
         name="last",
     )(x, normed, grad_qkv, w_qkv, grad, gain, early, out)
+
+
+def pack_kernel(
+    groups,
+    output_in,
+    inputs_in,
+    qkv_in,
+    out_in,
+    early_in,
+    late_in,
+    up_in,
+    down_in,
+    output,
+    grad_inputs,
+    g1,
+    o1,
+    wq,
+    bq,
+    wk,
+    wv,
+    bv,
+    wo,
+    bo,
+    g2,
+    o2,
+    wu,
+    bu,
+    wd,
+    bd,
+):
+    few, many = wq.shape[0], wd.shape[0]
+    output[...] = output_in[...]
+    grad_inputs[...] = inputs_in[...]
+    for place in range(GROUP):
+        for which, ref in enumerate((wq, wk, wv)):
+            for head in range(HEADS_HERE):
+                start = head_of(place, head) * HD
+                cols = which * HEAD_COLS + head * HD
+                ref[:, start : start + HD] = qkv_in[place, :, cols : cols + HD].astype(f32)
+        for group in range(groups):
+            start = (group * GROUP + place) * many
+            wu[:, start : start + many] = up_in[
+                place, :, group * many : (group + 1) * many
+            ].astype(f32)
+    wo[...] = out_in[...]
+    for index in range(down_in.shape[0]):
+        wd[index * few : (index + 1) * few, :] = down_in[index]
+    for index, ref in enumerate((g1, o1, bq, bv)):
+        ref[...] = late_in[index : index + 1, :few]
+    for index, ref in enumerate((g2, o2, bo, bd)):
+        ref[...] = early_in[index : index + 1, :few]
+    for start in range(0, many, LANES):
+        stop = min(start + LANES, many)
+        line = 4 + start // LANES
+        bu[:, start:stop] = early_in[line : line + 1, : stop - start]
+
+
+def pack(groups, output, grad_inputs, qkv, out, early, late, up, down):
+    rows, width = output.shape
+    few, many = out.shape[0], down.shape[0] * down.shape[1]
+    ff = groups * GROUP * many
+
+    def whole(*shape):
+        return jax.ShapeDtypeStruct(shape, f32)
+
+    line = whole(1, few)
+    square = whole(few, width)
+    big = whole(rows, width)
+    results = pl.pallas_call(
+        functools.partial(pack_kernel, groups),
+        out_shape=[big, big, line, line, square, line, square, square, line, square]
+        + [line, line, line, whole(few, ff), whole(1, many), whole(many, width), line],
+        in_specs=[VSPEC] * 8,
+        out_specs=[VSPEC] * 17,
+        name="pack",
+    )(output, grad_inputs, qkv, out, early, late, up, down)
+    return tuple(r.reshape(r.shape[1]) if r.shape[0] == 1 else r for r in results)
 
 
 def gelu_exact(values):
@@ -1505,7 +1744,8 @@
         small,
         0,
     )
-    b_up_here = lax.dynamic_index_in_dim(small_all, place, 1, keepdims=False)
+    b_up_here = small_all.reshape((groups, GROUP) + small_all.shape[1:])
+    b_up_here = lax.dynamic_index_in_dim(b_up_here, place, 1, keepdims=False)
     b_up_here = b_up_here[:, 8 : 8 + up_lanes].astype(f32)
     b_up_here = b_up_here.reshape(groups, up_lanes * LANES)[:, :many].reshape(ff_here)
     w_up_here = up_all.reshape(D, ff_here)
@@ -1540,7 +1780,9 @@
         grad_w_down.reshape(groups, many // few, few, D),
         2,
     )
-    grad_out = grad_out.reshape(HEADS_HERE, LANES, D)[:, :HD].reshape(groups, few, D)
+    if not on_lines(count):
+        grad_out = grad_out.reshape(HEADS_HERE, LANES, D)[:, :HD].reshape(groups, few, D)
+        grad_out = grad_out.astype(bf16)
     grad_b_up = jnp.pad(
         column_sums(grad_hidden).reshape(groups, 1, many),
         ((0, 0), (0, 0), (0, up_lanes * LANES - many)),
@@ -1567,34 +1809,16 @@
         3,
     )
 
-    def shard_of(which):
-        piece = qkv_got[:, :, which * HEAD_COLS : (which + 1) * HEAD_COLS]
-        return piece.transpose(1, 0, 2).reshape(few, D).astype(f32)
-
-    shard_w_up = (
-        up_got.reshape(GROUP, few, groups, many)
-        .transpose(1, 2, 0, 3)
-        .reshape(few, groups * GROUP * many)
-        .astype(f32)
-    )
-    return (
+    return pack(
+        groups,
         output,
         grad_inputs,
-        late_sum[0, :few],
-        late_sum[1, :few],
-        shard_of(0),
-        late_sum[2, :few],
-        shard_of(1),
-        shard_of(2),
-        late_sum[3, :few],
+        qkv_got,
         shard_w_out,
-        early_sum[2, :few],
-        early_sum[0, :few],
-        early_sum[1, :few],
-        shard_w_up,
-        early_sum[4 : 4 + up_lanes].reshape(up_lanes * LANES)[:many],
-        down_total.reshape(many, D),
-        early_sum[3, :few],
+        early_sum,
+        late_sum,
+        up_got,
+        down_total,
     )
 
 

time: 387 us -> 304 us (0.79)
  Pallas kernels: 313 us -> 252 us
  local copies, waits for them, and re-layouts: 21.4 us -> 3.35 us
    pallas_call x1, Pallas kernels: 84.9 us -> 54.1 us  [last(): pl.pallas_call(functools.partial(last_kernel, count), out_shape=[shaped(r...]
    pallas_call x1, Pallas kernels: 92.5 us -> 73.7 us  [middle(): pl.pallas_call(functools.partial(middle_kernel, count), out_shape=[shaped...]
    pallas_call x1, Pallas kernels: 135 us -> 119 us  [front(): pl.pallas_call(functools.partial(front_kernel, count), out_shape=[shaped(...]
    convert_element_type x9 -> x0, local copies, waits for them, and re-layouts: 6.32 us -> none  [the longest x3 3.49 us: on_device(): shard_w_up = up_got.reshape(GROUP, few, groups, many).transpose(1, 2, 0,...]
    unnamed x24 -> x14, local copies, waits for them, and re-layouts: 6.04 us -> 0.04 us
    pallas_call x0 -> x1, Pallas kernels: none -> 4.54 us  [pack(): pl.pallas_call(functools.partial(pack_kernel, groups), out_shape=[big, bi...]
where the time goes in v4:
time: 304 us; the launch traced here: 299 us
  Pallas kernels  252 us (83%)
  matrix products  37.5 us (12%)
  other arithmetic  5.41 us (2%)
  local copies, waits for them, and re-layouts  3.35 us (1%)
    pallas_call x1, Pallas kernels, front(): pl.pallas_call(functools.partial(front_kernel, count), out_shape=[shaped(...  119 us
    pallas_call x1, Pallas kernels, middle(): pl.pallas_call(functools.partial(middle_kernel, count), out_shape=[shaped...  73.7 us
    pallas_call x1, Pallas kernels, last(): pl.pallas_call(functools.partial(last_kernel, count), out_shape=[shaped(r...  54.1 us
    dot_general x2, matrix products, times_transposed(): lax.dot_general(left, right, (((1,), (1,)), ((), ())), preferred_element_...  16.6 us
    dot_general x2, matrix products, matmul(): return jnp.dot(left, right, preferred_element_type=f32)  12.3 us
    dot_general x2, matrix products, outer_sum(): lax.dot_general(left, right, (((0,), (0,)), ((), ())), preferred_element_...  8.58 us

profile of v4, /device:TPU:0, one launch (start us, length us, event | category | flops | bytes accessed | tf_op | source)
XLA Modules:
  0.0 299.1 jit_solution(16715027720335243826)
XLA Ops:
  0.7 1.2 dynamic_slice.7.length_ref
  1.9 0.1 broadcast_in_dim.35
  2.0 0.7 convert.54
  2.7 0.1 pad.27.clone
  2.8 0.7 convert_bitcast_fusion.6
  3.5 0.7 convert_bitcast_fusion.4
  4.2 0.7 convert_bitcast_fusion.2
  4.8 0.7 convert_bitcast_fusion
  5.5 0.7 fusion.9.small_ref
  6.2 119.1 %front.1 = (bf16[1536,1280]{1,0:T(8,128)(2,1)}, bf16[1280,768]{1,0:T(8,128)(2,1)}, bf16[1536,768]{1,0:T(8,128)(2,1)}, bf16[256,1280]{1,0:T(8,128)(2,1)}, bf16[15...) custom-call(s32[4]{0:T(128)} %length_ref.1, ...), custom_call_target="tpu_custom_call" | custom-call | tf_op jit(solution)/shard_map/front/pallas_call | solution.py:1076
  125.3 0.7 dynamic-slice_bitcast_fusion
  126.1 0.1 reshape.134
  126.1 0.0 copy-start
  126.2 0.0 copy-start.3
  126.2 6.0 %fusion.11 = f32[1536,640]{1,0:T(8,128)S(1)} fusion(bf16[1536,1280]{1,0:T(8,128)(2,1)} %bitcast.71, bf16[1280,640]{1,0:T(8,128)(2,1)} %bitcast.73), kind=kOutput, calls=%fused_computation.45 | convolution fusion | flops 2516582400 | bytes 9502720 | tf_op jit(solution)/shard_map/dot_general | solution.py:31
  132.2 0.0 copy-done
  132.2 0.0 copy-done.3
  132.2 0.0 copy-start.1
  132.2 11.9 %convert_reduce_fusion = (f32[640]{0:T(1024)S(1)}, bf16[1536,640]{1,0:T(8,128)(2,1)S(1)}, f32[1536,640]{1,0:T(8,128)S(1)}) fusion(f32[1536,640]{1,0:T(8,128)S(1)} %fusion.11, f32[640]{0:T(1024)S(1)} %reshape.134, bf16[1536,1280]{1,0:T(8,128)(2,1)S(1)} %bitcast.69, bf16[640,1280]{1,0:T(8,128)(2,1)S(1)} %bitcast.76), kind=kOutput, calls=%fused_computation.4 | convolution fusion | flops 2590309888 | bytes 15406080 | tf_op jit(solution)/shard_map/dot_general | solution.py:39
  144.1 0.0 copy-start.4
  144.1 0.0 copy-done.1
  144.1 4.5 %convolution_convert_fusion.3 = bf16[1280,640]{1,0:T(8,128)(2,1)} fusion(bf16[1536,1280]{1,0:T(8,128)(2,1)S(1)} %bitcast.72, bf16[1536,640]{1,0:T(8,128)(2,1)S(1)} %get-tuple-element.102), kind=kOutput, calls=%fused_computation.21 | convolution fusion | flops 2517401600 | bytes 7536640 | tf_op jit(solution)/shard_map/dot_general | solution.py:35
  148.6 0.0 copy-done.4
  148.6 0.5 multiply_convert_fusion
  149.2 4.1 %convolution_convert_fusion.2 = bf16[640,1280]{1,0:T(8,128)(2,1)} fusion(bf16[1536,640]{1,0:T(8,128)(2,1)S(1)} %multiply_convert_fusion, bf16[1536,1280]{1,0:T(8,128)(2,1)S(1)} %bitcast.70), kind=kOutput, calls=%fused_computation.20 | convolution fusion | flops 2517401600 | bytes 7536640 | tf_op jit(solution)/shard_map/dot_general | solution.py:35
  153.3 0.1 reshape.124
  153.4 0.1 bitcast_select_fusion
  153.5 0.0 copy-start.2
  153.5 0.0 copy-start.5
  153.5 6.3 %convolution_convert_fusion = bf16[1536,1280]{1,0:T(8,128)(2,1)} fusion(bf16[1536,640]{1,0:T(8,128)(2,1)S(1)} %multiply_convert_fusion, bf16[640,1280]{1,0:T(8,128)(2,1)} %bitcast.75), kind=kOutput, calls=%fused_computation | convolution fusion | flops 2518548480 | bytes 7536640 | tf_op jit(solution)/shard_map/dot_general | solution.py:31
  159.8 0.0 copy-done.2
  159.8 0.0 copy-done.5
  159.8 4.7 %convolution_convert_fusion.1 = bf16[1536,1280]{1,0:T(8,128)(2,1)} fusion(bf16[1536,640]{1,0:T(8,128)(2,1)S(1)} %copy-done.5, bf16[1280,640]{1,0:T(8,128)(2,1)S(1)} %bitcast.74), kind=kOutput, calls=%fused_computation.1 | convolution fusion | flops 2518548480 | bytes 7536640 | tf_op jit(solution)/shard_map/dot_general | solution.py:39
  164.5 73.7 %middle.1 = (f32[192,1280]{1,0:T(8,128)}, f32[192,1280]{1,0:T(8,128)}, bf16[1536,768]{1,0:T(8,128)(2,1)}, f32[256,1280]{1,0:T(8,128)}, f32[8,1280]{1,0:T(8,128)}...) custom-call(s32[1]{0:T(128)} %dynamic_slice.7.length_ref, bf16[8,192,1280]{2,1,0:T(8,128)(2,1)} %bitcast.63, ...), custom_call_target="tpu_custom_call" | custom-call | tf_op jit(solution)/shard_map/middle/pallas_call | solution.py:1330
  238.3 0.8 slice.12
  239.1 0.1 reshape.123
  239.3 0.7 fusion.6.early_ref
  240.0 54.1 %last.1 = (f32[192,1280]{1,0:T(8,128)}, bf16[8,40,480]{2,1,0:T(8,128)(2,1)}, f32[40,1280]{1,0:T(8,128)}, f32[8,128]{1,0:T(8,128)}, f32[8,128]{1,0:T(8,128)}) custom-call(bf16[192,1280]{1,0:T(8,128)(2,1)} %x_ref.3, bf16[1536,1280]{1,0:T(8,128)(2,1)} %get-tuple-element.71.normed_ref, bf16[1536,768]{1,0:T(8,128)(2,1)} %get-tuple-element.72.grad_qkv_ref, ...), custom_call_target="tpu_custom_call" | custom-call | tf_op jit(solution)/shard_map/last/pallas_call | solution.py:1563
  294.1 4.5 %pack.1 = (f32[192,1280]{1,0:T(8,128)}, f32[192,1280]{1,0:T(8,128)}, f32[1,40]{1,0:T(1,128)}, f32[1,40]{1,0:T(1,128)}, f32[40,1280]{1,0:T(8,128)}, /*index=5*/f3...) custom-call(f32[192,1280]{1,0:T(8,128)} %get-tuple-element.70.output, ...), custom_call_target="tpu_custom_call" | custom-call | tf_op jit(solution)/shard_map/pack/pallas_call | solution.py:1662
  (12 shorter events, 0.2 us)
Async XLA Ops:
  126.1 6.0 %copy-start = (bf16[8,192,1280]{2,1,0:T(8,128)(2,1)S(1)}, bf16[8,192,1280]{2,1,0:T(8,128)(2,1)}, u32[]{:S(2)}) copy-start(bf16[8,192,1280]{2,1,0:T(8,128)(2,1)} %get-tuple-element.62) | copy-start | bytes 11796484
  126.2 6.1 %copy-start.3 = (bf16[4,160,1280]{2,1,0:T(8,128)(2,1)S(1)}, bf16[4,160,1280]{2,1,0:T(8,128)(2,1)}, u32[]{:S(2)}) copy-start(bf16[4,160,1280]{2,1,0:T(8,128)(2,1)} %get-tuple-element.63) | copy-start | bytes 4915204
  132.2 11.9 %copy-start.1 = (bf16[8,192,1280]{2,1,0:T(8,128)(2,1)S(1)}, bf16[8,192,1280]{2,1,0:T(8,128)(2,1)}, u32[]{:S(2)}) copy-start(bf16[8,192,1280]{2,1,0:T(8,128)(2,1)} %get-tuple-element.59) | copy-start | bytes 11796484
  144.1 4.5 %copy-start.4 = (bf16[1536,640]{1,0:T(8,128)(2,1)}, bf16[1536,640]{1,0:T(8,128)(2,1)S(1)}, u32[]{:S(2)}) copy-start(bf16[1536,640]{1,0:T(8,128)(2,1)S(1)} %get-tuple-element.102) | copy-start | bytes 5898244
  153.5 6.3 %copy-start.2 = (bf16[4,8,40,640]{3,2,1,0:T(8,128)(2,1)S(1)}, bf16[4,8,40,640]{3,2,1,0:T(8,128)(2,1)}, u32[]{:S(2)}) copy-start(bf16[4,8,40,640]{3,2,1,0:T(8,128)(2,1)} %get-tuple-element.60) | copy-start | bytes 4915204
  153.5 6.3 %copy-start.5 = (bf16[1536,640]{1,0:T(8,128)(2,1)S(1)}, bf16[1536,640]{1,0:T(8,128)(2,1)}, u32[]{:S(2)}) copy-start(bf16[1536,640]{1,0:T(8,128)(2,1)} %copy-done.4) | copy-start | bytes 5898244
